TPU v7x, 512 devices: a whole 4x4x16 slice. The times are simulated.
512 devices in a mesh: req: 128 (over x, z, core), tp: 4 (over y).
Axes of the slice: x: 4, y: 4, z: 16, core: 2. Of those that a mesh axis runs over, the one named last changes fastest.
Arguments:
- x_pre: bfloat16 [65536, 1280], P('req', 'tp'), may hold values from -6 to 6
- x_dec: bfloat16 [512, 1280], P('req', 'tp'), may hold values from -6 to 6
- norm_gain: float32 [1280], replicated, may hold values from 0.1 to 1.9
- w_qkv: bfloat16 [3, 1280, 1280], P(None, None, 'tp'), may hold values from -0.15625 to 0.15625
- w_out: bfloat16 [1280, 1280], P('tp'), may hold values from -0.625 to 0.625
- pre_keys: bfloat16 [49152, 1280], P('req', 'tp'), may hold values from -70 to 70
- pre_values: bfloat16 [49152, 1280], P('req', 'tp'), may hold values from -6 to 6
- pre_lens: int32 [128], P('req'), may hold values from 0 to 384, as said below
- dec_keys: bfloat16 [81920, 1280], P('req', 'tp'), may hold values from -70 to 70
- dec_values: bfloat16 [81920, 1280], P('req', 'tp'), may hold values from -6 to 6
- dec_lens: int32 [512], replicated, may hold values from 1 to 41600, as said below
Outputs:
- pre_out: bfloat16 [65536, 1280], P('req', 'tp')
- dec_out: bfloat16 [512, 1280], P('req', 'tp')
Inputs may be any that keep to these rules, and one draw needn't show every extreme that they name: `pre_lens`: at least one prefill block has all 384 cached rows valid. `dec_lens`: the lengths sum to 61440; request 0 has exactly 41600 rows, every other request fewer.
All inputs are finite; a program needn't handle non-finite values.
Results may differ from a plain program's by a relative error of at most 0.012.
The roundings to bfloat16 on the way count: a program that leaves them out, or rounds other values in their place, can miss the bound.
Values may be sent and summed in bfloat16 or wider, within the bound.
No kernel may reach another device: no remote copies, remote signals or barrier semaphores. Data moves between devices by JAX's collectives and lax.ppermute only.
A program may use at most 64 MiB of HBM per device.

v0:
```python
import math

import jax
import jax.numpy as jnp
from jax import lax
from jax.sharding import PartitionSpec as P

HD = 80


EPSILON = 1e-06
MASKED_SCORE = -1e30


def normalize(tokens, norm_gain):
    tokens_f = tokens.astype(jnp.float32)
    mean_square = jnp.mean(tokens_f * tokens_f, axis=-1, keepdims=True)
    return (tokens_f * lax.rsqrt(mean_square + EPSILON) * norm_gain).astype(jnp.bfloat16)


def project(hidden, w_qkv):
    return tuple(
        (
            jnp.dot(hidden, w_qkv[matrix_index], preferred_element_type=jnp.float32).astype(
                jnp.bfloat16
            )
            for matrix_index in range(3)
        )
    )


def rounded(weights):
    held = lax.optimization_barrier(weights.astype(jnp.bfloat16))
    return held.astype(jnp.float32)


def prefill_attention(
    query_pre, key_pre, value_pre, pre_keys, pre_values, prefix, local_heads, score_scale
):
    rows_pre = query_pre.shape[0]
    cached = pre_keys.shape[0]
    keys_all = jnp.concatenate([pre_keys, key_pre], axis=0).reshape(-1, local_heads, HD)
    values_all = jnp.concatenate([pre_values, value_pre], axis=0).reshape(-1, local_heads, HD)
    scores = (
        jnp.einsum(
            "phd,rhd->hpr",
            query_pre.reshape(rows_pre, local_heads, HD),
            keys_all,
            preferred_element_type=jnp.float32,
        )
        * score_scale
    )
    column = jnp.arange(keys_all.shape[0], dtype=jnp.int32)[None, :]
    position = jnp.arange(rows_pre, dtype=jnp.int32)[:, None]
    allowed = jnp.where(column < cached, column < prefix, column - cached <= position)
    scores = jnp.where(allowed[None], scores, MASKED_SCORE)
    row_top = jnp.max(scores, axis=-1, keepdims=True)
    weights = jnp.where(allowed[None], jnp.exp(scores - row_top), 0.0)
    totals = jnp.transpose(jnp.sum(weights, axis=-1))
    mixed = (
        jnp.einsum(
            "hpr,rhd->phd",
            weights.astype(jnp.bfloat16),
            values_all,
            preferred_element_type=jnp.float32,
        )
        / totals[..., None]
    )
    return mixed.reshape(rows_pre, local_heads * HD).astype(jnp.bfloat16)


def body(
    x_pre,
    x_dec,
    norm_gain,
    w_qkv,
    w_out,
    pre_keys,
    pre_values,
    pre_lens,
    dec_keys,
    dec_values,
    dec_lens,
):
    full_pre, full_dec = (
        lax.all_gather(x_pre, "tp", axis=1, tiled=True),
        lax.all_gather(x_dec, "tp", axis=1, tiled=True),
    )
    local_width = w_qkv.shape[2]
    local_heads = local_width // HD
    score_scale = 1.0 / math.sqrt(HD)
    query_pre, key_pre, value_pre = project(normalize(full_pre, norm_gain), w_qkv)
    query_dec, key_dec, value_dec = project(normalize(full_dec, norm_gain), w_qkv)
    attn_pre = prefill_attention(
        query_pre, key_pre, value_pre, pre_keys, pre_values, pre_lens[0], local_heads, score_scale
    )
    all_queries = lax.all_gather(query_dec, "req", axis=0, tiled=True)
    requests = all_queries.shape[0]
    own_rows = query_dec.shape[0]
    pool_rows = dec_keys.shape[0]
    device = lax.axis_index("req")
    starts = jnp.cumsum(dec_lens) - dec_lens
    global_rows = device * pool_rows + jnp.arange(pool_rows, dtype=jnp.int32)
    allowed = (global_rows[None, :] >= starts[:, None]) & (
        global_rows[None, :] < (starts + dec_lens)[:, None]
    )
    cache_scores = (
        jnp.einsum(
            "qhd,rhd->qhr",
            all_queries.reshape(requests, local_heads, HD),
            dec_keys.reshape(pool_rows, local_heads, HD),
            preferred_element_type=jnp.float32,
        )
        * score_scale
    )
    cache_scores = jnp.where(allowed[:, None, :], cache_scores, MASKED_SCORE)
    self_score = (
        jnp.sum(
            query_dec.astype(jnp.float32).reshape(own_rows, local_heads, HD)
            * key_dec.astype(jnp.float32).reshape(own_rows, local_heads, HD),
            axis=-1,
        )
        * score_scale
    )
    self_rows = lax.dynamic_update_slice_in_dim(
        jnp.full((requests, local_heads), MASKED_SCORE, jnp.float32),
        self_score,
        device * own_rows,
        0,
    )
    local_top = jnp.maximum(jnp.max(cache_scores, axis=-1), self_rows)
    row_top = lax.pmax(local_top, "req")
    weights = jnp.where(allowed[:, None, :], jnp.exp(cache_scores - row_top[..., None]), 0.0)
    totals = jnp.sum(weights, axis=-1)
    partial_value = jnp.einsum(
        "qhr,rhd->qhd",
        weights.astype(jnp.bfloat16),
        dec_values.reshape(pool_rows, local_heads, HD),
        preferred_element_type=jnp.float32,
    ).reshape(requests, local_width)
    totals_all, partial_all = lax.psum((totals, partial_value), "req")
    own_totals = lax.dynamic_slice_in_dim(totals_all, device * own_rows, own_rows, 0)
    own_partial = lax.dynamic_slice_in_dim(partial_all, device * own_rows, own_rows, 0)
    own_top = lax.dynamic_slice_in_dim(row_top, device * own_rows, own_rows, 0)
    self_weight = jnp.exp(self_score - own_top)
    numerator = own_partial.reshape(own_rows, local_heads, HD) + rounded(self_weight)[
        ..., None
    ] * value_dec.astype(jnp.float32).reshape(own_rows, local_heads, HD)
    denominator = own_totals + self_weight
    attn_dec = (
        (numerator / denominator[..., None]).reshape(own_rows, local_width).astype(jnp.bfloat16)
    )
    terms_pre = jnp.dot(attn_pre, w_out, preferred_element_type=jnp.float32)
    terms_dec = jnp.dot(attn_dec, w_out, preferred_element_type=jnp.float32)
    out_pre, out_dec = (
        lax.psum_scatter(terms_pre, "tp", scatter_dimension=1, tiled=True),
        lax.psum_scatter(terms_dec, "tp", scatter_dimension=1, tiled=True),
    )
    return (out_pre.astype(jnp.bfloat16), out_dec.astype(jnp.bfloat16))


def solution(mesh):
    return jax.shard_map(
        body,
        mesh=mesh,
        in_specs=(
            P("req", "tp"),
            P("req", "tp"),
            P(),
            P(None, None, "tp"),
            P("tp", None),
            P("req", "tp"),
            P("req", "tp"),
            P("req"),
            P("req", "tp"),
            P("req", "tp"),
            P(),
        ),
        out_specs=(P("req", "tp"), P("req", "tp")),
        check_vma=False,
    )
```

profile of v0, /device:TPU:1, one launch (start us, length us, event | category | flops | bytes accessed | tf_op | source)
XLA Modules:
  0.0 785.2 jit_solution(5157148201678637434)
XLA Ops:
  8.0 0.0 copy-start
  8.0 0.0 all-reduce.2.cloned.1.call-start
  8.1 10.6 %all-gather = bf16[4,320,4]{1,2,0:T(4,128)(2,1)S(1)} all-gather(bf16[1,320,4]{1,2,0:T(4,128)(2,1)} %bitcast.80), channel_id=1, replica_groups=mesh['req'=128,'tp'=4] {'tp'}, dimensions={0}, use_global_device_ids=true | all-gather | bytes 12800 | tf_op jit(solution)/shard_map/all_gather | solution.py:87
  18.7 0.1 reshape.212
  18.8 0.1 multiply_reduce_fusion
  18.9 0.8 multiply_convert_fusion
  19.7 1.4 convolution_convert_fusion.5
  21.1 1.5 fusion.36
  22.6 0.1 mul.96
  22.7 0.1 reduce_sum.48
  22.8 0.1 copy.22
  22.9 1.0 reduce-window.9
  23.9 0.1 slice.22
  24.0 0.1 slice_reduce_fusion
  24.1 0.8 fusion.64
  24.9 92.8 %all-gather.1 = bf16[128,4,320]{2,1,0:T(4,128)(2,1)S(1)} all-gather(bf16[1,4,320]{2,1,0:T(4,128)(2,1)S(1)} %bitcast.78), channel_id=1, replica_groups=mesh['req'=128,'tp'=4] {'req'}, dimensions={0}, use_global_device_ids=true | all-gather | bytes 330240 | tf_op jit(solution)/shard_map/all_gather | solution.py:97
  117.7 0.4 reshape.203
  118.1 0.3 dynamic_update_slice.3
  118.4 0.3 compare_and_fusion
  118.7 0.0 copy-done.7
  118.7 0.0 copy-start.8
  118.7 3.6 bitcast_reduce_fusion
  122.3 250.3 %pmax.7 = f32[512,4]{0,1:T(4,128)S(1)} all-reduce(f32[512,4]{0,1:T(4,128)S(1)} %max.5), channel_id=1, replica_groups=mesh['req'=128,'tp'=4] {'req'}, use_global_device_ids=true, to_apply=%region_9.10 | all-reduce | flops 2048 | bytes 16384 | tf_op jit(solution)/shard_map/pmax | solution.py:132
  372.6 3.6 fusion.16
  376.2 1.1 copy.23
  377.4 0.0 all-reduce.2.cloned.1.call-update
  377.4 0.0 all-gather.4.cloned.1.call-start
  377.5 0.5 all-gather.4.cloned.1.call-update
  378.0 0.0 reduce-scatter.7.cloned.1.call-start
  378.0 3.8 fusion.6
  381.8 0.0 copy-start.6
  381.9 253.8 %psum.15 = f32[512,4]{0,1:T(4,128)S(1)} all-reduce(f32[512,4]{0,1:T(4,128)S(1)} %fusion.6), channel_id=1, replica_groups=mesh['req'=128,'tp'=4] {'req'}, use_global_device_ids=true, to_apply=%region_12.13 | all-reduce | flops 2048 | bytes 16384 | tf_op jit(solution)/shard_map/psum | solution.py:141
  635.6 0.1 fusion.55
  635.7 0.1 copy.25
  635.8 0.1 div.33
  635.9 0.1 div.34
  636.0 0.1 copy.24
  636.1 0.1 mul.99
  636.1 0.1 mul.100
  636.9 1.1 fusion.20
  638.1 63.4 %all-reduce.2.cloned.1.call-done = f32[512,320]{1,0:T(8,128)} async-done(((f32[512,320]{1,0:T(8,128)}), f32[512,320]{1,0:T(8,128)}) %all-reduce.2.cloned.1.call-update) | async-done | bytes 655376 | tf_op jit(solution)/shard_map/psum | solution.py:141
  701.5 0.0 copy-done
  701.5 2.9 convolution_bitcast_fusion
  704.4 0.0 reduce-scatter.7.cloned.1.call-update
  704.5 0.0 copy-start.4
  704.5 0.2 reduce-scatter.5.cloned.1.call-start
  704.7 0.0 all-gather.4.cloned.1.call-done
  704.7 1.7 fusion.13
  706.4 0.0 copy-done.6
  706.4 0.0 copy-start.2
  706.4 2.1 convolution_convert_fusion
  708.5 0.0 copy-start.5
  708.5 0.9 pad_maximum_fusion.1
  709.4 0.7 convolution_convert_fusion.2
  710.1 0.9 pad_maximum_fusion
  710.9 1.4 convolution_convert_fusion.1
  712.4 6.7 fusion.65
  719.1 3.3 fusion.27
  722.4 2.4 fusion.66
  724.8 0.0 reduce-scatter.5.cloned.1.call-update
  724.8 5.1 reduce-scatter.7.cloned.1.call-done
  729.9 1.6 copy.27
  731.5 44.2 %reduce-scatter.5.cloned.1.call-done = f32[512,320]{0,1:T(8,128)} async-done(((f32[512,1280]{0,1:T(8,128)}), f32[512,320]{0,1:T(8,128)}) %reduce-scatter.5.cloned.1.call-update) | async-done | bytes 655376 | tf_op jit(solution)/shard_map/reduce_scatter | solution.py:156
  775.7 1.9 convert_element_type.74
  (19 shorter events, 0.1 us)
Async XLA Ops:
  8.0 693.5 %copy-start = (bf16[320,1280]{1,0:T(8,128)(2,1)S(1)}, bf16[320,1280]{1,0:T(8,128)(2,1)}, u32[]{:S(2)}) copy-start(bf16[320,1280]{1,0:T(8,128)(2,1)} %param.15) | copy-start | bytes 2457604
  8.0 110.7 %copy-start.7 = (bf16[640,320]{0,1:T(8,128)(2,1)S(1)}, bf16[640,320]{0,1:T(8,128)(2,1)}, u32[]{:S(2)}) copy-start(bf16[640,320]{0,1:T(8,128)(2,1)} %param.19) | copy-start | bytes 1228804
  8.0 693.5 %all-reduce.2.cloned.1.call-start = ((), (), s32[]{:S(2)}) async-start(), calls=%async_computation.4 | async-start | bytes 1572864 | tf_op jit(solution)/shard_map/psum | solution.py:141
  118.7 253.9 %copy-start.8 = (bf16[640,320]{0,1:T(8,128)(2,1)S(1)}, bf16[640,320]{0,1:T(8,128)(2,1)}, u32[]{:S(2)}) copy-start(bf16[640,320]{0,1:T(8,128)(2,1)} %param.20) | copy-start | bytes 1228804
  377.4 327.3 %all-gather.4.cloned.1.call-start = ((), (), s32[]{:S(2)}) async-start(), calls=%async_computation.2 | async-start | bytes 1638400 | tf_op jit(solution)/shard_map/all_gather | solution.py:86
  378.0 351.9 %reduce-scatter.7.cloned.1.call-start = ((), (), s32[]{:S(2)}) async-start(), calls=%async_computation.5 | async-start | bytes 819200
  381.8 324.6 %copy-start.1 = (bf16[3,1280,320]{1,2,0:T(8,128)(2,1)S(1)}, bf16[3,1280,320]{1,2,0:T(8,128)(2,1)}, u32[]{:S(2)}) copy-start(bf16[3,1280,320]{1,2,0:T(8,128)(2,1)} %param.14) | copy-start | bytes 7372804
  381.8 324.5 %copy-start.6 = (f32[1280]{0:T(1024)S(1)}, f32[1280]{0:T(1024)}, u32[]{:S(2)}) copy-start(f32[1280]{0:T(1024)} %param.13) | copy-start | bytes 15364
  704.5 4.1 copy-start.4
  704.5 71.2 %reduce-scatter.5.cloned.1.call-start = ((), (), s32[]{:S(2)}) async-start(), calls=%async_computation.3 | async-start | bytes 3276800 | tf_op jit(solution)/shard_map/reduce_scatter | solution.py:156
  706.4 3.0 copy-start.2
  708.5 1.6 copy-start.5
  712.4 6.7 copy-start.3
Sparse Core Ops, SparseCore 0:
  377.5 323.8 all-reduce.1
Sparse Core Ops, SparseCore 1:
  380.0 21.8 all-gather.3
  704.5 25.3 reduce-scatter.6
  732.6 43.1 reduce-scatter.4
where the time goes:
time: 786 us; the launch traced here: 785 us
  blocking collectives  607 us (77%)
  waiting for transfers between devices  113 us (14%)
  matrix products  29.6 us (4%)
  between operations  16.5 us (2%)
  other arithmetic  13.4 us (2%)
    psum x1, blocking collectives, body(): totals_all, partial_all = lax.psum((totals, partial_value), 'req')  254 us
    pmax x1, blocking collectives, body(): row_top = lax.pmax(local_top, 'req')  250 us
    all_gather x1, blocking collectives, body(): all_queries = lax.all_gather(query_dec, 'req', axis=0, tiled=True)  92.8 us
    psum x1, waiting for transfers between devices, body(): totals_all, partial_all = lax.psum((totals, partial_value), 'req')  63.4 us
    reduce_scatter x1, waiting for transfers between devices, body(): lax.psum_scatter(terms_pre, 'tp', scatter_dimension=1, tiled=True)  44.2 us
  transfers between devices with their start and end apart: 4, of which 3 were waited for; matrix products, arithmetic and copies ran while one was open for 4% of the time, Pallas kernels for 0%

commit v1 on v0

v1 whole, which is shorter than its diff:
```python
import math

import jax
import jax.numpy as jnp
from jax import lax
from jax.experimental import pallas as pl
from jax.experimental.pallas import tpu as pltpu
from jax.sharding import Mesh
from jax.sharding import PartitionSpec as P

HD = 80
HEADS = 4
WIDTH = HEADS * HD
LANES = 384
EPSILON = 1e-06
MASKED = -1e30
NX, NZ, NC, NT = 4, 16, 2, 4
LOG2E_SCALE = math.log2(math.e) / math.sqrt(HD)
F32, BF16 = jnp.float32, jnp.bfloat16
VMEM_LIMIT = 40 * 1024 * 1024


def dot(a, b, dims):
    return lax.dot_general(a, b, (dims, ((), ())), preferred_element_type=F32)


def by_head(columns, rows):
    lane = lax.broadcasted_iota(jnp.int32, (rows, WIDTH), 1)
    out = jnp.broadcast_to(columns[HEADS - 1], (rows, WIDTH))
    for h in range(HEADS - 2, -1, -1):
        out = jnp.where(lane < (h + 1) * HD, columns[h], out)
    return out


def normed_rows(x, gain):
    mean_square = jnp.sum(x * x, axis=-1, keepdims=True) * (1.0 / x.shape[-1])
    return (x * lax.rsqrt(mean_square + EPSILON) * gain).astype(BF16)


def dec_project_kernel(x_ref, gain_ref, w_ref, qb_ref, qkv_ref, rows):
    rows[...] = jnp.zeros_like(rows)
    for t in range(NT):
        rows[0:4, t * WIDTH : (t + 1) * WIDTH] = x_ref[t].astype(F32)
    hidden = normed_rows(rows[...], gain_ref[...])
    for part in range(3):
        value = dot(hidden, w_ref[part], ((1,), (1,)))[0:4].astype(BF16)
        qkv_ref[part] = value
        if part == 0:
            for z in range(NZ):
                qb_ref[z] = value


def dec_attention_kernel(base_ref, q_ref, k_ref, v_ref, lens_ref, out_ref):
    requests, pool = q_ref.shape[0], k_ref.shape[1]
    place = lax.broadcasted_iota(jnp.int32, (requests, requests), 0)
    x, c, z, i = place >> 7, (place >> 6) & 1, (place >> 2) & 15, place & 3
    request = (x << 7) | (z << 3) | (c << 2) | i
    other = lax.broadcasted_iota(jnp.int32, (requests, requests), 1)
    lens = lens_ref[...].astype(F32)
    begin = jnp.sum(jnp.where(other < request, lens, 0.0), axis=1, keepdims=True)
    end = jnp.sum(jnp.where(other <= request, lens, 0.0), axis=1, keepdims=True)
    base = base_ref[0].astype(F32)
    row = lax.broadcasted_iota(jnp.int32, (requests, pool), 1).astype(F32) + base
    allowed = (row >= begin) & (row < end)
    lane = lax.broadcasted_iota(jnp.int32, (requests, LANES - WIDTH), 1)
    extra = jnp.zeros((requests, LANES - WIDTH), F32)
    for h in range(HEADS):
        s = dot(q_ref[:, h * HD : (h + 1) * HD], k_ref[h * HD : (h + 1) * HD, :], ((1,), (0,)))
        s = jnp.where(allowed, s, MASKED)
        top = jnp.max(s, axis=1, keepdims=True)
        w = jnp.where(allowed, jnp.exp2((s - top) * LOG2E_SCALE), 0.0)
        total = jnp.sum(w, axis=1, keepdims=True)
        mixed = dot(w.astype(BF16), v_ref[h * HD : (h + 1) * HD, :], ((1,), (1,)))
        out_ref[:, h * HD : (h + 1) * HD] = mixed
        extra = jnp.where(lane == h, top, extra)
        extra = jnp.where(lane == HEADS + h, total, extra)
    out_ref[:, WIDTH:LANES] = extra


def merged(parts, rows):
    tops, totals, values = [], [], jnp.zeros((rows, WIDTH), F32)
    scales = []
    for h in range(HEADS):
        best = parts[0][:, WIDTH + h : WIDTH + h + 1]
        for part in parts[1:]:
            best = jnp.maximum(best, part[:, WIDTH + h : WIDTH + h + 1])
        tops.append(best)
        scale = [jnp.exp2((part[:, WIDTH + h : WIDTH + h + 1] - best) * LOG2E_SCALE) for part in parts]
        scales.append(scale)
        total = jnp.zeros_like(best)
        for part, factor in zip(parts, scale):
            total = total + factor * part[:, WIDTH + HEADS + h : WIDTH + HEADS + h + 1]
        totals.append(total)
    for n, part in enumerate(parts):
        values = values + by_head([scales[h][n] for h in range(HEADS)], rows) * part[:, :WIDTH]
    return values, tops, totals


def dec_merge_kernel(in_ref, out_ref):
    count, rows = in_ref.shape[0], in_ref.shape[1]
    values, tops, totals = merged([in_ref[n] for n in range(count)], rows)
    lane = lax.broadcasted_iota(jnp.int32, (rows, LANES - WIDTH), 1)
    extra = jnp.zeros((rows, LANES - WIDTH), F32)
    for h in range(HEADS):
        extra = jnp.where(lane == h, tops[h], extra)
        extra = jnp.where(lane == HEADS + h, totals[h], extra)
    for z in range(NZ):
        out_ref[z, :, 0:WIDTH] = values[4 * z : 4 * z + 4]
        out_ref[z, :, WIDTH:LANES] = extra[4 * z : 4 * z + 4]


def dec_finish_kernel(in_ref, qkv_ref, w_ref, out_ref):
    rows = 4
    values, tops, totals = merged([in_ref[n] for n in range(NZ)], rows)
    query, key = qkv_ref[0].astype(F32), qkv_ref[1].astype(F32)
    value = qkv_ref[2].astype(F32)
    product = query * key
    lane = lax.broadcasted_iota(jnp.int32, (rows, WIDTH), 1)
    old, own, below = [], [], []
    for h in range(HEADS):
        inside = (lane >= h * HD) & (lane < (h + 1) * HD)
        score = jnp.sum(jnp.where(inside, product, 0.0), axis=1, keepdims=True)
        best = jnp.maximum(tops[h], score)
        factor = jnp.exp2((tops[h] - best) * LOG2E_SCALE)
        self_weight = jnp.exp2((score - best) * LOG2E_SCALE)
        old.append(factor)
        own.append(self_weight.astype(BF16).astype(F32))
        below.append(factor * totals[h] + self_weight)
    numerator = by_head(old, rows) * values + by_head(own, rows) * value
    attn = (numerator / by_head(below, rows)).astype(BF16)
    terms = dot(attn, w_ref[...], ((1,), (0,)))
    for t in range(NT):
        out_ref[t] = terms[:, t * WIDTH : (t + 1) * WIDTH]


def prefill_kernel(len_ref, x_ref, gain_ref, w_ref, kc_ref, vc_ref, wo_ref, out_ref, q_s, k_s, v_s, a_s):
    tokens, cached = x_ref.shape[1], kc_ref.shape[1]
    block = 256
    for b in range(tokens // block):
        cols = slice(b * block, (b + 1) * block)
        x = x_ref[:, cols].astype(F32)
        mean_square = jnp.sum(x * x, axis=0, keepdims=True) * (1.0 / x.shape[0])
        hidden = (x * lax.rsqrt(mean_square + EPSILON) * gain_ref[...]).astype(BF16)
        for part, held in enumerate((q_s, k_s, v_s)):
            held[:, cols] = dot(w_ref[part], hidden, ((1,), (0,))).astype(BF16)
    length = len_ref[0]
    for b in range(tokens // block):
        cols = slice(b * block, (b + 1) * block)
        seen = (b + 1) * block
        in_cache = lax.broadcasted_iota(jnp.int32, (cached, block), 0) < length
        causal = lax.broadcasted_iota(jnp.int32, (seen, block), 0) <= (
            lax.broadcasted_iota(jnp.int32, (seen, block), 1) + b * block
        )
        for h in range(HEADS):
            feats = slice(h * HD, (h + 1) * HD)
            query = q_s[feats, cols]
            s_old = jnp.where(in_cache, dot(kc_ref[feats, :], query, ((0,), (0,))), MASKED)
            s_new = jnp.where(causal, dot(k_s[feats, 0:seen], query, ((0,), (0,))), MASKED)
            top = jnp.maximum(
                jnp.max(s_old, axis=0, keepdims=True), jnp.max(s_new, axis=0, keepdims=True)
            )
            w_old = jnp.exp2((s_old - top) * LOG2E_SCALE)
            w_new = jnp.exp2((s_new - top) * LOG2E_SCALE)
            total = jnp.sum(w_old, axis=0, keepdims=True) + jnp.sum(w_new, axis=0, keepdims=True)
            mixed = dot(vc_ref[feats, :], w_old.astype(BF16), ((1,), (0,))) + dot(
                v_s[feats, 0:seen], w_new.astype(BF16), ((1,), (0,))
            )
            a_s[feats, cols] = (mixed / total).astype(BF16)
    for n in range(wo_ref.shape[1] // block):
        cols = slice(n * block, (n + 1) * block)
        out_ref[cols, :] = dot(wo_ref[:, cols], a_s[...], ((0,), (0,)))


def call(kernel, out_shape, scalars, arrays, scratch=(), flops=0, moved=0):
    return pl.pallas_call(
        kernel,
        out_shape=out_shape,
        in_specs=[pl.BlockSpec(memory_space=pltpu.SMEM)] * len(scalars)
        + [pl.BlockSpec(memory_space=pltpu.VMEM)] * len(arrays),
        out_specs=jax.tree.map(lambda _: pl.BlockSpec(memory_space=pltpu.VMEM), out_shape),
        scratch_shapes=scratch,
        compiler_params=pltpu.CompilerParams(vmem_limit_bytes=VMEM_LIMIT),
        cost_estimate=pl.CostEstimate(flops=flops, bytes_accessed=moved, transcendentals=0),
    )(*scalars, *arrays)


def shape(dims, dtype):
    return jax.ShapeDtypeStruct(dims, dtype)


def spread(block, axes, count):
    copies = jnp.broadcast_to(block[None], (count,) + block.shape)
    return lax.all_to_all(copies, axes, 0, 0, tiled=True)


def body(x_pre, x_dec, norm_gain, w_qkv, w_out, pre_keys, pre_values, pre_lens, dec_keys, dec_values, dec_lens):
    tokens, pool = x_pre.shape[0], dec_keys.shape[0]
    full = NT * WIDTH
    w_t = jnp.transpose(w_qkv, (0, 2, 1))
    index = (lax.axis_index("x") * NZ + lax.axis_index("z")) * NC + lax.axis_index("c")
    base = (index * pool).astype(jnp.int32).reshape(1)

    x_all = lax.all_gather(x_pre.T, "tp", axis=0, tiled=True)

    x_rows = spread(x_dec, "tp", NT)
    queries, qkv = call(
        dec_project_kernel,
        (shape((NZ, 4, WIDTH), BF16), shape((3, 4, WIDTH), BF16)),
        (),
        (x_rows, norm_gain.reshape(1, full), w_t),
        scratch=[pltpu.VMEM((8, full), F32)],
        flops=2 * 8 * full * full,
        moved=2 * 3 * full * WIDTH,
    )
    queries = lax.all_to_all(queries, "z", 0, 0, tiled=True)
    queries = spread(queries.reshape(NZ * 4, WIDTH), ("x", "c"), NX * NC)
    queries = queries.reshape(NX * NC * NZ * 4, WIDTH)
    requests = queries.shape[0]
    partial = call(
        dec_attention_kernel,
        shape((requests, LANES), F32),
        (base,),
        (queries, dec_keys.T, dec_values.T, dec_lens.reshape(1, requests)),
        flops=4 * requests * pool * WIDTH,
        moved=4 * pool * WIDTH,
    )
    partial = lax.all_to_all(partial.reshape(NX * NC, NZ * 4, LANES), ("x", "c"), 0, 0, tiled=True)
    partial = call(
        dec_merge_kernel,
        shape((NZ, 4, LANES), F32),
        (),
        (partial,),
        flops=NX * NC * NZ * 4 * LANES,
        moved=NX * NC * NZ * 16 * LANES,
    )
    partial = lax.all_to_all(partial, "z", 0, 0, tiled=True)
    terms = call(
        dec_finish_kernel,
        shape((NT, 4, WIDTH), F32),
        (),
        (partial, qkv, w_out),
        flops=2 * 8 * full * WIDTH,
        moved=2 * full * WIDTH,
    )
    terms = lax.all_to_all(terms, "tp", 0, 0, tiled=True)
    dec_out = jnp.sum(terms, axis=0).astype(BF16)

    terms_pre = call(
        prefill_kernel,
        shape((full, tokens), F32),
        (pre_lens,),
        (x_all, norm_gain.reshape(full, 1), w_t, pre_keys.T, pre_values.T, w_out),
        scratch=[pltpu.VMEM((WIDTH, tokens), BF16)] * 4,
        flops=8 * tokens * full * WIDTH + 4 * tokens * 896 * WIDTH,
        moved=8 * full * WIDTH,
    )
    pre_out = lax.psum_scatter(terms_pre, "tp", scatter_dimension=0, tiled=True)
    return pre_out.astype(BF16).T, dec_out


def solution(mesh):
    req = ("x", "z", "c")
    grid = Mesh(mesh.devices.reshape(NX, NZ, NC, NT), req + ("tp",))
    return jax.shard_map(
        body,
        mesh=grid,
        in_specs=(
            P(req, "tp"),
            P(req, "tp"),
            P(),
            P(None, None, "tp"),
            P("tp", None),
            P(req, "tp"),
            P(req, "tp"),
            P(req),
            P(req, "tp"),
            P(req, "tp"),
            P(),
        ),
        out_specs=(P(req, "tp"), P(req, "tp")),
        check_vma=False,
    )
```

time: 786 us -> 164 us (0.21)
  blocking collectives: 607 us -> 59.9 us
  waiting for transfers between devices: 113 us -> 50.3 us
  matrix products: 29.6 us -> 0 us
  Pallas kernels: 0 us -> 12.7 us
  starting transfers between devices: 0.35 us -> 12.3 us
  other arithmetic: 13.4 us -> 2.44 us
    psum x1 -> x0, blocking collectives: 254 us -> none  [body(): totals_all, partial_all = lax.psum((totals, partial_value), 'req')]
    pmax x1 -> x0, blocking collectives: 250 us -> none  [body(): row_top = lax.pmax(local_top, 'req')]
    all_gather x2 -> x0, blocking collectives: 103 us -> none  [the longest x1 92.8 us: body(): all_queries = lax.all_gather(query_dec, 'req', axis=0, tiled=True)]
    psum x1 -> x0, waiting for transfers between devices: 63.4 us -> none  [body(): totals_all, partial_all = lax.psum((totals, partial_value), 'req')]
    all_to_all x0 -> x4, blocking collectives: none -> 59.9 us  [the longest x1 23.4 us: body(): queries = lax.all_to_all(queries, 'z', 0, 0, tiled=True)]
    reduce_scatter x1, waiting for transfers between devices: 44.2 us -> 0.01 us  [body(): pre_out = lax.psum_scatter(terms_pre, 'tp', scatter_dimension=0, tiled=True)]
    all_gather x1, waiting for transfers between devices: 0.02 us -> 37.3 us  [body(): x_all = lax.all_gather(x_pre.T, 'tp', axis=0, tiled=True)]
    dot_general x9 -> x0, matrix products: 19.9 us -> none  [the longest x5 7.05 us: project(): jnp.dot(hidden, w_qkv[matrix_index], preferred_element_type=jnp.float32)]
  transfers between devices with their start and end apart: 4 -> 4, of which waited for: 3 -> 3; matrix products, arithmetic and copies ran while one was open for 4% -> 2% of each run, Pallas kernels for 0% -> 3%
where the time goes in v1:
time: 164 us; the launch traced here: 161 us
  blocking collectives  59.9 us (37%)
  waiting for transfers between devices  50.3 us (31%)
  between operations  14.7 us (9%)
  Pallas kernels  12.7 us (8%)
  starting transfers between devices  12.3 us (8%)
  local copies, waits for them, and re-layouts  9.05 us (6%)
  other arithmetic  2.44 us (1%)
    all_gather x1, waiting for transfers between devices, body(): x_all = lax.all_gather(x_pre.T, 'tp', axis=0, tiled=True)  37.3 us
    all_to_all x1, blocking collectives, body(): queries = lax.all_to_all(queries, 'z', 0, 0, tiled=True)  23.4 us
    all_to_all x1, blocking collectives, body(): lax.all_to_all(partial.reshape(NX * NC, NZ * 4, LANES), ('x', 'c'), 0, 0,...  15.5 us
    all_to_all x1, blocking collectives, body(): partial = lax.all_to_all(partial, 'z', 0, 0, tiled=True)  14.4 us
    pallas_call x5, Pallas kernels, call(): pl.pallas_call(kernel, out_shape=out_shape, in_specs=[pl.BlockSpec(memory...  12.7 us
    all_to_all x2, starting transfers between devices, spread(): return lax.all_to_all(copies, axes, 0, 0, tiled=True)  12.3 us
    all_to_all x2, waiting for transfers between devices, spread(): return lax.all_to_all(copies, axes, 0, 0, tiled=True)  12.3 us
    unnamed x24, local copies, waits for them, and re-layouts  6.72 us
  transfers between devices with their start and end apart: 4, of which 3 were waited for; matrix products, arithmetic and copies ran while one was open for 2% of the time, Pallas kernels for 3%

profile of v1, /device:TPU:1, one launch (start us, length us, event | category | flops | bytes accessed | tf_op | source)
XLA Modules:
  0.0 161.4 jit_solution(3577052189803408677)
XLA Ops:
  7.2 0.0 all-gather.2.cloned.1.call-start
  7.2 0.7 all-gather.2.cloned.1.call-update
  7.9 0.0 reduce-scatter.2.cloned.1.call-start
  8.6 0.9 reshape.30.gain_ref
  9.5 37.3 %all-gather.2.cloned.1.call-done.x_ref = bf16[1280,512]{1,0:T(8,128)(2,1)} async-done(((bf16[320,512]{1,0:T(8,128)(2,1)}), bf16[1280,512]{1,0:T(8,128)(2,1)}) %all-gather.2.cloned.1.call-update) | async-done | bytes 1310736 | tf_op jit(solution)/shard_map/all_gather | solution.py:203
  46.9 0.0 copy-start
  46.9 1.7 %copy-done = bf16[3,1280,320]{1,2,0:T(8,128)(2,1)S(1)} copy-done((bf16[3,1280,320]{1,2,0:T(8,128)(2,1)S(1)}, bf16[3,1280,320]{1,2,0:T(8,128)(2,1)}, u32[]{:S(2)}) %copy-start) | copy-done | bytes 2457624
  48.6 0.0 copy-start.2
  48.6 1.1 copy-done.2
  49.7 0.0 copy-start.7
  49.7 1.3 copy-done.7
  51.0 0.0 copy-start.8
  51.0 0.9 copy-done.8
  52.0 0.0 copy-start.9
  52.0 0.9 copy-done.9
  52.9 7.4 %shard_map.122 = f32[1280,512]{1,0:T(8,128)} custom-call(s32[1]{0:T(128)S(6)} %copy.14.len_ref, bf16[1280,512]{1,0:T(8,128)(2,1)S(1)} %copy-done.7, f32[1280,1]{1,0:T(8,128)S(1)} %reshape.30.gain_ref, bf16[3,320,1280]{2,1,0:T(8,128)(2,1)S(1)} %bitcast.13, bf16[320,384]{1,0:T(8,128)(2,1)S(1)} %bitcast.19, bf16[320,384]{1,0:T(8,128)(2,1)S(1)} %bitcast.20, ...), custom_call_target="tpu_custom_call" | custom-call | flops 2264924160 | bytes 3276800 | tf_op jit(solution)/shard_map/pallas_call | solution.py:175
  60.3 0.0 copy-start.11
  60.3 0.0 copy-start.10
  60.3 0.0 copy-start.1
  60.3 0.0 reduce-scatter.2.cloned.1.call-update
  60.4 0.7 copy-done.11
  61.0 0.0 copy-start.4
  61.0 0.0 copy-start.5
  61.0 0.0 copy-start.6
  61.0 0.6 broadcast_in_dim.6
  61.6 3.6 %all-to-all-start = ((bf16[4,4,320]{2,1,0:T(4,128)(2,1)}), bf16[4,4,320]{2,1,0:T(4,128)(2,1)S(1)}, u32[]{:S(2)}, u32[]{:S(2)}) async-start(bf16[4,4,320]{2,1,0:T(4,128)(2,1)} %broadcast_in_dim.6), calls=%async_computation.1 | async-start | bytes 24576 | tf_op jit(solution)/shard_map/all_to_all | solution.py:193
  65.2 0.0 copy-done.10
  65.2 4.2 %all-to-all-done.x_ref = bf16[4,4,320]{2,1,0:T(4,128)(2,1)S(1)} async-done(((bf16[4,4,320]{2,1,0:T(4,128)(2,1)}), bf16[4,4,320]{2,1,0:T(4,128)(2,1)S(1)}, u32[]{:S(2)}, u32[]{:S(2)}) %all-to-all-start) | async-done | bytes 10272 | tf_op jit(solution)/shard_map/all_to_all | solution.py:193
  69.4 0.0 copy-done.1
  69.4 0.8 shard_map.123
  70.2 23.4 %all_to_all.30 = bf16[16,4,320]{2,1,0:T(4,128)(2,1)S(1)} all-to-all(bf16[16,4,320]{2,1,0:T(4,128)(2,1)S(1)} %get-tuple-element.4), channel_id=1, replica_groups=mesh['x'=4,'z'=16,'c'=2,'tp'=4] {'z'}, dimensions={0} | all-to-all | bytes 81920 | tf_op jit(solution)/shard_map/all_to_all | solution.py:215
  93.6 0.8 broadcast_in_dim.15
  94.4 8.7 %all-to-all-start.2 = ((bf16[8,64,320]{2,1,0:T(8,128)(2,1)}), bf16[8,64,320]{2,1,0:T(8,128)(2,1)S(1)}, u32[]{:S(2)}, u32[]{:S(2)}) async-start(bf16[8,64,320]{2,1,0:T(8,128)(2,1)} %broadcast_in_dim.15), calls=%async_computation.3 | async-start | bytes 786432 | tf_op jit(solution)/shard_map/all_to_all | solution.py:193
  103.1 0.0 copy-start.3
  103.1 8.1 %all-to-all-done.2 = bf16[8,64,320]{2,1,0:T(8,128)(2,1)S(1)} async-done(((bf16[8,64,320]{2,1,0:T(8,128)(2,1)}), bf16[8,64,320]{2,1,0:T(8,128)(2,1)S(1)}, u32[]{:S(2)}, u32[]{:S(2)}) %all-to-all-start.2) | async-done | bytes 327712 | tf_op jit(solution)/shard_map/all_to_all | solution.py:193
  111.2 0.0 copy-done.4
  111.2 0.0 copy-done.5
  111.2 0.0 copy-done.6
  111.2 3.3 %shard_map.124 = f32[512,384]{1,0:T(8,128)S(1)} custom-call(s32[1]{0:T(128)} %bitcast.5.base_ref, bf16[512,320]{1,0:T(8,128)(2,1)S(1)} %bitcast.15, bf16[320,640]{1,0:T(8,128)(2,1)S(1)} %bitcast.16, bf16[320,640]{1,0:T(8,128)(2,1)S(1)} %bitcast.17, s32[1,512]{1,0:T(1,128)S(1)} %bitcast.18), custom_call_target="tpu_custom_call" | custom-call | flops 419430400 | bytes 819200 | tf_op jit(solution)/shard_map/pallas_call | solution.py:175
  114.4 15.5 %all_to_all.31.in_ref = f32[8,64,384]{2,1,0:T(8,128)S(1)} all-to-all(f32[8,64,384]{2,1,0:T(8,128)S(1)} %bitcast.12), channel_id=1, replica_groups=mesh['x'=4,'z'=16,'c'=2,'tp'=4] {'x','c'}, dimensions={0} | all-to-all | bytes 1572864 | tf_op jit(solution)/shard_map/all_to_all | solution.py:227
  129.9 0.6 shard_map.125
  130.6 14.4 %all_to_all.32.in_ref = f32[16,4,384]{2,1,0:T(4,128)S(1)} all-to-all(f32[16,4,384]{2,1,0:T(4,128)S(1)} %shard_map.125), channel_id=1, replica_groups=mesh['x'=4,'z'=16,'c'=2,'tp'=4] {'z'}, dimensions={0} | all-to-all | bytes 196608 | tf_op jit(solution)/shard_map/all_to_all | solution.py:236
  144.9 0.0 copy-done.3
  144.9 0.6 shard_map.126
  145.5 6.6 %all_to_all.33 = f32[4,4,320]{2,1,0:T(4,128)S(1)} all-to-all(f32[4,4,320]{2,1,0:T(4,128)S(1)} %shard_map.126), channel_id=1, replica_groups=mesh['x'=4,'z'=16,'c'=2,'tp'=4] {'tp'}, dimensions={0} | all-to-all | bytes 40960 | tf_op jit(solution)/shard_map/all_to_all | solution.py:245
  152.1 0.6 reduce_sum.9
  152.7 0.0 reduce-scatter.2.cloned.1.call-done
  152.7 1.9 %convert_bitcast_fusion = bf16[512,320]{0,1:T(8,128)(2,1)} fusion(f32[320,512]{1,0:T(8,128)} %reduce-scatter.2.cloned.1.call-done), kind=kLoop, calls=%fused_computation | loop fusion | flops 163840 | bytes 983040 | tf_op jit(solution)/shard_map/transpose | solution.py:258
  (2 shorter events, 0.0 us)
Async XLA Ops:
  7.2 39.7 %all-gather.2.cloned.1.call-start = ((), (), s32[]{:S(2)}) async-start(), calls=%async_computation.7 | async-start | bytes 1638400 | tf_op jit(solution)/shard_map/all_gather | solution.py:203
  7.9 144.8 %reduce-scatter.2.cloned.1.call-start = ((), (), s32[]{:S(2)}) async-start(), calls=%async_computation.8 | async-start | bytes 3276800 | tf_op jit(solution)/shard_map/reduce_scatter | solution.py:257
  46.9 1.7 %copy-start = (bf16[3,1280,320]{1,2,0:T(8,128)(2,1)S(1)}, bf16[3,1280,320]{1,2,0:T(8,128)(2,1)}, u32[]{:S(2)}) copy-start(bf16[3,1280,320]{1,2,0:T(8,128)(2,1)} %param.14) | copy-start | bytes 7372804
  48.6 1.1 copy-start.2
  49.7 1.3 copy-start.7
  51.0 0.9 copy-start.8
  52.0 0.9 copy-start.9
  60.3 0.7 copy-start.11
  60.3 4.9 %copy-start.10 = (f32[1280]{0:T(1024)S(1)}, f32[1280]{0:T(1024)}, u32[]{:S(2)}) copy-start(f32[1280]{0:T(1024)} %param.13) | copy-start | bytes 15364
  60.3 9.0 %copy-start.1 = (bf16[3,1280,320]{1,2,0:T(8,128)(2,1)S(1)}, bf16[3,1280,320]{1,2,0:T(8,128)(2,1)}, u32[]{:S(2)}) copy-start(bf16[3,1280,320]{1,2,0:T(8,128)(2,1)} %param.14) | copy-start | bytes 7372804
  61.0 50.2 %copy-start.4 = (bf16[640,320]{0,1:T(8,128)(2,1)S(1)}, bf16[640,320]{0,1:T(8,128)(2,1)}, u32[]{:S(2)}) copy-start(bf16[640,320]{0,1:T(8,128)(2,1)} %param.19) | copy-start | bytes 1228804
  61.0 50.2 %copy-start.5 = (bf16[640,320]{0,1:T(8,128)(2,1)S(1)}, bf16[640,320]{0,1:T(8,128)(2,1)}, u32[]{:S(2)}) copy-start(bf16[640,320]{0,1:T(8,128)(2,1)} %param.20) | copy-start | bytes 1228804
  61.0 50.2 %copy-start.6 = (s32[512]{0:T(512)S(1)}, s32[512]{0:T(512)}, u32[]{:S(2)}) copy-start(s32[512]{0:T(512)} %param.21) | copy-start | bytes 6148
  61.6 7.8 %all-to-all-start = ((bf16[4,4,320]{2,1,0:T(4,128)(2,1)}), bf16[4,4,320]{2,1,0:T(4,128)(2,1)S(1)}, u32[]{:S(2)}, u32[]{:S(2)}) async-start(bf16[4,4,320]{2,1,0:T(4,128)(2,1)} %broadcast_in_dim.6), calls=%async_computation.1 | async-start | bytes 24576 | tf_op jit(solution)/shard_map/all_to_all | solution.py:193
  94.4 16.8 %all-to-all-start.2 = ((bf16[8,64,320]{2,1,0:T(8,128)(2,1)}), bf16[8,64,320]{2,1,0:T(8,128)(2,1)S(1)}, u32[]{:S(2)}, u32[]{:S(2)}) async-start(bf16[8,64,320]{2,1,0:T(8,128)(2,1)} %broadcast_in_dim.15), calls=%async_computation.3 | async-start | bytes 786432 | tf_op jit(solution)/shard_map/all_to_all | solution.py:193
  103.1 41.8 %copy-start.3 = (bf16[320,1280]{1,0:T(8,128)(2,1)S(1)}, bf16[320,1280]{1,0:T(8,128)(2,1)}, u32[]{:S(2)}) copy-start(bf16[320,1280]{1,0:T(8,128)(2,1)} %w_ref.1) | copy-start | bytes 2457604
Sparse Core Ops, SparseCore 0:
  10.1 36.7 all-gather.1
  60.5 43.5 reduce-scatter.1

commit v2 on v1

--- a/solution.py
+++ b/solution.py
@@ -17,7 +17,8 @@
 NX, NZ, NC, NT = 4, 16, 2, 4
 LOG2E_SCALE = math.log2(math.e) / math.sqrt(HD)
 F32, BF16 = jnp.float32, jnp.bfloat16
-VMEM_LIMIT = 40 * 1024 * 1024
+VMEM_LIMIT = 24 * 1024 * 1024
+VMEM_ALL = 58 * 1024 * 1024
 
 
 def dot(a, b, dims):
@@ -37,20 +38,25 @@
     return (x * lax.rsqrt(mean_square + EPSILON) * gain).astype(BF16)
 
 
-def dec_project_kernel(x_ref, gain_ref, w_ref, qb_ref, qkv_ref, rows):
+def dec_project_kernel(x_ref, gain_ref, w_hbm, qb_ref, hidden_ref, rows, w_ref, sem):
+    fetch = pltpu.make_async_copy(w_hbm.at[0], w_ref, sem)
+    fetch.start()
     rows[...] = jnp.zeros_like(rows)
     for t in range(NT):
         rows[0:4, t * WIDTH : (t + 1) * WIDTH] = x_ref[t].astype(F32)
     hidden = normed_rows(rows[...], gain_ref[...])
-    for part in range(3):
-        value = dot(hidden, w_ref[part], ((1,), (1,)))[0:4].astype(BF16)
-        qkv_ref[part] = value
-        if part == 0:
-            for z in range(NZ):
-                qb_ref[z] = value
-
-
-def dec_attention_kernel(base_ref, q_ref, k_ref, v_ref, lens_ref, out_ref):
+    hidden_ref[...] = hidden
+    fetch.wait()
+    value = dot(hidden, w_ref[...], ((1,), (1,)))[0:4].astype(BF16)
+    for z in range(NZ):
+        qb_ref[z] = value
+
+
+def dec_attention_kernel(base_ref, q_ref, lens_ref, k_hbm, v_hbm, out_ref, k_ref, v_ref, sems):
+    fetch_k = pltpu.make_async_copy(k_hbm, k_ref, sems.at[0])
+    fetch_v = pltpu.make_async_copy(v_hbm, v_ref, sems.at[1])
+    fetch_k.start()
+    fetch_v.start()
     requests, pool = q_ref.shape[0], k_ref.shape[1]
     place = lax.broadcasted_iota(jnp.int32, (requests, requests), 0)
     x, c, z, i = place >> 7, (place >> 6) & 1, (place >> 2) & 15, place & 3
@@ -62,8 +68,9 @@
     base = base_ref[0].astype(F32)
     row = lax.broadcasted_iota(jnp.int32, (requests, pool), 1).astype(F32) + base
     allowed = (row >= begin) & (row < end)
-    lane = lax.broadcasted_iota(jnp.int32, (requests, LANES - WIDTH), 1)
-    extra = jnp.zeros((requests, LANES - WIDTH), F32)
+    tops, totals = [], []
+    fetch_k.wait()
+    fetch_v.wait()
     for h in range(HEADS):
         s = dot(q_ref[:, h * HD : (h + 1) * HD], k_ref[h * HD : (h + 1) * HD, :], ((1,), (0,)))
         s = jnp.where(allowed, s, MASKED)
@@ -71,25 +78,48 @@
         w = jnp.where(allowed, jnp.exp2((s - top) * LOG2E_SCALE), 0.0)
         total = jnp.sum(w, axis=1, keepdims=True)
         mixed = dot(w.astype(BF16), v_ref[h * HD : (h + 1) * HD, :], ((1,), (1,)))
-        out_ref[:, h * HD : (h + 1) * HD] = mixed
-        extra = jnp.where(lane == h, top, extra)
-        extra = jnp.where(lane == HEADS + h, total, extra)
-    out_ref[:, WIDTH:LANES] = extra
+        out_ref[:, h * HD : (h + 1) * HD] = mixed.astype(BF16)
+        tops.append(top)
+        totals.append(total)
+    out_ref[:, WIDTH:LANES] = stats(tops, totals, requests)
+
+
+def thirds(value):
+    high = value.astype(BF16)
+    rest = value - high.astype(F32)
+    middle = rest.astype(BF16)
+    return high, middle, (rest - middle.astype(F32)).astype(BF16)
+
+
+def stats(tops, totals, rows):
+    lane = lax.broadcasted_iota(jnp.int32, (rows, LANES - WIDTH), 1)
+    out = jnp.zeros((rows, LANES - WIDTH), F32)
+    for n, value in enumerate(tops + totals):
+        for k, part in enumerate(thirds(value)):
+            out = jnp.where(lane == 3 * n + k, part.astype(F32), out)
+    return out.astype(BF16)
+
+
+def stat(block, n):
+    at = WIDTH + 3 * n
+    return block[:, at : at + 1] + block[:, at + 1 : at + 2] + block[:, at + 2 : at + 3]
 
 
 def merged(parts, rows):
+    parts = [part.astype(F32) for part in parts]
     tops, totals, values = [], [], jnp.zeros((rows, WIDTH), F32)
     scales = []
     for h in range(HEADS):
-        best = parts[0][:, WIDTH + h : WIDTH + h + 1]
-        for part in parts[1:]:
-            best = jnp.maximum(best, part[:, WIDTH + h : WIDTH + h + 1])
+        part_tops = [stat(part, h) for part in parts]
+        best = part_tops[0]
+        for top in part_tops[1:]:
+            best = jnp.maximum(best, top)
         tops.append(best)
-        scale = [jnp.exp2((part[:, WIDTH + h : WIDTH + h + 1] - best) * LOG2E_SCALE) for part in parts]
+        scale = [jnp.exp2((top - best) * LOG2E_SCALE) for top in part_tops]
         scales.append(scale)
         total = jnp.zeros_like(best)
         for part, factor in zip(parts, scale):
-            total = total + factor * part[:, WIDTH + HEADS + h : WIDTH + HEADS + h + 1]
+            total = total + factor * stat(part, HEADS + h)
         totals.append(total)
     for n, part in enumerate(parts):
         values = values + by_head([scales[h][n] for h in range(HEADS)], rows) * part[:, :WIDTH]
@@ -99,21 +129,18 @@
 def dec_merge_kernel(in_ref, out_ref):
     count, rows = in_ref.shape[0], in_ref.shape[1]
     values, tops, totals = merged([in_ref[n] for n in range(count)], rows)
-    lane = lax.broadcasted_iota(jnp.int32, (rows, LANES - WIDTH), 1)
-    extra = jnp.zeros((rows, LANES - WIDTH), F32)
-    for h in range(HEADS):
-        extra = jnp.where(lane == h, tops[h], extra)
-        extra = jnp.where(lane == HEADS + h, totals[h], extra)
+    extra = stats(tops, totals, rows)
+    values = values.astype(BF16)
     for z in range(NZ):
         out_ref[z, :, 0:WIDTH] = values[4 * z : 4 * z + 4]
         out_ref[z, :, WIDTH:LANES] = extra[4 * z : 4 * z + 4]
 
 
-def dec_finish_kernel(in_ref, qkv_ref, w_ref, out_ref):
+def dec_finish_kernel(in_ref, q_ref, kv_ref, w_ref, out_ref):
     rows = 4
     values, tops, totals = merged([in_ref[n] for n in range(NZ)], rows)
-    query, key = qkv_ref[0].astype(F32), qkv_ref[1].astype(F32)
-    value = qkv_ref[2].astype(F32)
+    query, key = q_ref[0].astype(F32), kv_ref[0].astype(F32)
+    value = kv_ref[1].astype(F32)
     product = query * key
     lane = lax.broadcasted_iota(jnp.int32, (rows, WIDTH), 1)
     old, own, below = [], [], []
@@ -133,16 +160,37 @@
         out_ref[t] = terms[:, t * WIDTH : (t + 1) * WIDTH]
 
 
-def prefill_kernel(len_ref, x_ref, gain_ref, w_ref, kc_ref, vc_ref, wo_ref, out_ref, q_s, k_s, v_s, a_s):
+def prefill_kernel(
+    len_ref, gain_ref, hd_ref, x_hbm, w_hbm, kc_hbm, vc_hbm, wo_hbm,
+    first_ref, second_ref, kv_ref,
+    x_ref, w_ref, kc_ref, vc_ref, wo_ref, q_s, k_s, v_s, a_s, sems,
+):
     tokens, cached = x_ref.shape[1], kc_ref.shape[1]
     block = 256
+    fetches = [
+        pltpu.make_async_copy(source, target, sems.at[n])
+        for n, (source, target) in enumerate(
+            [(x_hbm.at[:, 0:block], x_ref.at[:, 0:block]), (w_hbm, w_ref)]
+            + [(x_hbm.at[:, block:tokens], x_ref.at[:, block:tokens])]
+            + [(kc_hbm, kc_ref), (vc_hbm, vc_ref), (wo_hbm, wo_ref)]
+        )
+    ]
+    for fetch in fetches:
+        fetch.start()
     for b in range(tokens // block):
         cols = slice(b * block, (b + 1) * block)
+        fetches[0 if b == 0 else 2].wait()
         x = x_ref[:, cols].astype(F32)
         mean_square = jnp.sum(x * x, axis=0, keepdims=True) * (1.0 / x.shape[0])
         hidden = (x * lax.rsqrt(mean_square + EPSILON) * gain_ref[...]).astype(BF16)
+        if b == 0:
+            fetches[1].wait()
+            for part in (1, 2):
+                kv_ref[part - 1] = dot(hd_ref[...], w_ref[part], ((1,), (1,)))[0:4].astype(BF16)
         for part, held in enumerate((q_s, k_s, v_s)):
             held[:, cols] = dot(w_ref[part], hidden, ((1,), (0,))).astype(BF16)
+    fetches[3].wait()
+    fetches[4].wait()
     length = len_ref[0]
     for b in range(tokens // block):
         cols = slice(b * block, (b + 1) * block)
@@ -166,22 +214,28 @@
                 v_s[feats, 0:seen], w_new.astype(BF16), ((1,), (0,))
             )
             a_s[feats, cols] = (mixed / total).astype(BF16)
-    for n in range(wo_ref.shape[1] // block):
-        cols = slice(n * block, (n + 1) * block)
-        out_ref[cols, :] = dot(wo_ref[:, cols], a_s[...], ((0,), (0,)))
-
-
-def call(kernel, out_shape, scalars, arrays, scratch=(), flops=0, moved=0):
+        if b == 0:
+            fetches[5].wait()
+        out_ref = first_ref if b == 0 else second_ref
+        for n in range(wo_ref.shape[1] // block):
+            outs = slice(n * block, (n + 1) * block)
+            out_ref[outs, :] = dot(wo_ref[:, outs], a_s[:, cols], ((0,), (0,)))
+
+
+def call(
+    kernel, out_shape, scalars, arrays, stored=(), scratch=(), flops=0, moved=0, limit=VMEM_LIMIT
+):
     return pl.pallas_call(
         kernel,
         out_shape=out_shape,
         in_specs=[pl.BlockSpec(memory_space=pltpu.SMEM)] * len(scalars)
-        + [pl.BlockSpec(memory_space=pltpu.VMEM)] * len(arrays),
+        + [pl.BlockSpec(memory_space=pltpu.VMEM)] * len(arrays)
+        + [pl.BlockSpec(memory_space=pltpu.HBM)] * len(stored),
         out_specs=jax.tree.map(lambda _: pl.BlockSpec(memory_space=pltpu.VMEM), out_shape),
         scratch_shapes=scratch,
-        compiler_params=pltpu.CompilerParams(vmem_limit_bytes=VMEM_LIMIT),
+        compiler_params=pltpu.CompilerParams(vmem_limit_bytes=limit),
         cost_estimate=pl.CostEstimate(flops=flops, bytes_accessed=moved, transcendentals=0),
-    )(*scalars, *arrays)
+    )(*scalars, *arrays, *stored)
 
 
 def shape(dims, dtype):
@@ -200,34 +254,72 @@
     index = (lax.axis_index("x") * NZ + lax.axis_index("z")) * NC + lax.axis_index("c")
     base = (index * pool).astype(jnp.int32).reshape(1)
 
+    x_rows = spread(x_dec, "tp", NT)
     x_all = lax.all_gather(x_pre.T, "tp", axis=0, tiled=True)
-
-    x_rows = spread(x_dec, "tp", NT)
-    queries, qkv = call(
+    queries, hidden = call(
         dec_project_kernel,
-        (shape((NZ, 4, WIDTH), BF16), shape((3, 4, WIDTH), BF16)),
+        (shape((NZ, 4, WIDTH), BF16), shape((8, full), BF16)),
         (),
-        (x_rows, norm_gain.reshape(1, full), w_t),
-        scratch=[pltpu.VMEM((8, full), F32)],
-        flops=2 * 8 * full * full,
-        moved=2 * 3 * full * WIDTH,
-    )
+        (x_rows, norm_gain.reshape(1, full)),
+        (w_t,),
+        scratch=[
+            pltpu.VMEM((8, full), F32),
+            pltpu.VMEM((WIDTH, full), BF16),
+            pltpu.SemaphoreType.DMA,
+        ],
+        flops=2 * 8 * full * WIDTH,
+        moved=2 * full * WIDTH,
+        limit=VMEM_ALL,
+    )
+    own_queries = queries
     queries = lax.all_to_all(queries, "z", 0, 0, tiled=True)
+    x_all, queries = lax.optimization_barrier((x_all, queries))
+    half = tokens // 2
+    first, second, own_kv = call(
+        prefill_kernel,
+        (shape((full, half), F32), shape((full, half), F32), shape((2, 4, WIDTH), BF16)),
+        (pre_lens,),
+        (norm_gain.reshape(full, 1), hidden),
+        (x_all, w_t, pre_keys.T, pre_values.T, w_out),
+        scratch=[
+            pltpu.VMEM((full, tokens), BF16),
+            pltpu.VMEM((3, WIDTH, full), BF16),
+            pltpu.VMEM((WIDTH, pre_keys.shape[0]), BF16),
+            pltpu.VMEM((WIDTH, pre_keys.shape[0]), BF16),
+            pltpu.VMEM((WIDTH, full), BF16),
+        ]
+        + [pltpu.VMEM((WIDTH, tokens), BF16)] * 4
+        + [pltpu.SemaphoreType.DMA((6,))],
+        flops=8 * tokens * full * WIDTH + 4 * tokens * 896 * WIDTH,
+        moved=8 * full * WIDTH,
+        limit=VMEM_ALL,
+    )
     queries = spread(queries.reshape(NZ * 4, WIDTH), ("x", "c"), NX * NC)
+    first, second, queries = lax.optimization_barrier((first, second, queries))
+    pre_out = jnp.concatenate(
+        [lax.psum_scatter(part, "tp", scatter_dimension=0, tiled=True) for part in (first, second)],
+        axis=1,
+    )
     queries = queries.reshape(NX * NC * NZ * 4, WIDTH)
     requests = queries.shape[0]
     partial = call(
         dec_attention_kernel,
-        shape((requests, LANES), F32),
+        shape((requests, LANES), BF16),
         (base,),
-        (queries, dec_keys.T, dec_values.T, dec_lens.reshape(1, requests)),
+        (queries, dec_lens.reshape(1, requests)),
+        (dec_keys.T, dec_values.T),
+        scratch=[
+            pltpu.VMEM((WIDTH, pool), BF16),
+            pltpu.VMEM((WIDTH, pool), BF16),
+            pltpu.SemaphoreType.DMA((2,)),
+        ],
         flops=4 * requests * pool * WIDTH,
         moved=4 * pool * WIDTH,
     )
     partial = lax.all_to_all(partial.reshape(NX * NC, NZ * 4, LANES), ("x", "c"), 0, 0, tiled=True)
     partial = call(
         dec_merge_kernel,
-        shape((NZ, 4, LANES), F32),
+        shape((NZ, 4, LANES), BF16),
         (),
         (partial,),
         flops=NX * NC * NZ * 4 * LANES,
@@ -238,23 +330,12 @@
         dec_finish_kernel,
         shape((NT, 4, WIDTH), F32),
         (),
-        (partial, qkv, w_out),
+        (partial, own_queries, own_kv, w_out),
         flops=2 * 8 * full * WIDTH,
         moved=2 * full * WIDTH,
     )
     terms = lax.all_to_all(terms, "tp", 0, 0, tiled=True)
     dec_out = jnp.sum(terms, axis=0).astype(BF16)
-
-    terms_pre = call(
-        prefill_kernel,
-        shape((full, tokens), F32),
-        (pre_lens,),
-        (x_all, norm_gain.reshape(full, 1), w_t, pre_keys.T, pre_values.T, w_out),
-        scratch=[pltpu.VMEM((WIDTH, tokens), BF16)] * 4,
-        flops=8 * tokens * full * WIDTH + 4 * tokens * 896 * WIDTH,
-        moved=8 * full * WIDTH,
-    )
-    pre_out = lax.psum_scatter(terms_pre, "tp", scatter_dimension=0, tiled=True)
     return pre_out.astype(BF16).T, dec_out
 
 

time: 164 us -> 143 us (0.87)
  waiting for transfers between devices: 50.3 us -> 18.7 us
  Pallas kernels: 12.7 us -> 20.2 us
  blocking collectives: 59.9 us -> 66.8 us
  local copies, waits for them, and re-layouts: 9.05 us -> 5.47 us
    all_gather x1, waiting for transfers between devices: 37.3 us -> 0.01 us  [body(): x_all = lax.all_gather(x_pre.T, 'tp', axis=0, tiled=True)]
    reduce_scatter x1 -> x2, waiting for transfers between devices: 0.01 us -> 14.4 us  [body(): lax.psum_scatter(part, 'tp', scatter_dimension=0, tiled=True)]
    all_to_all x2, waiting for transfers between devices: 12.3 us -> 2.9 us  [spread(): return lax.all_to_all(copies, axes, 0, 0, tiled=True)]
    pallas_call x5, Pallas kernels: 12.7 us -> 20.2 us  [call(): pl.pallas_call(kernel, out_shape=out_shape, in_specs=[pl.BlockSpec(memory...]
    all_to_all x1, blocking collectives: 14.4 us -> 20.2 us  [body(): partial = lax.all_to_all(partial, 'z', 0, 0, tiled=True)]
    unnamed x24 -> x16, local copies, waits for them, and re-layouts: 6.72 us -> 0.95 us
    all_to_all x1, blocking collectives: 23.4 us -> 26.6 us  [body(): queries = lax.all_to_all(queries, 'z', 0, 0, tiled=True)]
    all_to_all x1, blocking collectives: 15.5 us -> 12.7 us  [body(): lax.all_to_all(partial.reshape(NX * NC, NZ * 4, LANES), ('x', 'c'), 0, 0,...]
  transfers between devices with their start and end apart: 4 -> 5, of which waited for: 3 -> 2; matrix products, arithmetic and copies ran while one was open for 2% -> 4% of each run, Pallas kernels for 3% -> 14%
where the time goes in v2:
time: 143 us; the launch traced here: 142 us
  blocking collectives  66.8 us (47%)
  Pallas kernels  20.2 us (14%)
  waiting for transfers between devices  18.7 us (13%)
  between operations  14.5 us (10%)
  starting transfers between devices  12.8 us (9%)
  local copies, waits for them, and re-layouts  5.47 us (4%)
  other arithmetic  3.33 us (2%)
    all_to_all x1, blocking collectives, body(): queries = lax.all_to_all(queries, 'z', 0, 0, tiled=True)  26.6 us
    pallas_call x5, Pallas kernels, call(): pl.pallas_call(kernel, out_shape=out_shape, in_specs=[pl.BlockSpec(memory...  20.2 us
    all_to_all x1, blocking collectives, body(): partial = lax.all_to_all(partial, 'z', 0, 0, tiled=True)  20.2 us
    reduce_scatter x2, waiting for transfers between devices, body(): lax.psum_scatter(part, 'tp', scatter_dimension=0, tiled=True)  14.4 us
    all_to_all x2, starting transfers between devices, spread(): return lax.all_to_all(copies, axes, 0, 0, tiled=True)  12.8 us
    all_to_all x1, blocking collectives, body(): lax.all_to_all(partial.reshape(NX * NC, NZ * 4, LANES), ('x', 'c'), 0, 0,...  12.7 us
    all_to_all x1, blocking collectives, body(): terms = lax.all_to_all(terms, 'tp', 0, 0, tiled=True)  7.38 us
    all_to_all x2, waiting for transfers between devices, spread(): return lax.all_to_all(copies, axes, 0, 0, tiled=True)  2.9 us
  transfers between devices with their start and end apart: 5, of which 2 were waited for; matrix products, arithmetic and copies ran while one was open for 4% of the time, Pallas kernels for 14%

profile of v2, /device:TPU:1, one launch (start us, length us, event | category | flops | bytes accessed | tf_op | source)
XLA Modules:
  0.0 141.9 jit_solution(16980520041441169126)
XLA Ops:
  7.2 0.0 all-gather.2.cloned.1.call-start
  7.2 0.7 all-gather.2.cloned.1.call-update
  7.9 1.3 broadcast_in_dim.6
  9.2 5.0 %all-to-all-start = ((bf16[4,4,320]{2,1,0:T(4,128)(2,1)}), bf16[4,4,320]{2,1,0:T(4,128)(2,1)S(1)}, u32[]{:S(2)}, u32[]{:S(2)}) async-start(bf16[4,4,320]{2,1,0:T(4,128)(2,1)} %broadcast_in_dim.6), calls=%async_computation | async-start | bytes 24576 | tf_op jit(solution)/shard_map/all_to_all | solution.py:247
  14.2 1.3 reshape.25.gain_ref
  15.5 2.9 %all-to-all-done.x_ref = bf16[4,4,320]{2,1,0:T(4,128)(2,1)S(1)} async-done(((bf16[4,4,320]{2,1,0:T(4,128)(2,1)}), bf16[4,4,320]{2,1,0:T(4,128)(2,1)S(1)}, u32[]{:S(2)}, u32[]{:S(2)}) %all-to-all-start) | async-done | bytes 10272 | tf_op jit(solution)/shard_map/all_to_all | solution.py:247
  18.4 0.0 copy-start.6
  18.4 0.6 copy-done.6
  19.0 2.8 %shard_map.122 = (bf16[16,4,320]{2,1,0:T(4,128)(2,1)}, bf16[8,1280]{1,0:T(8,128)(2,1)}) custom-call(bf16[4,4,320]{2,1,0:T(4,128)(2,1)} %copy-done.6, f32[1,1280]{1,0:T(1,128)} %reshape.25.gain_ref, bf16[3,320,1280]{2,1,0:T(8,128)(2,1)} %bitcast.17), custom_call_target="tpu_custom_call" | custom-call | flops 6553600 | bytes 819200 | tf_op jit(solution)/shard_map/pallas_call | solution.py:228
  21.8 0.0 copy-start.7
  21.8 26.6 %all_to_all.30 = bf16[16,4,320]{2,1,0:T(4,128)(2,1)S(1)} all-to-all(bf16[16,4,320]{2,1,0:T(4,128)(2,1)} %get-tuple-element.13.q_ref), channel_id=1, replica_groups=mesh['x'=4,'z'=16,'c'=2,'tp'=4] {'z'}, dimensions={0} | all-to-all | bytes 81920 | tf_op jit(solution)/shard_map/all_to_all | solution.py:275
  48.4 0.0 all-gather.2.cloned.1.call-done.x_hbm
  48.4 0.8 broadcast_in_dim.15
  49.3 7.7 %all-to-all-start.2 = ((bf16[8,64,320]{2,1,0:T(8,128)(2,1)}), bf16[8,64,320]{2,1,0:T(8,128)(2,1)S(1)}, u32[]{:S(2)}, u32[]{:S(2)}) async-start(bf16[8,64,320]{2,1,0:T(8,128)(2,1)} %broadcast_in_dim.15), calls=%async_computation.2 | async-start | bytes 786432 | tf_op jit(solution)/shard_map/all_to_all | solution.py:247
  57.0 0.0 reduce-scatter.3.cloned.1.call-start
  57.0 0.0 copy-done.7
  57.0 1.1 reshape.30.gain_ref
  58.7 11.5 %shard_map.123 = (f32[1280,256]{1,0:T(8,128)}, f32[1280,256]{1,0:T(8,128)}, bf16[2,4,320]{2,1,0:T(4,128)(2,1)}) custom-call(s32[1]{0:T(128)S(6)} %copy.14.len_ref, f32[1280,1]{1,0:T(8,128)} %reshape.30.gain_ref, bf16[8,1280]{1,0:T(8,128)(2,1)} %get-tuple-element.12.hd_ref, bf16[1280,512]{1,0:T(8,128)(2,1)} %all-gather.2.cloned.1.call-done.x_hbm, ...), custom_call_target="tpu_custom_call" | custom-call | flops 2264924160 | bytes 3276800 | tf_op jit(solution)/shard_map/pallas_call | solution.py:228
  70.2 0.0 all-to-all-done.2
  70.2 0.0 copy-start.1
  70.2 0.0 copy-start.2
  70.3 0.0 copy-start.5
  70.3 0.0 reduce-scatter.3.cloned.1.call-update
  70.3 0.0 reduce-scatter.5.cloned.1.call-start
  70.3 0.7 reduce-scatter.5.cloned.1.call-update
  71.0 0.2 copy-done.1
  71.2 0.1 copy-done.2
  71.4 0.0 copy-done.5
  71.4 0.0 copy-start
  71.4 0.0 copy-start.3
  71.4 0.0 copy-start.4
  71.4 4.5 %shard_map.124 = bf16[512,384]{1,0:T(8,128)(2,1)S(1)} custom-call(s32[1]{0:T(128)} %bitcast.5.base_ref, bf16[512,320]{1,0:T(8,128)(2,1)S(1)} %bitcast.12, s32[1,512]{1,0:T(1,128)S(1)} %bitcast.16, bf16[320,640]{1,0:T(8,128)(2,1)S(1)} %bitcast.14, bf16[320,640]{1,0:T(8,128)(2,1)S(1)} %bitcast.15), custom_call_target="tpu_custom_call" | custom-call | flops 419430400 | bytes 819200 | tf_op jit(solution)/shard_map/pallas_call | solution.py:228
  75.9 12.7 %all_to_all.31.in_ref = bf16[8,64,384]{2,1,0:T(8,128)(2,1)S(1)} all-to-all(bf16[8,64,384]{2,1,0:T(8,128)(2,1)S(1)} %bitcast.13), channel_id=1, replica_groups=mesh['x'=4,'z'=16,'c'=2,'tp'=4] {'x','c'}, dimensions={0} | all-to-all | bytes 786432 | tf_op jit(solution)/shard_map/all_to_all | solution.py:319
  88.6 0.8 shard_map.125
  89.4 20.2 %all_to_all.32.in_ref = bf16[16,4,384]{2,1,0:T(4,128)(2,1)S(1)} all-to-all(bf16[16,4,384]{2,1,0:T(4,128)(2,1)S(1)} %shard_map.125), channel_id=1, replica_groups=mesh['x'=4,'z'=16,'c'=2,'tp'=4] {'z'}, dimensions={0} | all-to-all | bytes 98304 | tf_op jit(solution)/shard_map/all_to_all | solution.py:328
  109.6 0.0 copy-done
  109.6 0.0 copy-done.3
  109.6 0.0 copy-done.4
  109.6 0.6 shard_map.126
  110.2 7.4 %all_to_all.33 = f32[4,4,320]{2,1,0:T(4,128)S(1)} all-to-all(f32[4,4,320]{2,1,0:T(4,128)S(1)} %shard_map.126), channel_id=1, replica_groups=mesh['x'=4,'z'=16,'c'=2,'tp'=4] {'tp'}, dimensions={0} | all-to-all | bytes 40960 | tf_op jit(solution)/shard_map/all_to_all | solution.py:337
  117.5 0.6 reduce_sum.9
  118.1 0.0 reduce-scatter.3.cloned.1.call-done
  118.1 1.0 convert.6
  119.1 14.4 %reduce-scatter.5.cloned.1.call-done = f32[320,256]{1,0:T(8,128)} async-done(((f32[1280,256]{1,0:T(8,128)}), f32[320,256]{1,0:T(8,128)}) %reduce-scatter.5.cloned.1.call-update) | async-done | bytes 327696 | tf_op jit(solution)/shard_map/reduce_scatter | solution.py:300
  133.6 1.0 convert.7
  134.6 0.7 maximum_bitcast_fusion
  (1 shorter events, 0.0 us)
Async XLA Ops:
  7.2 41.2 %all-gather.2.cloned.1.call-start = ((), (), s32[]{:S(2)}) async-start(), calls=%async_computation.8 | async-start | bytes 1638400 | tf_op jit(solution)/shard_map/all_gather | solution.py:258
  9.2 9.2 %all-to-all-start = ((bf16[4,4,320]{2,1,0:T(4,128)(2,1)}), bf16[4,4,320]{2,1,0:T(4,128)(2,1)S(1)}, u32[]{:S(2)}, u32[]{:S(2)}) async-start(bf16[4,4,320]{2,1,0:T(4,128)(2,1)} %broadcast_in_dim.6), calls=%async_computation | async-start | bytes 24576 | tf_op jit(solution)/shard_map/all_to_all | solution.py:247
  18.4 0.6 copy-start.6
  21.8 35.2 %copy-start.7 = (f32[1280]{0:T(1024)S(1)}, f32[1280]{0:T(1024)}, u32[]{:S(2)}) copy-start(f32[1280]{0:T(1024)} %param.13) | copy-start | bytes 15364
  49.3 21.0 %all-to-all-start.2 = ((bf16[8,64,320]{2,1,0:T(8,128)(2,1)}), bf16[8,64,320]{2,1,0:T(8,128)(2,1)S(1)}, u32[]{:S(2)}, u32[]{:S(2)}) async-start(bf16[8,64,320]{2,1,0:T(8,128)(2,1)} %broadcast_in_dim.15), calls=%async_computation.2 | async-start | bytes 786432 | tf_op jit(solution)/shard_map/all_to_all | solution.py:247
  57.0 61.1 %reduce-scatter.3.cloned.1.call-start = ((), (), s32[]{:S(2)}) async-start(), calls=%async_computation.9 | async-start | bytes 1638400 | tf_op jit(solution)/shard_map/reduce_scatter | solution.py:300
  70.2 1.0 copy-start.1
  70.2 1.1 copy-start.2
  70.3 1.1 copy-start.5
  70.3 63.3 %reduce-scatter.5.cloned.1.call-start = ((), (), s32[]{:S(2)}) async-start(), calls=%async_computation.10 | async-start | bytes 1638400 | tf_op jit(solution)/shard_map/reduce_scatter | solution.py:300
  71.4 38.2 %copy-start = (bf16[320,1280]{1,0:T(8,128)(2,1)S(1)}, bf16[320,1280]{1,0:T(8,128)(2,1)}, u32[]{:S(2)}) copy-start(bf16[320,1280]{1,0:T(8,128)(2,1)} %w_ref.1) | copy-start | bytes 2457604
  71.4 38.2 %copy-start.3 = (bf16[16,4,320]{2,1,0:T(4,128)(2,1)S(1)}, bf16[16,4,320]{2,1,0:T(4,128)(2,1)}, u32[]{:S(2)}) copy-start(bf16[16,4,320]{2,1,0:T(4,128)(2,1)} %get-tuple-element.13.q_ref) | copy-start | bytes 122884
  71.4 38.2 %copy-start.4 = (bf16[2,4,320]{2,1,0:T(4,128)(2,1)S(1)}, bf16[2,4,320]{2,1,0:T(4,128)(2,1)}, u32[]{:S(2)}) copy-start(bf16[2,4,320]{2,1,0:T(4,128)(2,1)} %get-tuple-element.21.kv_ref) | copy-start | bytes 15364
Sparse Core Ops, SparseCore 0:
  10.1 36.7 all-gather.1
  70.4 28.2 reduce-scatter.2
  101.6 31.9 reduce-scatter.4

commit v3 on v2

--- a/solution.py
+++ b/solution.py
@@ -38,33 +38,45 @@
     return (x * lax.rsqrt(mean_square + EPSILON) * gain).astype(BF16)
 
 
-def dec_project_kernel(x_ref, gain_ref, w_hbm, qb_ref, hidden_ref, rows, w_ref, sem):
+def dec_project_kernel(x_ref, gain_ref, w_hbm, qb_ref, q_ref, hidden_ref, rows, w_ref, sem):
     fetch = pltpu.make_async_copy(w_hbm.at[0], w_ref, sem)
     fetch.start()
-    rows[...] = jnp.zeros_like(rows)
-    for t in range(NT):
-        rows[0:4, t * WIDTH : (t + 1) * WIDTH] = x_ref[t].astype(F32)
+    for n in range(NX * NC):
+        for t in range(NT):
+            rows[4 * n : 4 * n + 4, t * WIDTH : (t + 1) * WIDTH] = x_ref[NT * n + t].astype(F32)
     hidden = normed_rows(rows[...], gain_ref[...])
     hidden_ref[...] = hidden
     fetch.wait()
-    value = dot(hidden, w_ref[...], ((1,), (1,)))[0:4].astype(BF16)
+    value = dot(hidden, w_ref[...], ((1,), (1,)))
+    q_ref[...] = value.astype(BF16)
+    tail = jnp.concatenate([value[0:16, 256:WIDTH], value[16:32, 256:WIDTH]], axis=1)
+    packed = jnp.concatenate([value[:, 0:128], value[:, 128:256], tail], axis=0).astype(BF16)
     for z in range(NZ):
-        qb_ref[z] = value
-
-
-def dec_attention_kernel(base_ref, q_ref, lens_ref, k_hbm, v_hbm, out_ref, k_ref, v_ref, sems):
+        qb_ref[z] = packed
+
+
+def dec_attention_kernel(base_ref, qp_ref, lens_ref, k_hbm, v_hbm, out_ref, q_s, k_ref, v_ref, sems):
     fetch_k = pltpu.make_async_copy(k_hbm, k_ref, sems.at[0])
     fetch_v = pltpu.make_async_copy(v_hbm, v_ref, sems.at[1])
     fetch_k.start()
     fetch_v.start()
-    requests, pool = q_ref.shape[0], k_ref.shape[1]
+    for z in range(NZ):
+        rows = slice(32 * z, 32 * z + 32)
+        q_s[rows, 0:128] = qp_ref[z, 0:32]
+        q_s[rows, 128:256] = qp_ref[z, 32:64]
+        q_s[32 * z : 32 * z + 16, 256:WIDTH] = qp_ref[z, 64:80, 0:64]
+        q_s[32 * z + 16 : 32 * z + 32, 256:WIDTH] = qp_ref[z, 64:80, 64:128]
+    requests, pool = q_s.shape[0], k_ref.shape[1]
     place = lax.broadcasted_iota(jnp.int32, (requests, requests), 0)
     x, c, z, i = place >> 7, (place >> 6) & 1, (place >> 2) & 15, place & 3
     request = (x << 7) | (z << 3) | (c << 2) | i
+    arrived = (z << 5) | (x << 3) | (c << 2) | i
     other = lax.broadcasted_iota(jnp.int32, (requests, requests), 1)
     lens = lens_ref[...].astype(F32)
     begin = jnp.sum(jnp.where(other < request, lens, 0.0), axis=1, keepdims=True)
     end = jnp.sum(jnp.where(other <= request, lens, 0.0), axis=1, keepdims=True)
+    order = jnp.where(other == arrived, 1.0, 0.0).astype(BF16)
+    queries = dot(order, q_s[...], ((1,), (0,))).astype(BF16)
     base = base_ref[0].astype(F32)
     row = lax.broadcasted_iota(jnp.int32, (requests, pool), 1).astype(F32) + base
     allowed = (row >= begin) & (row < end)
@@ -72,7 +84,7 @@
     fetch_k.wait()
     fetch_v.wait()
     for h in range(HEADS):
-        s = dot(q_ref[:, h * HD : (h + 1) * HD], k_ref[h * HD : (h + 1) * HD, :], ((1,), (0,)))
+        s = dot(queries[:, h * HD : (h + 1) * HD], k_ref[h * HD : (h + 1) * HD, :], ((1,), (0,)))
         s = jnp.where(allowed, s, MASKED)
         top = jnp.max(s, axis=1, keepdims=True)
         w = jnp.where(allowed, jnp.exp2((s - top) * LOG2E_SCALE), 0.0)
@@ -136,11 +148,14 @@
         out_ref[z, :, WIDTH:LANES] = extra[4 * z : 4 * z + 4]
 
 
-def dec_finish_kernel(in_ref, q_ref, kv_ref, w_ref, out_ref):
+def dec_finish_kernel(own_ref, in_ref, q_ref, kv_ref, w_ref, out_ref):
     rows = 4
     values, tops, totals = merged([in_ref[n] for n in range(NZ)], rows)
-    query, key = q_ref[0].astype(F32), kv_ref[0].astype(F32)
-    value = kv_ref[1].astype(F32)
+    row = lax.broadcasted_iota(jnp.int32, (8, 32), 0) + 4 * own_ref[0]
+    mine = jnp.where(row == lax.broadcasted_iota(jnp.int32, (8, 32), 1), 1.0, 0.0).astype(BF16)
+    query = dot(mine, q_ref[...], ((1,), (0,)))[0:rows]
+    key = dot(mine, kv_ref[0], ((1,), (0,)))[0:rows]
+    value = dot(mine, kv_ref[1], ((1,), (0,)))[0:rows]
     product = query * key
     lane = lax.broadcasted_iota(jnp.int32, (rows, WIDTH), 1)
     old, own, below = [], [], []
@@ -161,36 +176,45 @@
 
 
 def prefill_kernel(
-    len_ref, gain_ref, hd_ref, x_hbm, w_hbm, kc_hbm, vc_hbm, wo_hbm,
-    first_ref, second_ref, kv_ref,
-    x_ref, w_ref, kc_ref, vc_ref, wo_ref, q_s, k_s, v_s, a_s, sems,
+    len_ref, tp_ref, gain_ref, hd_ref, x0_hbm, x1_hbm, x2_hbm, x3_hbm, w_hbm, kc_hbm, vc_hbm, wo_hbm,
+    o0_ref, o1_ref, o2_ref, o3_ref, kv_ref,
+    x_ref, w_ref, kc_ref, vc_ref, wo_ref, wo4_s, q_s, k_s, v_s, a_s, sems,
 ):
     tokens, cached = x_ref.shape[1], kc_ref.shape[1]
     block = 256
+    me = tp_ref[0]
+
+    def piece(source, shift, b):
+        at = pl.ds(pl.multiple_of(((me - shift + NT) & (NT - 1)) * WIDTH, WIDTH), WIDTH)
+        cols = slice(b * block, (b + 1) * block)
+        return source.at[:, cols], x_ref.at[at, cols]
+
+    sources = (x0_hbm, x1_hbm, x2_hbm, x3_hbm)
+    plan = [piece(source, shift, 0) for shift, source in enumerate(sources)] + [(w_hbm, w_ref)]
+    plan += [piece(source, shift, 1) for shift, source in enumerate(sources)]
+    plan += [(wo_hbm, wo_ref), (kc_hbm, kc_ref), (vc_hbm, vc_ref)]
     fetches = [
-        pltpu.make_async_copy(source, target, sems.at[n])
-        for n, (source, target) in enumerate(
-            [(x_hbm.at[:, 0:block], x_ref.at[:, 0:block]), (w_hbm, w_ref)]
-            + [(x_hbm.at[:, block:tokens], x_ref.at[:, block:tokens])]
-            + [(kc_hbm, kc_ref), (vc_hbm, vc_ref), (wo_hbm, wo_ref)]
-        )
+        pltpu.make_async_copy(source, target, sems.at[n]) for n, (source, target) in enumerate(plan)
     ]
     for fetch in fetches:
         fetch.start()
     for b in range(tokens // block):
         cols = slice(b * block, (b + 1) * block)
-        fetches[0 if b == 0 else 2].wait()
+        for fetch in fetches[5 * b : 5 * b + 4]:
+            fetch.wait()
         x = x_ref[:, cols].astype(F32)
         mean_square = jnp.sum(x * x, axis=0, keepdims=True) * (1.0 / x.shape[0])
         hidden = (x * lax.rsqrt(mean_square + EPSILON) * gain_ref[...]).astype(BF16)
         if b == 0:
-            fetches[1].wait()
+            fetches[4].wait()
             for part in (1, 2):
-                kv_ref[part - 1] = dot(hd_ref[...], w_ref[part], ((1,), (1,)))[0:4].astype(BF16)
+                kv_ref[part - 1] = dot(hd_ref[...], w_ref[part], ((1,), (1,))).astype(BF16)
         for part, held in enumerate((q_s, k_s, v_s)):
             held[:, cols] = dot(w_ref[part], hidden, ((1,), (0,))).astype(BF16)
-    fetches[3].wait()
-    fetches[4].wait()
+    for fetch in fetches[9:]:
+        fetch.wait()
+    for t in range(NT):
+        wo4_s[t] = wo_ref[:, t * WIDTH : (t + 1) * WIDTH]
     length = len_ref[0]
     for b in range(tokens // block):
         cols = slice(b * block, (b + 1) * block)
@@ -214,12 +238,9 @@
                 v_s[feats, 0:seen], w_new.astype(BF16), ((1,), (0,))
             )
             a_s[feats, cols] = (mixed / total).astype(BF16)
-        if b == 0:
-            fetches[5].wait()
-        out_ref = first_ref if b == 0 else second_ref
-        for n in range(wo_ref.shape[1] // block):
-            outs = slice(n * block, (n + 1) * block)
-            out_ref[outs, :] = dot(wo_ref[:, outs], a_s[:, cols], ((0,), (0,)))
+    for shift, out_ref in enumerate((o0_ref, o1_ref, o2_ref, o3_ref)):
+        terms = dot(wo4_s[(me + shift) & (NT - 1)], a_s[...], ((0,), (0,)))
+        out_ref[...] = terms.astype(out_ref.dtype)
 
 
 def call(
@@ -254,54 +275,57 @@
     index = (lax.axis_index("x") * NZ + lax.axis_index("z")) * NC + lax.axis_index("c")
     base = (index * pool).astype(jnp.int32).reshape(1)
 
-    x_rows = spread(x_dec, "tp", NT)
-    x_all = lax.all_gather(x_pre.T, "tp", axis=0, tiled=True)
-    queries, hidden = call(
+    def turned(block, shift):
+        return lax.ppermute(block, "tp", [(t, (t + shift) % NT) for t in range(NT)])
+
+    tp = lax.axis_index("tp").astype(jnp.int32).reshape(1)
+    own = (lax.axis_index("x") * NC + lax.axis_index("c")).astype(jnp.int32).reshape(1)
+    x_rows = spread(x_dec, ("x", "c", "tp"), NX * NC * NT)
+    x_t = x_pre.T
+    x_blocks = [x_t] + [turned(x_t, shift) for shift in range(1, NT)]
+    queries, own_queries, hidden = call(
         dec_project_kernel,
-        (shape((NZ, 4, WIDTH), BF16), shape((8, full), BF16)),
+        (shape((NZ, 80, 128), BF16), shape((32, WIDTH), BF16), shape((32, full), BF16)),
         (),
         (x_rows, norm_gain.reshape(1, full)),
         (w_t,),
         scratch=[
-            pltpu.VMEM((8, full), F32),
+            pltpu.VMEM((32, full), F32),
             pltpu.VMEM((WIDTH, full), BF16),
             pltpu.SemaphoreType.DMA,
         ],
-        flops=2 * 8 * full * WIDTH,
+        flops=2 * 32 * full * WIDTH,
         moved=2 * full * WIDTH,
         limit=VMEM_ALL,
     )
-    own_queries = queries
-    queries = lax.all_to_all(queries, "z", 0, 0, tiled=True)
-    x_all, queries = lax.optimization_barrier((x_all, queries))
-    half = tokens // 2
-    first, second, own_kv = call(
+    term_blocks = call(
         prefill_kernel,
-        (shape((full, half), F32), shape((full, half), F32), shape((2, 4, WIDTH), BF16)),
-        (pre_lens,),
+        (shape((WIDTH, tokens), F32),)
+        + (shape((WIDTH, tokens), BF16),) * 3
+        + (shape((2, 32, WIDTH), BF16),),
+        (pre_lens, tp),
         (norm_gain.reshape(full, 1), hidden),
-        (x_all, w_t, pre_keys.T, pre_values.T, w_out),
+        (*x_blocks, w_t, pre_keys.T, pre_values.T, w_out),
         scratch=[
             pltpu.VMEM((full, tokens), BF16),
             pltpu.VMEM((3, WIDTH, full), BF16),
             pltpu.VMEM((WIDTH, pre_keys.shape[0]), BF16),
             pltpu.VMEM((WIDTH, pre_keys.shape[0]), BF16),
             pltpu.VMEM((WIDTH, full), BF16),
+            pltpu.VMEM((NT, WIDTH, WIDTH), BF16),
         ]
         + [pltpu.VMEM((WIDTH, tokens), BF16)] * 4
-        + [pltpu.SemaphoreType.DMA((6,))],
+        + [pltpu.SemaphoreType.DMA((12,))],
         flops=8 * tokens * full * WIDTH + 4 * tokens * 896 * WIDTH,
         moved=8 * full * WIDTH,
         limit=VMEM_ALL,
     )
-    queries = spread(queries.reshape(NZ * 4, WIDTH), ("x", "c"), NX * NC)
-    first, second, queries = lax.optimization_barrier((first, second, queries))
-    pre_out = jnp.concatenate(
-        [lax.psum_scatter(part, "tp", scatter_dimension=0, tiled=True) for part in (first, second)],
-        axis=1,
-    )
-    queries = queries.reshape(NX * NC * NZ * 4, WIDTH)
-    requests = queries.shape[0]
+    queries = lax.all_to_all(queries, "z", 0, 0, tiled=True)
+    *term_blocks, own_kv = term_blocks
+    own_kv, queries = lax.optimization_barrier((own_kv, queries))
+    arrived = [turned(block, shift) for shift, block in enumerate(term_blocks) if shift > 0]
+    pre_out = term_blocks[0] + sum(block.astype(F32) for block in arrived)
+    requests = dec_lens.shape[0]
     partial = call(
         dec_attention_kernel,
         shape((requests, LANES), BF16),
@@ -309,6 +333,7 @@
         (queries, dec_lens.reshape(1, requests)),
         (dec_keys.T, dec_values.T),
         scratch=[
+            pltpu.VMEM((requests, WIDTH), BF16),
             pltpu.VMEM((WIDTH, pool), BF16),
             pltpu.VMEM((WIDTH, pool), BF16),
             pltpu.SemaphoreType.DMA((2,)),
@@ -329,7 +354,7 @@
     terms = call(
         dec_finish_kernel,
         shape((NT, 4, WIDTH), F32),
-        (),
+        (own,),
         (partial, own_queries, own_kv, w_out),
         flops=2 * 8 * full * WIDTH,
         moved=2 * full * WIDTH,

time: 143 us -> 127 us (0.89)
  the two profiles are of different devices: /device:TPU:1 before, /device:TPU:2 now
where the time goes in v3:
time: 127 us; the launch traced here: 126 us
  starting transfers between devices  62.2 us (49%)
  waiting for transfers between devices  32.9 us (26%)
  Pallas kernels  22.6 us (18%)
  local copies, waits for them, and re-layouts  5.21 us (4%)
  between operations  1.53 us (1%)
  other arithmetic  1.49 us (1%)
    pallas_call x5, Pallas kernels, call(): pl.pallas_call(kernel, out_shape=out_shape, in_specs=[pl.BlockSpec(memory...  22.6 us
    ppermute x6, starting transfers between devices, turned(): return lax.ppermute(block, 'tp', [(t, (t + shift) % NT) for t in range(NT)])  19.5 us
    all_to_all x1, starting transfers between devices, body(): queries = lax.all_to_all(queries, 'z', 0, 0, tiled=True)  13.3 us
    all_to_all x1, waiting for transfers between devices, body(): partial = lax.all_to_all(partial, 'z', 0, 0, tiled=True)  12.6 us
    all_to_all x1, starting transfers between devices, body(): partial = lax.all_to_all(partial, 'z', 0, 0, tiled=True)  11.7 us
    ppermute x6, waiting for transfers between devices, turned(): return lax.ppermute(block, 'tp', [(t, (t + shift) % NT) for t in range(NT)])  10.6 us
    all_to_all x1, starting transfers between devices, spread(): return lax.all_to_all(copies, axes, 0, 0, tiled=True)  9.47 us
    all_to_all x1, waiting for transfers between devices, spread(): return lax.all_to_all(copies, axes, 0, 0, tiled=True)  5.1 us
  transfers between devices with their start and end apart: 11, of which 5 were waited for; matrix products, arithmetic and copies ran while one was open for 3% of the time, Pallas kernels for 11%

profile of v3, /device:TPU:2, one launch (start us, length us, event | category | flops | bytes accessed | tf_op | source)
XLA Modules:
  0.0 125.9 jit_solution(11622569204146051973)
XLA Ops:
  0.6 0.0 copy-start.8
  0.6 0.0 copy-start.9
  0.7 1.4 %broadcast_in_dim.2 = bf16[32,4,320]{2,1,0:T(4,128)(2,1)} broadcast(bf16[4,320]{1,0:T(4,128)(2,1)} %param.12), dimensions={1,2} | broadcast | bytes 84480 | tf_op jit(solution)/shard_map/broadcast_in_dim | solution.py:267
  2.1 9.5 %all-to-all-start = ((bf16[32,4,320]{2,1,0:T(4,128)(2,1)}), bf16[32,4,320]{2,1,0:T(4,128)(2,1)S(1)}, u32[]{:S(2)}, u32[]{:S(2)}) async-start(bf16[32,4,320]{2,1,0:T(4,128)(2,1)} %broadcast_in_dim.2), calls=%async_computation | async-start | bytes 196608 | tf_op jit(solution)/shard_map/all_to_all | solution.py:268
  11.5 1.3 %reshape.28.gain_ref = f32[1,1280]{1,0:T(1,128)} reshape(f32[1280]{0:T(1024)} %param.13) | data formatting | bytes 10240 | tf_op jit(solution)/shard_map/reshape | solution.py:290
  12.8 5.1 %all-to-all-done.x_ref = bf16[32,4,320]{2,1,0:T(4,128)(2,1)S(1)} async-done(((bf16[32,4,320]{2,1,0:T(4,128)(2,1)}), bf16[32,4,320]{2,1,0:T(4,128)(2,1)S(1)}, u32[]{:S(2)}, u32[]{:S(2)}) %all-to-all-start) | async-done | bytes 81952 | tf_op jit(solution)/shard_map/all_to_all | solution.py:268
  17.9 0.0 copy-start.7
  17.9 0.6 copy-done.7
  18.6 3.2 %shard_map.122 = (bf16[16,80,128]{2,1,0:T(8,128)(2,1)}, bf16[32,320]{1,0:T(8,128)(2,1)}, bf16[32,1280]{1,0:T(8,128)(2,1)}) custom-call(bf16[32,4,320]{2,1,0:T(4,128)(2,1)} %copy-done.7, f32[1,1280]{1,0:T(1,128)} %reshape.28.gain_ref, bf16[3,320,1280]{2,1,0:T(8,128)(2,1)} %bitcast.16), custom_call_target="tpu_custom_call" | custom-call | flops 26214400 | bytes 819200 | tf_op jit(solution)/shard_map/pallas_call | solution.py:249
  21.8 13.3 %all-to-all-start.1 = ((bf16[16,80,128]{2,1,0:T(8,128)(2,1)}), bf16[16,80,128]{2,1,0:T(8,128)(2,1)S(1)}, u32[]{:S(2)}, u32[]{:S(2)}) async-start(bf16[16,80,128]{2,1,0:T(8,128)(2,1)} %get-tuple-element.18), calls=%async_computation.1 | async-start | bytes 655360 | tf_op jit(solution)/shard_map/all_to_all | solution.py:323
  35.1 0.0 copy-done.9
  35.1 2.4 %collective-permute-start = (bf16[320,512]{1,0:T(8,128)(2,1)S(1)}, bf16[320,512]{1,0:T(8,128)(2,1)S(1)}, u32[]{:S(2)}, u32[]{:S(2)}) collective-permute-start(bf16[320,512]{1,0:T(8,128)(2,1)S(1)} %bitcast.19), channel_id=1, source_target_pairs={{0,1},{1,2},{2,3},{3,0},{4,5},{5,6},{6,7},{7,4},{8,9},{9,10},{10,1... | collective-permute-start | bytes 983048 | tf_op jit(solution)/shard_map/ppermute | solution.py:279
  37.5 4.3 %collective-permute-start.1 = (bf16[320,512]{1,0:T(8,128)(2,1)S(1)}, bf16[320,512]{1,0:T(8,128)(2,1)S(1)}, u32[]{:S(2)}, u32[]{:S(2)}) collective-permute-start(bf16[320,512]{1,0:T(8,128)(2,1)S(1)} %bitcast.20), channel_id=1, source_target_pairs={{0,2},{1,3},{2,0},{3,1},{4,6},{5,7},{6,4},{7,5},{8,10},{9,11},{10,... | collective-permute-start | bytes 983048 | tf_op jit(solution)/shard_map/ppermute | solution.py:279
  41.8 3.0 %collective-permute-start.2 = (bf16[320,512]{1,0:T(8,128)(2,1)S(1)}, bf16[320,512]{1,0:T(8,128)(2,1)S(1)}, u32[]{:S(2)}, u32[]{:S(2)}) collective-permute-start(bf16[320,512]{1,0:T(8,128)(2,1)S(1)} %bitcast.21), channel_id=1, source_target_pairs={{0,3},{1,0},{2,1},{3,2},{4,7},{5,4},{6,5},{7,6},{8,11},{9,8},{10,9... | collective-permute-start | bytes 983048 | tf_op jit(solution)/shard_map/ppermute | solution.py:279
  44.8 0.0 copy-done.8
  44.8 1.1 reshape.33.gain_ref
  46.6 8.1 %collective-permute-done.x1_hbm = bf16[320,512]{1,0:T(8,128)(2,1)S(1)} collective-permute-done((bf16[320,512]{1,0:T(8,128)(2,1)S(1)}, bf16[320,512]{1,0:T(8,128)(2,1)S(1)}, u32[]{:S(2)}, u32[]{:S(2)}) %collective-permute-start) | collective-permute-done | bytes 327712 | tf_op jit(solution)/shard_map/ppermute | solution.py:279
  54.6 0.0 copy-start.10
  54.6 0.0 collective-permute-done.1.x2_hbm
  54.6 0.0 copy-start.11
  54.6 2.5 %collective-permute-done.2.x3_hbm = bf16[320,512]{1,0:T(8,128)(2,1)S(1)} collective-permute-done((bf16[320,512]{1,0:T(8,128)(2,1)S(1)}, bf16[320,512]{1,0:T(8,128)(2,1)S(1)}, u32[]{:S(2)}, u32[]{:S(2)}) %collective-permute-start.2) | collective-permute-done | bytes 327712 | tf_op jit(solution)/shard_map/ppermute | solution.py:279
  57.2 0.0 copy-start.12
  57.2 0.0 copy-done.10
  57.2 0.0 copy-done.11
  57.2 0.7 copy-done.12
  57.9 0.0 copy-start.3
  57.9 0.0 copy-start.4
  57.9 0.0 copy-start.5
  57.9 11.2 %shard_map.123 = (f32[320,512]{1,0:T(8,128)}, bf16[320,512]{1,0:T(8,128)(2,1)}, bf16[320,512]{1,0:T(8,128)(2,1)}, bf16[320,512]{1,0:T(8,128)(2,1)}, bf16[2,32,320]{2,1,0:T(8,128)(2,1)}) custom-call(s32[1]{0:T(128)S(6)} %copy.14.len_ref, s32[1]{0:T(128)} %bitcast.tp_ref, f32[1280,1]{1,0:T(8,128)} %reshape.33.gain_ref, ...), custom_call_target="tpu_custom_call" | custom-call | flops 2264924160 | bytes 3276800 | tf_op jit(solution)/shard_map/pallas_call | solution.py:249
  69.1 0.0 copy-start
  69.1 0.0 copy-start.1
  69.2 0.0 copy-start.2
  69.2 0.0 copy-start.6
  69.2 0.0 all-to-all-done.1.qp_ref
  69.2 0.0 copy-done.3
  69.2 0.0 copy-done.4
  69.2 0.0 copy-done.5
  69.2 5.5 %shard_map.124 = bf16[512,384]{1,0:T(8,128)(2,1)} custom-call(s32[1]{0:T(128)} %bitcast.7.base_ref, bf16[16,80,128]{2,1,0:T(8,128)(2,1)S(1)} %all-to-all-done.1.qp_ref, s32[1,512]{1,0:T(1,128)S(1)} %bitcast.15, bf16[320,640]{1,0:T(8,128)(2,1)S(1)} %bitcast.13, bf16[320,640]{1,0:T(8,128)(2,1)S(1)} %bitcast.14), custom_call_target="tpu_custom_call" | custom-call | flops 419430400 | bytes 819200 | tf_op jit(solution)/shard_map/pallas_call | solution.py:249
  74.7 4.8 %all-to-all-start.2 = ((bf16[8,64,384]{2,1,0:T(8,128)(2,1)}), bf16[8,64,384]{2,1,0:T(8,128)(2,1)S(1)}, u32[]{:S(2)}, u32[]{:S(2)}) async-start(bf16[8,64,384]{2,1,0:T(8,128)(2,1)} %bitcast.11), calls=%async_computation.2 | async-start | bytes 786432 | tf_op jit(solution)/shard_map/all_to_all | solution.py:344
  79.5 2.2 %collective-permute-start.3 = (bf16[320,512]{1,0:T(8,128)(2,1)}, bf16[320,512]{1,0:T(8,128)(2,1)S(1)}, u32[]{:S(2)}, u32[]{:S(2)}) collective-permute-start(bf16[320,512]{1,0:T(8,128)(2,1)} %get-tuple-element.14), channel_id=1, source_target_pairs={{0,1},{1,2},{2,3},{3,0},{4,5},{5,6},{6,7},{7,4},{8,9},{9,10},{10,1... | collective-permute-start | bytes 983048 | tf_op jit(solution)/shard_map/ppermute | solution.py:279
  81.7 5.7 %collective-permute-start.4 = (bf16[320,512]{1,0:T(8,128)(2,1)}, bf16[320,512]{1,0:T(8,128)(2,1)S(1)}, u32[]{:S(2)}, u32[]{:S(2)}) collective-permute-start(bf16[320,512]{1,0:T(8,128)(2,1)} %get-tuple-element.15), channel_id=1, source_target_pairs={{0,2},{1,3},{2,0},{3,1},{4,6},{5,7},{6,4},{7,5},{8,10},{9,11},{10,... | collective-permute-start | bytes 983048 | tf_op jit(solution)/shard_map/ppermute | solution.py:279
  87.4 1.9 %collective-permute-start.5 = (bf16[320,512]{1,0:T(8,128)(2,1)}, bf16[320,512]{1,0:T(8,128)(2,1)S(1)}, u32[]{:S(2)}, u32[]{:S(2)}) collective-permute-start(bf16[320,512]{1,0:T(8,128)(2,1)} %get-tuple-element.16), channel_id=1, source_target_pairs={{0,3},{1,0},{2,1},{3,2},{4,7},{5,4},{6,5},{7,6},{8,11},{9,8},{10,9... | collective-permute-start | bytes 983048 | tf_op jit(solution)/shard_map/ppermute | solution.py:279
  89.4 0.0 all-to-all-done.2.in_ref
  89.4 1.4 %shard_map.125 = bf16[16,4,384]{2,1,0:T(4,128)(2,1)} custom-call(bf16[8,64,384]{2,1,0:T(8,128)(2,1)S(1)} %all-to-all-done.2.in_ref), custom_call_target="tpu_custom_call" | custom-call | flops 196608 | bytes 786432 | tf_op jit(solution)/shard_map/pallas_call | solution.py:249
  90.8 11.7 %all-to-all-start.3 = ((bf16[16,4,384]{2,1,0:T(4,128)(2,1)}), bf16[16,4,384]{2,1,0:T(4,128)(2,1)S(1)}, u32[]{:S(2)}, u32[]{:S(2)}) async-start(bf16[16,4,384]{2,1,0:T(4,128)(2,1)} %shard_map.125), calls=%async_computation.3 | async-start | bytes 98304 | tf_op jit(solution)/shard_map/all_to_all | solution.py:353
  102.5 12.6 %all-to-all-done.3.in_ref = bf16[16,4,384]{2,1,0:T(4,128)(2,1)S(1)} async-done(((bf16[16,4,384]{2,1,0:T(4,128)(2,1)}), bf16[16,4,384]{2,1,0:T(4,128)(2,1)S(1)}, u32[]{:S(2)}, u32[]{:S(2)}) %all-to-all-start.3) | async-done | bytes 49184 | tf_op jit(solution)/shard_map/all_to_all | solution.py:353
  115.2 0.0 copy-done
  115.2 0.0 copy-done.1
  115.2 0.0 copy-done.2
  115.2 1.3 %shard_map.126 = f32[4,4,320]{2,1,0:T(4,128)} custom-call(s32[1]{0:T(128)} %bitcast.6.own_ref, bf16[16,4,384]{2,1,0:T(4,128)(2,1)S(1)} %all-to-all-done.3.in_ref, bf16[32,320]{1,0:T(8,128)(2,1)S(1)} %copy-done.2, bf16[2,32,320]{2,1,0:T(8,128)(2,1)S(1)} %copy-done.1, bf16[320,1280]{1,0:T(8,128)(2,1)S(1)} %copy-done), custom_call_target="tpu_custom_call" | custom-call | flops 6553600 | bytes 819200 | tf_op jit(solution)/shard_map/pallas_call | solution.py:249
  116.5 3.4 %all-to-all-start.4 = ((f32[4,4,320]{2,1,0:T(4,128)}), f32[4,4,320]{2,1,0:T(4,128)S(1)}, u32[]{:S(2)}, u32[]{:S(2)}) async-start(f32[4,4,320]{2,1,0:T(4,128)} %shard_map.126), calls=%async_computation.4 | async-start | bytes 49152 | tf_op jit(solution)/shard_map/all_to_all | solution.py:362
  119.9 0.0 collective-permute-done.3
  119.9 0.0 collective-permute-done.4
  119.9 0.0 collective-permute-done.5
  119.9 0.0 copy-done.6
  119.9 0.9 fusion
  120.8 4.5 %all-to-all-done.4 = f32[4,4,320]{2,1,0:T(4,128)S(1)} async-done(((f32[4,4,320]{2,1,0:T(4,128)}), f32[4,4,320]{2,1,0:T(4,128)S(1)}, u32[]{:S(2)}, u32[]{:S(2)}) %all-to-all-start.4) | async-done | bytes 20512 | tf_op jit(solution)/shard_map/all_to_all | solution.py:362
  125.3 0.6 reduce_sum.9
Async XLA Ops:
  0.6 44.2 %copy-start.8 = (f32[1280]{0:T(1024)S(1)}, f32[1280]{0:T(1024)}, u32[]{:S(2)}) copy-start(f32[1280]{0:T(1024)} %param.13) | copy-start | bytes 15364
  0.6 34.4 %copy-start.9 = (bf16[512,320]{0,1:T(8,128)(2,1)S(1)}, bf16[512,320]{0,1:T(8,128)(2,1)}, u32[]{:S(2)}) copy-start(bf16[512,320]{0,1:T(8,128)(2,1)} %param.11) | copy-start | bytes 983044
  2.1 15.9 %all-to-all-start = ((bf16[32,4,320]{2,1,0:T(4,128)(2,1)}), bf16[32,4,320]{2,1,0:T(4,128)(2,1)S(1)}, u32[]{:S(2)}, u32[]{:S(2)}) async-start(bf16[32,4,320]{2,1,0:T(4,128)(2,1)} %broadcast_in_dim.2), calls=%async_computation | async-start | bytes 196608 | tf_op jit(solution)/shard_map/all_to_all | solution.py:268
  17.9 0.6 copy-start.7
  21.8 47.4 %all-to-all-start.1 = ((bf16[16,80,128]{2,1,0:T(8,128)(2,1)}), bf16[16,80,128]{2,1,0:T(8,128)(2,1)S(1)}, u32[]{:S(2)}, u32[]{:S(2)}) async-start(bf16[16,80,128]{2,1,0:T(8,128)(2,1)} %get-tuple-element.18), calls=%async_computation.1 | async-start | bytes 655360 | tf_op jit(solution)/shard_map/all_to_all | solution.py:323
  35.1 19.5 %collective-permute-start = (bf16[320,512]{1,0:T(8,128)(2,1)S(1)}, bf16[320,512]{1,0:T(8,128)(2,1)S(1)}, u32[]{:S(2)}, u32[]{:S(2)}) collective-permute-start(bf16[320,512]{1,0:T(8,128)(2,1)S(1)} %bitcast.19), channel_id=1, source_target_pairs={{0,1},{1,2},{2,3},{3,0},{4,5},{5,6},{6,7},{7,4},{8,9},{9,10},{10,1... | collective-permute-start | bytes 983048 | tf_op jit(solution)/shard_map/ppermute | solution.py:279
  37.5 17.1 %collective-permute-start.1 = (bf16[320,512]{1,0:T(8,128)(2,1)S(1)}, bf16[320,512]{1,0:T(8,128)(2,1)S(1)}, u32[]{:S(2)}, u32[]{:S(2)}) collective-permute-start(bf16[320,512]{1,0:T(8,128)(2,1)S(1)} %bitcast.20), channel_id=1, source_target_pairs={{0,2},{1,3},{2,0},{3,1},{4,6},{5,7},{6,4},{7,5},{8,10},{9,11},{10,... | collective-permute-start | bytes 983048 | tf_op jit(solution)/shard_map/ppermute | solution.py:279
  41.8 15.4 %collective-permute-start.2 = (bf16[320,512]{1,0:T(8,128)(2,1)S(1)}, bf16[320,512]{1,0:T(8,128)(2,1)S(1)}, u32[]{:S(2)}, u32[]{:S(2)}) collective-permute-start(bf16[320,512]{1,0:T(8,128)(2,1)S(1)} %bitcast.21), channel_id=1, source_target_pairs={{0,3},{1,0},{2,1},{3,2},{4,7},{5,4},{6,5},{7,6},{8,11},{9,8},{10,9... | collective-permute-start | bytes 983048 | tf_op jit(solution)/shard_map/ppermute | solution.py:279
  54.6 2.5 %copy-start.10 = (bf16[320,512]{1,0:T(8,128)(2,1)}, bf16[320,512]{1,0:T(8,128)(2,1)S(1)}, u32[]{:S(2)}) copy-start(bf16[320,512]{1,0:T(8,128)(2,1)S(1)} %collective-permute-done.x1_hbm) | copy-start | bytes 983044
  54.6 2.5 %copy-start.11 = (bf16[320,512]{1,0:T(8,128)(2,1)}, bf16[320,512]{1,0:T(8,128)(2,1)S(1)}, u32[]{:S(2)}) copy-start(bf16[320,512]{1,0:T(8,128)(2,1)S(1)} %collective-permute-done.1.x2_hbm) | copy-start | bytes 983044
  57.2 0.7 copy-start.12
  57.9 11.3 %copy-start.3 = (bf16[640,320]{0,1:T(8,128)(2,1)S(1)}, bf16[640,320]{0,1:T(8,128)(2,1)}, u32[]{:S(2)}) copy-start(bf16[640,320]{0,1:T(8,128)(2,1)} %param.19) | copy-start | bytes 1228804
  57.9 11.3 %copy-start.4 = (bf16[640,320]{0,1:T(8,128)(2,1)S(1)}, bf16[640,320]{0,1:T(8,128)(2,1)}, u32[]{:S(2)}) copy-start(bf16[640,320]{0,1:T(8,128)(2,1)} %param.20) | copy-start | bytes 1228804
  57.9 11.3 %copy-start.5 = (s32[512]{0:T(512)S(1)}, s32[512]{0:T(512)}, u32[]{:S(2)}) copy-start(s32[512]{0:T(512)} %param.21) | copy-start | bytes 6148
  69.1 46.0 %copy-start = (bf16[320,1280]{1,0:T(8,128)(2,1)S(1)}, bf16[320,1280]{1,0:T(8,128)(2,1)}, u32[]{:S(2)}) copy-start(bf16[320,1280]{1,0:T(8,128)(2,1)} %w_ref.1) | copy-start | bytes 2457604
  69.1 46.0 %copy-start.1 = (bf16[2,32,320]{2,1,0:T(8,128)(2,1)S(1)}, bf16[2,32,320]{2,1,0:T(8,128)(2,1)}, u32[]{:S(2)}) copy-start(bf16[2,32,320]{2,1,0:T(8,128)(2,1)} %get-tuple-element.21.kv_ref) | copy-start | bytes 122884
  69.2 46.0 %copy-start.2 = (bf16[32,320]{1,0:T(8,128)(2,1)S(1)}, bf16[32,320]{1,0:T(8,128)(2,1)}, u32[]{:S(2)}) copy-start(bf16[32,320]{1,0:T(8,128)(2,1)} %get-tuple-element.20.q_ref) | copy-start | bytes 61444
  69.2 50.7 %copy-start.6 = (f32[320,512]{1,0:T(8,128)S(1)}, f32[320,512]{1,0:T(8,128)}, u32[]{:S(2)}) copy-start(f32[320,512]{1,0:T(8,128)} %get-tuple-element.13) | copy-start | bytes 1966084
  74.7 14.7 %all-to-all-start.2 = ((bf16[8,64,384]{2,1,0:T(8,128)(2,1)}), bf16[8,64,384]{2,1,0:T(8,128)(2,1)S(1)}, u32[]{:S(2)}, u32[]{:S(2)}) async-start(bf16[8,64,384]{2,1,0:T(8,128)(2,1)} %bitcast.11), calls=%async_computation.2 | async-start | bytes 786432 | tf_op jit(solution)/shard_map/all_to_all | solution.py:344
  79.5 40.4 %collective-permute-start.3 = (bf16[320,512]{1,0:T(8,128)(2,1)}, bf16[320,512]{1,0:T(8,128)(2,1)S(1)}, u32[]{:S(2)}, u32[]{:S(2)}) collective-permute-start(bf16[320,512]{1,0:T(8,128)(2,1)} %get-tuple-element.14), channel_id=1, source_target_pairs={{0,1},{1,2},{2,3},{3,0},{4,5},{5,6},{6,7},{7,4},{8,9},{9,10},{10,1... | collective-permute-start | bytes 983048 | tf_op jit(solution)/shard_map/ppermute | solution.py:279
  81.7 38.2 %collective-permute-start.4 = (bf16[320,512]{1,0:T(8,128)(2,1)}, bf16[320,512]{1,0:T(8,128)(2,1)S(1)}, u32[]{:S(2)}, u32[]{:S(2)}) collective-permute-start(bf16[320,512]{1,0:T(8,128)(2,1)} %get-tuple-element.15), channel_id=1, source_target_pairs={{0,2},{1,3},{2,0},{3,1},{4,6},{5,7},{6,4},{7,5},{8,10},{9,11},{10,... | collective-permute-start | bytes 983048 | tf_op jit(solution)/shard_map/ppermute | solution.py:279
  87.4 32.4 %collective-permute-start.5 = (bf16[320,512]{1,0:T(8,128)(2,1)}, bf16[320,512]{1,0:T(8,128)(2,1)S(1)}, u32[]{:S(2)}, u32[]{:S(2)}) collective-permute-start(bf16[320,512]{1,0:T(8,128)(2,1)} %get-tuple-element.16), channel_id=1, source_target_pairs={{0,3},{1,0},{2,1},{3,2},{4,7},{5,4},{6,5},{7,6},{8,11},{9,8},{10,9... | collective-permute-start | bytes 983048 | tf_op jit(solution)/shard_map/ppermute | solution.py:279
  90.8 24.4 %all-to-all-start.3 = ((bf16[16,4,384]{2,1,0:T(4,128)(2,1)}), bf16[16,4,384]{2,1,0:T(4,128)(2,1)S(1)}, u32[]{:S(2)}, u32[]{:S(2)}) async-start(bf16[16,4,384]{2,1,0:T(4,128)(2,1)} %shard_map.125), calls=%async_computation.3 | async-start | bytes 98304 | tf_op jit(solution)/shard_map/all_to_all | solution.py:353
  116.5 8.8 %all-to-all-start.4 = ((f32[4,4,320]{2,1,0:T(4,128)}), f32[4,4,320]{2,1,0:T(4,128)S(1)}, u32[]{:S(2)}, u32[]{:S(2)}) async-start(f32[4,4,320]{2,1,0:T(4,128)} %shard_map.126), calls=%async_computation.4 | async-start | bytes 49152 | tf_op jit(solution)/shard_map/all_to_all | solution.py:362

commit v4 on v3

--- a/solution.py
+++ b/solution.py
@@ -38,15 +38,12 @@
     return (x * lax.rsqrt(mean_square + EPSILON) * gain).astype(BF16)
 
 
-def dec_project_kernel(x_ref, gain_ref, w_hbm, qb_ref, q_ref, hidden_ref, rows, w_ref, sem):
-    fetch = pltpu.make_async_copy(w_hbm.at[0], w_ref, sem)
-    fetch.start()
+def dec_project_kernel(x_ref, gain_ref, w_ref, qb_ref, q_ref, hidden_ref, rows):
     for n in range(NX * NC):
         for t in range(NT):
             rows[4 * n : 4 * n + 4, t * WIDTH : (t + 1) * WIDTH] = x_ref[NT * n + t].astype(F32)
     hidden = normed_rows(rows[...], gain_ref[...])
     hidden_ref[...] = hidden
-    fetch.wait()
     value = dot(hidden, w_ref[...], ((1,), (1,)))
     q_ref[...] = value.astype(BF16)
     tail = jnp.concatenate([value[0:16, 256:WIDTH], value[16:32, 256:WIDTH]], axis=1)
@@ -55,11 +52,21 @@
         qb_ref[z] = packed
 
 
-def dec_attention_kernel(base_ref, qp_ref, lens_ref, k_hbm, v_hbm, out_ref, q_s, k_ref, v_ref, sems):
-    fetch_k = pltpu.make_async_copy(k_hbm, k_ref, sems.at[0])
-    fetch_v = pltpu.make_async_copy(v_hbm, v_ref, sems.at[1])
-    fetch_k.start()
-    fetch_v.start()
+def dec_bounds_kernel(base_ref, lens_ref, bounds_ref, order_ref):
+    requests = bounds_ref.shape[0]
+    place = lax.broadcasted_iota(jnp.int32, (requests, requests), 0)
+    x, c, z, i = place >> 7, (place >> 6) & 1, (place >> 2) & 15, place & 3
+    request = (x << 7) | (z << 3) | (c << 2) | i
+    arrived = (z << 5) | (x << 3) | (c << 2) | i
+    other = lax.broadcasted_iota(jnp.int32, (requests, requests), 1)
+    lens = lens_ref[...].astype(F32)
+    base = base_ref[0].astype(F32)
+    bounds_ref[:, 0:1] = jnp.sum(jnp.where(other < request, lens, 0.0), axis=1, keepdims=True) - base
+    bounds_ref[:, 1:2] = jnp.sum(jnp.where(other <= request, lens, 0.0), axis=1, keepdims=True) - base
+    order_ref[...] = jnp.where(other == arrived, 1.0, 0.0).astype(BF16)
+
+
+def dec_attention_kernel(qp_ref, bounds_ref, order_ref, k_ref, v_ref, out_ref, q_s):
     for z in range(NZ):
         rows = slice(32 * z, 32 * z + 32)
         q_s[rows, 0:128] = qp_ref[z, 0:32]
@@ -67,22 +74,10 @@
         q_s[32 * z : 32 * z + 16, 256:WIDTH] = qp_ref[z, 64:80, 0:64]
         q_s[32 * z + 16 : 32 * z + 32, 256:WIDTH] = qp_ref[z, 64:80, 64:128]
     requests, pool = q_s.shape[0], k_ref.shape[1]
-    place = lax.broadcasted_iota(jnp.int32, (requests, requests), 0)
-    x, c, z, i = place >> 7, (place >> 6) & 1, (place >> 2) & 15, place & 3
-    request = (x << 7) | (z << 3) | (c << 2) | i
-    arrived = (z << 5) | (x << 3) | (c << 2) | i
-    other = lax.broadcasted_iota(jnp.int32, (requests, requests), 1)
-    lens = lens_ref[...].astype(F32)
-    begin = jnp.sum(jnp.where(other < request, lens, 0.0), axis=1, keepdims=True)
-    end = jnp.sum(jnp.where(other <= request, lens, 0.0), axis=1, keepdims=True)
-    order = jnp.where(other == arrived, 1.0, 0.0).astype(BF16)
-    queries = dot(order, q_s[...], ((1,), (0,))).astype(BF16)
-    base = base_ref[0].astype(F32)
-    row = lax.broadcasted_iota(jnp.int32, (requests, pool), 1).astype(F32) + base
-    allowed = (row >= begin) & (row < end)
+    queries = dot(order_ref[...], q_s[...], ((1,), (0,))).astype(BF16)
+    row = lax.broadcasted_iota(jnp.int32, (requests, pool), 1).astype(F32)
+    allowed = (row >= bounds_ref[:, 0:1]) & (row < bounds_ref[:, 1:2])
     tops, totals = [], []
-    fetch_k.wait()
-    fetch_v.wait()
     for h in range(HEADS):
         s = dot(queries[:, h * HD : (h + 1) * HD], k_ref[h * HD : (h + 1) * HD, :], ((1,), (0,)))
         s = jnp.where(allowed, s, MASKED)
@@ -117,7 +112,7 @@
     return block[:, at : at + 1] + block[:, at + 1 : at + 2] + block[:, at + 2 : at + 3]
 
 
-def merged(parts, rows):
+def merged(parts, rows, stat=stat):
     parts = [part.astype(F32) for part in parts]
     tops, totals, values = [], [], jnp.zeros((rows, WIDTH), F32)
     scales = []
@@ -141,8 +136,10 @@
 def dec_merge_kernel(in_ref, out_ref):
     count, rows = in_ref.shape[0], in_ref.shape[1]
     values, tops, totals = merged([in_ref[n] for n in range(count)], rows)
-    extra = stats(tops, totals, rows)
-    values = values.astype(BF16)
+    lane = lax.broadcasted_iota(jnp.int32, (rows, LANES - WIDTH), 1)
+    extra = jnp.zeros((rows, LANES - WIDTH), F32)
+    for n, value in enumerate(tops + totals):
+        extra = jnp.where(lane == n, value, extra)
     for z in range(NZ):
         out_ref[z, :, 0:WIDTH] = values[4 * z : 4 * z + 4]
         out_ref[z, :, WIDTH:LANES] = extra[4 * z : 4 * z + 4]
@@ -150,7 +147,8 @@
 
 def dec_finish_kernel(own_ref, in_ref, q_ref, kv_ref, w_ref, out_ref):
     rows = 4
-    values, tops, totals = merged([in_ref[n] for n in range(NZ)], rows)
+    whole = lambda block, n: block[:, WIDTH + n : WIDTH + n + 1]
+    values, tops, totals = merged([in_ref[n] for n in range(NZ)], rows, whole)
     row = lax.broadcasted_iota(jnp.int32, (8, 32), 0) + 4 * own_ref[0]
     mine = jnp.where(row == lax.broadcasted_iota(jnp.int32, (8, 32), 1), 1.0, 0.0).astype(BF16)
     query = dot(mine, q_ref[...], ((1,), (0,)))[0:rows]
@@ -275,6 +273,16 @@
     index = (lax.axis_index("x") * NZ + lax.axis_index("z")) * NC + lax.axis_index("c")
     base = (index * pool).astype(jnp.int32).reshape(1)
 
+    requests = dec_lens.shape[0]
+    bounds, order = call(
+        dec_bounds_kernel,
+        (shape((requests, 2), F32), shape((requests, requests), BF16)),
+        (base,),
+        (dec_lens.reshape(1, requests),),
+        flops=8 * requests * requests,
+        moved=4 * requests * requests,
+    )
+
     def turned(block, shift):
         return lax.ppermute(block, "tp", [(t, (t + shift) % NT) for t in range(NT)])
 
@@ -287,17 +295,12 @@
         dec_project_kernel,
         (shape((NZ, 80, 128), BF16), shape((32, WIDTH), BF16), shape((32, full), BF16)),
         (),
-        (x_rows, norm_gain.reshape(1, full)),
-        (w_t,),
-        scratch=[
-            pltpu.VMEM((32, full), F32),
-            pltpu.VMEM((WIDTH, full), BF16),
-            pltpu.SemaphoreType.DMA,
-        ],
+        (x_rows, norm_gain.reshape(1, full), w_t[0]),
+        scratch=[pltpu.VMEM((32, full), F32)],
         flops=2 * 32 * full * WIDTH,
         moved=2 * full * WIDTH,
-        limit=VMEM_ALL,
-    )
+    )
+    *x_blocks, queries = lax.optimization_barrier((*x_blocks, queries))
     term_blocks = call(
         prefill_kernel,
         (shape((WIDTH, tokens), F32),)
@@ -325,26 +328,19 @@
     own_kv, queries = lax.optimization_barrier((own_kv, queries))
     arrived = [turned(block, shift) for shift, block in enumerate(term_blocks) if shift > 0]
     pre_out = term_blocks[0] + sum(block.astype(F32) for block in arrived)
-    requests = dec_lens.shape[0]
     partial = call(
         dec_attention_kernel,
         shape((requests, LANES), BF16),
-        (base,),
-        (queries, dec_lens.reshape(1, requests)),
-        (dec_keys.T, dec_values.T),
-        scratch=[
-            pltpu.VMEM((requests, WIDTH), BF16),
-            pltpu.VMEM((WIDTH, pool), BF16),
-            pltpu.VMEM((WIDTH, pool), BF16),
-            pltpu.SemaphoreType.DMA((2,)),
-        ],
+        (),
+        (queries, bounds, order, dec_keys.T, dec_values.T),
+        scratch=[pltpu.VMEM((requests, WIDTH), BF16)],
         flops=4 * requests * pool * WIDTH,
         moved=4 * pool * WIDTH,
     )
     partial = lax.all_to_all(partial.reshape(NX * NC, NZ * 4, LANES), ("x", "c"), 0, 0, tiled=True)
     partial = call(
         dec_merge_kernel,
-        shape((NZ, 4, LANES), BF16),
+        shape((NZ, 4, LANES), F32),
         (),
         (partial,),
         flops=NX * NC * NZ * 4 * LANES,

time: 127 us -> 112 us (0.88)
  the two profiles are of different devices: /device:TPU:2 before, /device:TPU:1 now
where the time goes in v4:
time: 112 us; the launch traced here: 110 us
  starting transfers between devices  52.9 us (47%)
  Pallas kernels  19.9 us (18%)
  blocking collectives  17.3 us (15%)
  waiting for transfers between devices  12.1 us (11%)
  local copies, waits for them, and re-layouts  5.02 us (4%)
  other arithmetic  1.52 us (1%)
  between operations  1.52 us (1%)
    ppermute x6, starting transfers between devices, turned(): return lax.ppermute(block, 'tp', [(t, (t + shift) % NT) for t in range(NT)])  22.2 us
    pallas_call x6, Pallas kernels, call(): pl.pallas_call(kernel, out_shape=out_shape, in_specs=[pl.BlockSpec(memory...  19.9 us
    all_to_all x1, blocking collectives, body(): lax.all_to_all(partial.reshape(NX * NC, NZ * 4, LANES), ('x', 'c'), 0, 0,...  17.3 us
    all_to_all x1, starting transfers between devices, body(): queries = lax.all_to_all(queries, 'z', 0, 0, tiled=True)  12.4 us
    all_to_all x1, starting transfers between devices, spread(): return lax.all_to_all(copies, axes, 0, 0, tiled=True)  8.65 us
    all_to_all x1, starting transfers between devices, body(): partial = lax.all_to_all(partial, 'z', 0, 0, tiled=True)  5.65 us
    all_to_all x1, waiting for transfers between devices, spread(): return lax.all_to_all(copies, axes, 0, 0, tiled=True)  5.42 us
    all_to_all x1, starting transfers between devices, body(): terms = lax.all_to_all(terms, 'tp', 0, 0, tiled=True)  4.01 us
  transfers between devices with their start and end apart: 10, of which 5 were waited for; matrix products, arithmetic and copies ran while one was open for 5% of the time, Pallas kernels for 13%

profile of v4, /device:TPU:1, one launch (start us, length us, event | category | flops | bytes accessed | tf_op | source)
XLA Modules:
  0.0 110.1 jit_solution(4113074355728863965)
XLA Ops:
  0.6 0.0 copy-start.7
  0.6 0.0 copy-start.5
  0.7 4.2 %collective-permute-start = (bf16[320,512]{1,0:T(8,128)(2,1)}, bf16[320,512]{1,0:T(8,128)(2,1)S(1)}, u32[]{:S(2)}, u32[]{:S(2)}) collective-permute-start(bf16[320,512]{1,0:T(8,128)(2,1)} %bitcast.21), channel_id=1, source_target_pairs={{0,1},{1,2},{2,3},{3,0},{4,5},{5,6},{6,7},{7,4},{8,9},{9,10},{10,1... | collective-permute-start | bytes 983048 | tf_op jit(solution)/shard_map/ppermute | solution.py:287
  4.8 4.5 %collective-permute-start.1 = (bf16[320,512]{1,0:T(8,128)(2,1)}, bf16[320,512]{1,0:T(8,128)(2,1)S(1)}, u32[]{:S(2)}, u32[]{:S(2)}) collective-permute-start(bf16[320,512]{1,0:T(8,128)(2,1)} %bitcast.22), channel_id=1, source_target_pairs={{0,2},{1,3},{2,0},{3,1},{4,6},{5,7},{6,4},{7,5},{8,10},{9,11},{10,... | collective-permute-start | bytes 983048 | tf_op jit(solution)/shard_map/ppermute | solution.py:287
  9.4 3.0 %collective-permute-start.2 = (bf16[320,512]{1,0:T(8,128)(2,1)}, bf16[320,512]{1,0:T(8,128)(2,1)S(1)}, u32[]{:S(2)}, u32[]{:S(2)}) collective-permute-start(bf16[320,512]{1,0:T(8,128)(2,1)} %bitcast.23), channel_id=1, source_target_pairs={{0,3},{1,0},{2,1},{3,2},{4,7},{5,4},{6,5},{7,6},{8,11},{9,8},{10,9... | collective-permute-start | bytes 983048 | tf_op jit(solution)/shard_map/ppermute | solution.py:287
  12.4 1.4 %broadcast_in_dim.2 = bf16[32,4,320]{2,1,0:T(4,128)(2,1)} broadcast(bf16[4,320]{1,0:T(4,128)(2,1)} %param.12), dimensions={1,2} | broadcast | bytes 84480 | tf_op jit(solution)/shard_map/broadcast_in_dim | solution.py:265
  13.7 8.7 %all-to-all-start = ((bf16[32,4,320]{2,1,0:T(4,128)(2,1)}), bf16[32,4,320]{2,1,0:T(4,128)(2,1)S(1)}, u32[]{:S(2)}, u32[]{:S(2)}) async-start(bf16[32,4,320]{2,1,0:T(4,128)(2,1)} %broadcast_in_dim.2), calls=%async_computation | async-start | bytes 196608 | tf_op jit(solution)/shard_map/all_to_all | solution.py:266
  22.4 1.2 %slice_bitcast_fusion.w_ref = bf16[320,1280]{1,0:T(8,128)(2,1)S(1)} fusion(bf16[3,320,1280]{2,1,0:T(8,128)(2,1)} %bitcast.19), kind=kLoop, calls=%fused_computation | loop fusion | bytes 1638400 | tf_op jit(solution)/shard_map/squeeze | solution.py:298
  23.6 0.7 reshape.28.gain_ref
  24.3 5.4 %all-to-all-done.x_ref = bf16[32,4,320]{2,1,0:T(4,128)(2,1)S(1)} async-done(((bf16[32,4,320]{2,1,0:T(4,128)(2,1)}), bf16[32,4,320]{2,1,0:T(4,128)(2,1)S(1)}, u32[]{:S(2)}, u32[]{:S(2)}) %all-to-all-start) | async-done | bytes 81952 | tf_op jit(solution)/shard_map/all_to_all | solution.py:266
  29.7 1.3 %shard_map.122 = (bf16[16,80,128]{2,1,0:T(8,128)(2,1)}, bf16[32,320]{1,0:T(8,128)(2,1)S(1)}, bf16[32,1280]{1,0:T(8,128)(2,1)S(1)}) custom-call(bf16[32,4,320]{2,1,0:T(4,128)(2,1)S(1)} %all-to-all-done.x_ref, f32[1,1280]{1,0:T(1,128)S(1)} %reshape.28.gain_ref, bf16[320,1280]{1,0:T(8,128)(2,1)S(1)} %slice_bitcast_fusion.w_ref), custom_call_target="tpu_custom_call" | custom-call | flops 26214400 | bytes 819200 | tf_op jit(solution)/shard_map/pallas_call | solution.py:247
  31.0 0.0 copy-start.4
  31.0 0.6 copy-done.4
  31.6 0.0 collective-permute-done.x1_hbm
  31.6 0.0 copy-start.8
  31.6 0.0 collective-permute-done.1.x2_hbm
  31.6 0.0 copy-start.9
  31.6 0.0 collective-permute-done.2.x3_hbm
  31.7 0.0 copy-start.10
  31.7 12.4 %all-to-all-start.1 = ((bf16[16,80,128]{2,1,0:T(8,128)(2,1)}), bf16[16,80,128]{2,1,0:T(8,128)(2,1)S(1)}, u32[]{:S(2)}, u32[]{:S(2)}) async-start(bf16[16,80,128]{2,1,0:T(8,128)(2,1)} %get-tuple-element.30), calls=%async_computation.1 | async-start | bytes 655360 | tf_op jit(solution)/shard_map/all_to_all | solution.py:326
  44.0 0.0 copy-done.7
  44.0 1.1 reshape.33.gain_ref
  45.8 0.0 copy-done.10
  45.8 0.0 copy-done.5
  45.8 0.6 shard_map.124
  46.4 0.0 copy-done.8
  46.4 0.0 copy-done.9
  46.4 0.0 copy-start.1
  46.4 0.0 copy-start.2
  46.4 11.3 %shard_map.123 = (f32[320,512]{1,0:T(8,128)}, bf16[320,512]{1,0:T(8,128)(2,1)}, bf16[320,512]{1,0:T(8,128)(2,1)}, bf16[320,512]{1,0:T(8,128)(2,1)}, bf16[2,32,320]{2,1,0:T(8,128)(2,1)}) custom-call(s32[1]{0:T(128)S(6)} %copy.14.len_ref, s32[1]{0:T(128)} %bitcast.tp_ref, f32[1280,1]{1,0:T(8,128)} %reshape.33.gain_ref, bf16[32,1280]{1,0:T(8,128)(2,1)} %copy-done.4, ...), custom_call_target="tpu_custom_call" | custom-call | flops 2264924160 | bytes 3276800 | tf_op jit(solution)/shard_map/pallas_call | solution.py:247
  57.7 0.0 copy-start
  57.7 0.0 copy-start.3
  57.7 0.0 copy-start.6
  57.7 1.5 %all-to-all-done.1.qp_ref = bf16[16,80,128]{2,1,0:T(8,128)(2,1)S(1)} async-done(((bf16[16,80,128]{2,1,0:T(8,128)(2,1)}), bf16[16,80,128]{2,1,0:T(8,128)(2,1)S(1)}, u32[]{:S(2)}, u32[]{:S(2)}) %all-to-all-start.1) | async-done | bytes 327712 | tf_op jit(solution)/shard_map/all_to_all | solution.py:326
  59.2 0.0 copy-done.1
  59.2 0.0 copy-done.2
  59.2 4.0 %shard_map.125 = bf16[512,384]{1,0:T(8,128)(2,1)S(1)} custom-call(bf16[16,80,128]{2,1,0:T(8,128)(2,1)S(1)} %all-to-all-done.1.qp_ref, f32[512,2]{1,0:T(8,128)S(1)} %get-tuple-element.32.bounds_ref, bf16[512,512]{1,0:T(8,128)(2,1)S(1)} %get-tuple-element.33.order_ref, bf16[320,640]{1,0:T(8,128)(2,1)S(1)} %bitcast.16, bf16[320,640]{1,0:T(8,128)(2,1)S(1)} %bitcast.17), custom_call_target="tpu_custom_call" | custom-call | flops 419430400 | bytes 819200 | tf_op jit(solution)/shard_map/pallas_call | solution.py:247
  63.2 17.3 %all_to_all.25.in_ref = bf16[8,64,384]{2,1,0:T(8,128)(2,1)S(1)} all-to-all(bf16[8,64,384]{2,1,0:T(8,128)(2,1)S(1)} %bitcast.15), channel_id=1, replica_groups=mesh['x'=4,'z'=16,'c'=2,'tp'=4] {'x','c'}, dimensions={0} | all-to-all | bytes 786432 | tf_op jit(solution)/shard_map/all_to_all | solution.py:340
  80.5 1.4 %shard_map.126 = f32[16,4,384]{2,1,0:T(4,128)} custom-call(bf16[8,64,384]{2,1,0:T(8,128)(2,1)S(1)} %all_to_all.25.in_ref), custom_call_target="tpu_custom_call" | custom-call | flops 196608 | bytes 786432 | tf_op jit(solution)/shard_map/pallas_call | solution.py:247
  81.9 5.7 %all-to-all-start.3 = ((f32[16,4,384]{2,1,0:T(4,128)}), f32[16,4,384]{2,1,0:T(4,128)S(1)}, u32[]{:S(2)}, u32[]{:S(2)}) async-start(f32[16,4,384]{2,1,0:T(4,128)} %shard_map.126), calls=%async_computation.3 | async-start | bytes 196608 | tf_op jit(solution)/shard_map/all_to_all | solution.py:349
  87.5 4.0 %collective-permute-start.3 = (bf16[320,512]{1,0:T(8,128)(2,1)}, bf16[320,512]{1,0:T(8,128)(2,1)S(1)}, u32[]{:S(2)}, u32[]{:S(2)}) collective-permute-start(bf16[320,512]{1,0:T(8,128)(2,1)} %get-tuple-element.26), channel_id=1, source_target_pairs={{0,1},{1,2},{2,3},{3,0},{4,5},{5,6},{6,7},{7,4},{8,9},{9,10},{10,1... | collective-permute-start | bytes 983048 | tf_op jit(solution)/shard_map/ppermute | solution.py:287
  91.5 3.2 %collective-permute-start.4 = (bf16[320,512]{1,0:T(8,128)(2,1)}, bf16[320,512]{1,0:T(8,128)(2,1)S(1)}, u32[]{:S(2)}, u32[]{:S(2)}) collective-permute-start(bf16[320,512]{1,0:T(8,128)(2,1)} %get-tuple-element.27), channel_id=1, source_target_pairs={{0,2},{1,3},{2,0},{3,1},{4,6},{5,7},{6,4},{7,5},{8,10},{9,11},{10,... | collective-permute-start | bytes 983048 | tf_op jit(solution)/shard_map/ppermute | solution.py:287
  94.7 3.4 %collective-permute-start.5 = (bf16[320,512]{1,0:T(8,128)(2,1)}, bf16[320,512]{1,0:T(8,128)(2,1)S(1)}, u32[]{:S(2)}, u32[]{:S(2)}) collective-permute-start(bf16[320,512]{1,0:T(8,128)(2,1)} %get-tuple-element.28), channel_id=1, source_target_pairs={{0,3},{1,0},{2,1},{3,2},{4,7},{5,4},{6,5},{7,6},{8,11},{9,8},{10,9... | collective-permute-start | bytes 983048 | tf_op jit(solution)/shard_map/ppermute | solution.py:287
  98.1 1.3 %all-to-all-done.3.in_ref = f32[16,4,384]{2,1,0:T(4,128)S(1)} async-done(((f32[16,4,384]{2,1,0:T(4,128)}), f32[16,4,384]{2,1,0:T(4,128)S(1)}, u32[]{:S(2)}, u32[]{:S(2)}) %all-to-all-start.3) | async-done | bytes 98336 | tf_op jit(solution)/shard_map/all_to_all | solution.py:349
  99.4 0.0 copy-done
  99.4 0.0 copy-done.3
  99.4 1.3 %shard_map.127 = f32[4,4,320]{2,1,0:T(4,128)} custom-call(s32[1]{0:T(128)} %bitcast.7.own_ref, f32[16,4,384]{2,1,0:T(4,128)S(1)} %all-to-all-done.3.in_ref, bf16[32,320]{1,0:T(8,128)(2,1)S(1)} %get-tuple-element.34.q_ref, bf16[2,32,320]{2,1,0:T(8,128)(2,1)S(1)} %copy-done.3, bf16[320,1280]{1,0:T(8,128)(2,1)S(1)} %copy-done), custom_call_target="tpu_custom_call" | custom-call | flops 6553600 | bytes 819200 | tf_op jit(solution)/shard_map/pallas_call | solution.py:247
  100.7 4.0 %all-to-all-start.4 = ((f32[4,4,320]{2,1,0:T(4,128)}), f32[4,4,320]{2,1,0:T(4,128)S(1)}, u32[]{:S(2)}, u32[]{:S(2)}) async-start(f32[4,4,320]{2,1,0:T(4,128)} %shard_map.127), calls=%async_computation.4 | async-start | bytes 49152 | tf_op jit(solution)/shard_map/all_to_all | solution.py:358
  104.7 0.0 collective-permute-done.3
  104.7 1.9 %collective-permute-done.4 = bf16[320,512]{1,0:T(8,128)(2,1)S(1)} collective-permute-done((bf16[320,512]{1,0:T(8,128)(2,1)}, bf16[320,512]{1,0:T(8,128)(2,1)S(1)}, u32[]{:S(2)}, u32[]{:S(2)}) %collective-permute-start.4) | collective-permute-done | bytes 327712 | tf_op jit(solution)/shard_map/ppermute | solution.py:287
  106.6 2.0 %collective-permute-done.5 = bf16[320,512]{1,0:T(8,128)(2,1)S(1)} collective-permute-done((bf16[320,512]{1,0:T(8,128)(2,1)}, bf16[320,512]{1,0:T(8,128)(2,1)S(1)}, u32[]{:S(2)}, u32[]{:S(2)}) %collective-permute-start.5) | collective-permute-done | bytes 327712 | tf_op jit(solution)/shard_map/ppermute | solution.py:287
  108.6 0.0 copy-done.6
  108.6 0.9 fusion
  109.5 0.0 all-to-all-done.4
  109.5 0.6 reduce_sum.9
Async XLA Ops:
  0.6 43.4 %copy-start.7 = (f32[1280]{0:T(1024)S(1)}, f32[1280]{0:T(1024)}, u32[]{:S(2)}) copy-start(f32[1280]{0:T(1024)} %param.13) | copy-start | bytes 15364
  0.6 45.2 %copy-start.5 = (s32[512]{0:T(512)S(1)}, s32[512]{0:T(512)}, u32[]{:S(2)}) copy-start(s32[512]{0:T(512)} %param.21) | copy-start | bytes 6148
  0.7 31.0 %collective-permute-start = (bf16[320,512]{1,0:T(8,128)(2,1)}, bf16[320,512]{1,0:T(8,128)(2,1)S(1)}, u32[]{:S(2)}, u32[]{:S(2)}) collective-permute-start(bf16[320,512]{1,0:T(8,128)(2,1)} %bitcast.21), channel_id=1, source_target_pairs={{0,1},{1,2},{2,3},{3,0},{4,5},{5,6},{6,7},{7,4},{8,9},{9,10},{10,1... | collective-permute-start | bytes 983048 | tf_op jit(solution)/shard_map/ppermute | solution.py:287
  4.8 26.8 %collective-permute-start.1 = (bf16[320,512]{1,0:T(8,128)(2,1)}, bf16[320,512]{1,0:T(8,128)(2,1)S(1)}, u32[]{:S(2)}, u32[]{:S(2)}) collective-permute-start(bf16[320,512]{1,0:T(8,128)(2,1)} %bitcast.22), channel_id=1, source_target_pairs={{0,2},{1,3},{2,0},{3,1},{4,6},{5,7},{6,4},{7,5},{8,10},{9,11},{10,... | collective-permute-start | bytes 983048 | tf_op jit(solution)/shard_map/ppermute | solution.py:287
  9.4 22.3 %collective-permute-start.2 = (bf16[320,512]{1,0:T(8,128)(2,1)}, bf16[320,512]{1,0:T(8,128)(2,1)S(1)}, u32[]{:S(2)}, u32[]{:S(2)}) collective-permute-start(bf16[320,512]{1,0:T(8,128)(2,1)} %bitcast.23), channel_id=1, source_target_pairs={{0,3},{1,0},{2,1},{3,2},{4,7},{5,4},{6,5},{7,6},{8,11},{9,8},{10,9... | collective-permute-start | bytes 983048 | tf_op jit(solution)/shard_map/ppermute | solution.py:287
  13.7 16.0 %all-to-all-start = ((bf16[32,4,320]{2,1,0:T(4,128)(2,1)}), bf16[32,4,320]{2,1,0:T(4,128)(2,1)S(1)}, u32[]{:S(2)}, u32[]{:S(2)}) async-start(bf16[32,4,320]{2,1,0:T(4,128)(2,1)} %broadcast_in_dim.2), calls=%async_computation | async-start | bytes 196608 | tf_op jit(solution)/shard_map/all_to_all | solution.py:266
  31.0 0.6 copy-start.4
  31.6 14.8 %copy-start.8 = (bf16[320,512]{1,0:T(8,128)(2,1)}, bf16[320,512]{1,0:T(8,128)(2,1)S(1)}, u32[]{:S(2)}) copy-start(bf16[320,512]{1,0:T(8,128)(2,1)S(1)} %collective-permute-done.x1_hbm) | copy-start | bytes 983044
  31.6 14.8 %copy-start.9 = (bf16[320,512]{1,0:T(8,128)(2,1)}, bf16[320,512]{1,0:T(8,128)(2,1)S(1)}, u32[]{:S(2)}) copy-start(bf16[320,512]{1,0:T(8,128)(2,1)S(1)} %collective-permute-done.1.x2_hbm) | copy-start | bytes 983044
  31.7 14.1 %copy-start.10 = (bf16[320,512]{1,0:T(8,128)(2,1)}, bf16[320,512]{1,0:T(8,128)(2,1)S(1)}, u32[]{:S(2)}) copy-start(bf16[320,512]{1,0:T(8,128)(2,1)S(1)} %collective-permute-done.2.x3_hbm) | copy-start | bytes 983044
  31.7 27.5 %all-to-all-start.1 = ((bf16[16,80,128]{2,1,0:T(8,128)(2,1)}), bf16[16,80,128]{2,1,0:T(8,128)(2,1)S(1)}, u32[]{:S(2)}, u32[]{:S(2)}) async-start(bf16[16,80,128]{2,1,0:T(8,128)(2,1)} %get-tuple-element.30), calls=%async_computation.1 | async-start | bytes 655360 | tf_op jit(solution)/shard_map/all_to_all | solution.py:326
  46.4 12.8 %copy-start.1 = (bf16[640,320]{0,1:T(8,128)(2,1)S(1)}, bf16[640,320]{0,1:T(8,128)(2,1)}, u32[]{:S(2)}) copy-start(bf16[640,320]{0,1:T(8,128)(2,1)} %param.19) | copy-start | bytes 1228804
  46.4 12.8 %copy-start.2 = (bf16[640,320]{0,1:T(8,128)(2,1)S(1)}, bf16[640,320]{0,1:T(8,128)(2,1)}, u32[]{:S(2)}) copy-start(bf16[640,320]{0,1:T(8,128)(2,1)} %param.20) | copy-start | bytes 1228804
  57.7 41.7 %copy-start = (bf16[320,1280]{1,0:T(8,128)(2,1)S(1)}, bf16[320,1280]{1,0:T(8,128)(2,1)}, u32[]{:S(2)}) copy-start(bf16[320,1280]{1,0:T(8,128)(2,1)} %w_ref.1) | copy-start | bytes 2457604
  57.7 41.7 %copy-start.3 = (bf16[2,32,320]{2,1,0:T(8,128)(2,1)S(1)}, bf16[2,32,320]{2,1,0:T(8,128)(2,1)}, u32[]{:S(2)}) copy-start(bf16[2,32,320]{2,1,0:T(8,128)(2,1)} %get-tuple-element.35.kv_ref) | copy-start | bytes 122884
  57.7 50.9 %copy-start.6 = (f32[320,512]{1,0:T(8,128)S(1)}, f32[320,512]{1,0:T(8,128)}, u32[]{:S(2)}) copy-start(f32[320,512]{1,0:T(8,128)} %get-tuple-element.25) | copy-start | bytes 1966084
  81.9 17.5 %all-to-all-start.3 = ((f32[16,4,384]{2,1,0:T(4,128)}), f32[16,4,384]{2,1,0:T(4,128)S(1)}, u32[]{:S(2)}, u32[]{:S(2)}) async-start(f32[16,4,384]{2,1,0:T(4,128)} %shard_map.126), calls=%async_computation.3 | async-start | bytes 196608 | tf_op jit(solution)/shard_map/all_to_all | solution.py:349
  87.5 17.2 %collective-permute-start.3 = (bf16[320,512]{1,0:T(8,128)(2,1)}, bf16[320,512]{1,0:T(8,128)(2,1)S(1)}, u32[]{:S(2)}, u32[]{:S(2)}) collective-permute-start(bf16[320,512]{1,0:T(8,128)(2,1)} %get-tuple-element.26), channel_id=1, source_target_pairs={{0,1},{1,2},{2,3},{3,0},{4,5},{5,6},{6,7},{7,4},{8,9},{9,10},{10,1... | collective-permute-start | bytes 983048 | tf_op jit(solution)/shard_map/ppermute | solution.py:287
  91.5 15.1 %collective-permute-start.4 = (bf16[320,512]{1,0:T(8,128)(2,1)}, bf16[320,512]{1,0:T(8,128)(2,1)S(1)}, u32[]{:S(2)}, u32[]{:S(2)}) collective-permute-start(bf16[320,512]{1,0:T(8,128)(2,1)} %get-tuple-element.27), channel_id=1, source_target_pairs={{0,2},{1,3},{2,0},{3,1},{4,6},{5,7},{6,4},{7,5},{8,10},{9,11},{10,... | collective-permute-start | bytes 983048 | tf_op jit(solution)/shard_map/ppermute | solution.py:287
  94.7 13.9 %collective-permute-start.5 = (bf16[320,512]{1,0:T(8,128)(2,1)}, bf16[320,512]{1,0:T(8,128)(2,1)S(1)}, u32[]{:S(2)}, u32[]{:S(2)}) collective-permute-start(bf16[320,512]{1,0:T(8,128)(2,1)} %get-tuple-element.28), channel_id=1, source_target_pairs={{0,3},{1,0},{2,1},{3,2},{4,7},{5,4},{6,5},{7,6},{8,11},{9,8},{10,9... | collective-permute-start | bytes 983048 | tf_op jit(solution)/shard_map/ppermute | solution.py:287
  100.7 8.8 %all-to-all-start.4 = ((f32[4,4,320]{2,1,0:T(4,128)}), f32[4,4,320]{2,1,0:T(4,128)S(1)}, u32[]{:S(2)}, u32[]{:S(2)}) async-start(f32[4,4,320]{2,1,0:T(4,128)} %shard_map.127), calls=%async_computation.4 | async-start | bytes 49152 | tf_op jit(solution)/shard_map/all_to_all | solution.py:358

commit v5 on v4

--- a/solution.py
+++ b/solution.py
@@ -39,14 +39,14 @@
 
 
 def dec_project_kernel(x_ref, gain_ref, w_ref, qb_ref, q_ref, hidden_ref, rows):
-    for n in range(NX * NC):
+    for n in range(NX):
         for t in range(NT):
             rows[4 * n : 4 * n + 4, t * WIDTH : (t + 1) * WIDTH] = x_ref[NT * n + t].astype(F32)
     hidden = normed_rows(rows[...], gain_ref[...])
     hidden_ref[...] = hidden
     value = dot(hidden, w_ref[...], ((1,), (1,)))
     q_ref[...] = value.astype(BF16)
-    tail = jnp.concatenate([value[0:16, 256:WIDTH], value[16:32, 256:WIDTH]], axis=1)
+    tail = jnp.concatenate([value[0:8, 256:WIDTH], value[8:16, 256:WIDTH]], axis=1)
     packed = jnp.concatenate([value[:, 0:128], value[:, 128:256], tail], axis=0).astype(BF16)
     for z in range(NZ):
         qb_ref[z] = packed
@@ -57,7 +57,7 @@
     place = lax.broadcasted_iota(jnp.int32, (requests, requests), 0)
     x, c, z, i = place >> 7, (place >> 6) & 1, (place >> 2) & 15, place & 3
     request = (x << 7) | (z << 3) | (c << 2) | i
-    arrived = (z << 5) | (x << 3) | (c << 2) | i
+    arrived = (c << 8) | (z << 4) | (x << 2) | i
     other = lax.broadcasted_iota(jnp.int32, (requests, requests), 1)
     lens = lens_ref[...].astype(F32)
     base = base_ref[0].astype(F32)
@@ -67,12 +67,12 @@
 
 
 def dec_attention_kernel(qp_ref, bounds_ref, order_ref, k_ref, v_ref, out_ref, q_s):
-    for z in range(NZ):
-        rows = slice(32 * z, 32 * z + 32)
-        q_s[rows, 0:128] = qp_ref[z, 0:32]
-        q_s[rows, 128:256] = qp_ref[z, 32:64]
-        q_s[32 * z : 32 * z + 16, 256:WIDTH] = qp_ref[z, 64:80, 0:64]
-        q_s[32 * z + 16 : 32 * z + 32, 256:WIDTH] = qp_ref[z, 64:80, 64:128]
+    for n in range(NC * NZ):
+        at = 16 * n
+        q_s[at : at + 16, 0:128] = qp_ref[n, 0:16]
+        q_s[at : at + 16, 128:256] = qp_ref[n, 16:32]
+        q_s[at : at + 8, 256:WIDTH] = qp_ref[n, 32:40, 0:64]
+        q_s[at + 8 : at + 16, 256:WIDTH] = qp_ref[n, 32:40, 64:128]
     requests, pool = q_s.shape[0], k_ref.shape[1]
     queries = dot(order_ref[...], q_s[...], ((1,), (0,))).astype(BF16)
     row = lax.broadcasted_iota(jnp.int32, (requests, pool), 1).astype(F32)
@@ -149,8 +149,8 @@
     rows = 4
     whole = lambda block, n: block[:, WIDTH + n : WIDTH + n + 1]
     values, tops, totals = merged([in_ref[n] for n in range(NZ)], rows, whole)
-    row = lax.broadcasted_iota(jnp.int32, (8, 32), 0) + 4 * own_ref[0]
-    mine = jnp.where(row == lax.broadcasted_iota(jnp.int32, (8, 32), 1), 1.0, 0.0).astype(BF16)
+    row = lax.broadcasted_iota(jnp.int32, (8, 16), 0) + 4 * own_ref[0]
+    mine = jnp.where(row == lax.broadcasted_iota(jnp.int32, (8, 16), 1), 1.0, 0.0).astype(BF16)
     query = dot(mine, q_ref[...], ((1,), (0,)))[0:rows]
     key = dot(mine, kv_ref[0], ((1,), (0,)))[0:rows]
     value = dot(mine, kv_ref[1], ((1,), (0,)))[0:rows]
@@ -287,27 +287,30 @@
         return lax.ppermute(block, "tp", [(t, (t + shift) % NT) for t in range(NT)])
 
     tp = lax.axis_index("tp").astype(jnp.int32).reshape(1)
-    own = (lax.axis_index("x") * NC + lax.axis_index("c")).astype(jnp.int32).reshape(1)
-    x_rows = spread(x_dec, ("x", "c", "tp"), NX * NC * NT)
+    own = lax.axis_index("x").astype(jnp.int32).reshape(1)
+    x_rows = spread(x_dec, ("x", "tp"), NX * NT)
     x_t = x_pre.T
     x_blocks = [x_t] + [turned(x_t, shift) for shift in range(1, NT)]
     queries, own_queries, hidden = call(
         dec_project_kernel,
-        (shape((NZ, 80, 128), BF16), shape((32, WIDTH), BF16), shape((32, full), BF16)),
+        (shape((NZ, 40, 128), BF16), shape((16, WIDTH), BF16), shape((16, full), BF16)),
         (),
         (x_rows, norm_gain.reshape(1, full), w_t[0]),
-        scratch=[pltpu.VMEM((32, full), F32)],
-        flops=2 * 32 * full * WIDTH,
+        scratch=[pltpu.VMEM((16, full), F32)],
+        flops=2 * 16 * full * WIDTH,
         moved=2 * full * WIDTH,
     )
-    *x_blocks, queries = lax.optimization_barrier((*x_blocks, queries))
+    gain_column = norm_gain.reshape(full, 1)
+    *x_blocks, gain_column, bounds, order, queries = lax.optimization_barrier(
+        (*x_blocks, gain_column, bounds, order, queries)
+    )
     term_blocks = call(
         prefill_kernel,
         (shape((WIDTH, tokens), F32),)
         + (shape((WIDTH, tokens), BF16),) * 3
-        + (shape((2, 32, WIDTH), BF16),),
+        + (shape((2, 16, WIDTH), BF16),),
         (pre_lens, tp),
-        (norm_gain.reshape(full, 1), hidden),
+        (gain_column, hidden),
         (*x_blocks, w_t, pre_keys.T, pre_values.T, w_out),
         scratch=[
             pltpu.VMEM((full, tokens), BF16),
@@ -326,6 +329,7 @@
     queries = lax.all_to_all(queries, "z", 0, 0, tiled=True)
     *term_blocks, own_kv = term_blocks
     own_kv, queries = lax.optimization_barrier((own_kv, queries))
+    queries = lax.all_gather(queries, "c", axis=0, tiled=True)
     arrived = [turned(block, shift) for shift, block in enumerate(term_blocks) if shift > 0]
     pre_out = term_blocks[0] + sum(block.astype(F32) for block in arrived)
     partial = call(

time: 112 us -> 112 us (level); the launches traced: 110 us -> 111 us
    all_gather x0 -> x1, blocking collectives: none -> 5.14 us  [body(): queries = lax.all_gather(queries, 'c', axis=0, tiled=True)]
    all_to_all x1, blocking collectives: 17.3 us -> 12.6 us  [body(): lax.all_to_all(partial.reshape(NX * NC, NZ * 4, LANES), ('x', 'c'), 0, 0,...]
    all_to_all x1, starting transfers between devices: 12.4 us -> 16.9 us  [body(): queries = lax.all_to_all(queries, 'z', 0, 0, tiled=True)]
    all_to_all x1, starting transfers between devices: 5.65 us -> 9.26 us  [body(): partial = lax.all_to_all(partial, 'z', 0, 0, tiled=True)]
    ppermute x6, starting transfers between devices: 22.2 us -> 18.7 us  [turned(): return lax.ppermute(block, 'tp', [(t, (t + shift) % NT) for t in range(NT)])]
    all_to_all x1, starting transfers between devices: 8.65 us -> 5.83 us  [spread(): return lax.all_to_all(copies, axes, 0, 0, tiled=True)]
    all_to_all x1, waiting for transfers between devices: 5.42 us -> 2.8 us  [spread(): return lax.all_to_all(copies, axes, 0, 0, tiled=True)]
    all_to_all x1, waiting for transfers between devices: 1.28 us -> 3.4 us  [body(): partial = lax.all_to_all(partial, 'z', 0, 0, tiled=True)]
  transfers between devices with their start and end apart: 10 -> 10, of which waited for: 5 -> 4; matrix products, arithmetic and copies ran while one was open for 5% -> 5% of each run, Pallas kernels for 13% -> 13%
where the time goes in v5:
time: 112 us; the launch traced here: 111 us
  starting transfers between devices  54 us (48%)
  Pallas kernels  19.7 us (18%)
  blocking collectives  17.7 us (16%)
  waiting for transfers between devices  11.3 us (10%)
  local copies, waits for them, and re-layouts  5.78 us (5%)
  other arithmetic  1.49 us (1%)
  between operations  1.48 us (1%)
    pallas_call x6, Pallas kernels, call(): pl.pallas_call(kernel, out_shape=out_shape, in_specs=[pl.BlockSpec(memory...  19.7 us
    ppermute x6, starting transfers between devices, turned(): return lax.ppermute(block, 'tp', [(t, (t + shift) % NT) for t in range(NT)])  18.7 us
    all_to_all x1, starting transfers between devices, body(): queries = lax.all_to_all(queries, 'z', 0, 0, tiled=True)  16.9 us
    all_to_all x1, blocking collectives, body(): lax.all_to_all(partial.reshape(NX * NC, NZ * 4, LANES), ('x', 'c'), 0, 0,...  12.6 us
    all_to_all x1, starting transfers between devices, body(): partial = lax.all_to_all(partial, 'z', 0, 0, tiled=True)  9.26 us
    all_to_all x1, starting transfers between devices, spread(): return lax.all_to_all(copies, axes, 0, 0, tiled=True)  5.83 us
    all_gather x1, blocking collectives, body(): queries = lax.all_gather(queries, 'c', axis=0, tiled=True)  5.14 us
    ppermute x6, waiting for transfers between devices, turned(): return lax.ppermute(block, 'tp', [(t, (t + shift) % NT) for t in range(NT)])  5.05 us
  transfers between devices with their start and end apart: 10, of which 4 were waited for; matrix products, arithmetic and copies ran while one was open for 5% of the time, Pallas kernels for 13%

profile of v5, /device:TPU:1, one launch (start us, length us, event | category | flops | bytes accessed | tf_op | source)
XLA Modules:
  0.0 111.5 jit_solution(5873785483506942752)
XLA Ops:
  0.6 5.5 %collective-permute-start.2 = (bf16[320,512]{1,0:T(8,128)(2,1)}, bf16[320,512]{1,0:T(8,128)(2,1)S(1)}, u32[]{:S(2)}, u32[]{:S(2)}) collective-permute-start(bf16[320,512]{1,0:T(8,128)(2,1)} %bitcast.21), channel_id=1, source_target_pairs={{0,3},{1,0},{2,1},{3,2},{4,7},{5,4},{6,5},{7,6},{8,11},{9,8},{10,9... | collective-permute-start | bytes 983048 | tf_op jit(solution)/shard_map/ppermute | solution.py:287
  6.1 2.3 %collective-permute-start.1 = (bf16[320,512]{1,0:T(8,128)(2,1)}, bf16[320,512]{1,0:T(8,128)(2,1)S(1)}, u32[]{:S(2)}, u32[]{:S(2)}) collective-permute-start(bf16[320,512]{1,0:T(8,128)(2,1)} %bitcast.22), channel_id=1, source_target_pairs={{0,2},{1,3},{2,0},{3,1},{4,6},{5,7},{6,4},{7,5},{8,10},{9,11},{10,... | collective-permute-start | bytes 983048 | tf_op jit(solution)/shard_map/ppermute | solution.py:287
  8.4 2.6 %collective-permute-start = (bf16[320,512]{1,0:T(8,128)(2,1)}, bf16[320,512]{1,0:T(8,128)(2,1)S(1)}, u32[]{:S(2)}, u32[]{:S(2)}) collective-permute-start(bf16[320,512]{1,0:T(8,128)(2,1)} %bitcast.23), channel_id=1, source_target_pairs={{0,1},{1,2},{2,3},{3,0},{4,5},{5,6},{6,7},{7,4},{8,9},{9,10},{10,1... | collective-permute-start | bytes 983048 | tf_op jit(solution)/shard_map/ppermute | solution.py:287
  11.0 1.3 %broadcast_in_dim.2 = bf16[16,4,320]{2,1,0:T(4,128)(2,1)} broadcast(bf16[4,320]{1,0:T(4,128)(2,1)} %param.12), dimensions={1,2} | broadcast | bytes 43520 | tf_op jit(solution)/shard_map/broadcast_in_dim | solution.py:265
  12.3 5.8 %all-to-all-start = ((bf16[16,4,320]{2,1,0:T(4,128)(2,1)}), bf16[16,4,320]{2,1,0:T(4,128)(2,1)S(1)}, u32[]{:S(2)}, u32[]{:S(2)}) async-start(bf16[16,4,320]{2,1,0:T(4,128)(2,1)} %broadcast_in_dim.2), calls=%async_computation | async-start | bytes 98304 | tf_op jit(solution)/shard_map/all_to_all | solution.py:266
  18.1 1.2 %slice_bitcast_fusion.w_ref = bf16[320,1280]{1,0:T(8,128)(2,1)S(1)} fusion(bf16[3,320,1280]{2,1,0:T(8,128)(2,1)} %bitcast.19), kind=kLoop, calls=%fused_computation | loop fusion | bytes 1638400 | tf_op jit(solution)/shard_map/squeeze | solution.py:298
  19.3 0.7 reshape.30.gain_ref
  20.1 0.7 reshape.27
  20.8 0.0 copy-start.5
  20.8 0.7 copy-done.5
  21.4 0.6 shard_map.122
  22.0 2.8 %all-to-all-done.x_ref = bf16[16,4,320]{2,1,0:T(4,128)(2,1)S(1)} async-done(((bf16[16,4,320]{2,1,0:T(4,128)(2,1)}), bf16[16,4,320]{2,1,0:T(4,128)(2,1)S(1)}, u32[]{:S(2)}, u32[]{:S(2)}) %all-to-all-start) | async-done | bytes 40992 | tf_op jit(solution)/shard_map/all_to_all | solution.py:266
  24.8 1.2 %shard_map.123 = (bf16[16,40,128]{2,1,0:T(8,128)(2,1)}, bf16[16,320]{1,0:T(8,128)(2,1)S(1)}, bf16[16,1280]{1,0:T(8,128)(2,1)S(1)}) custom-call(bf16[16,4,320]{2,1,0:T(4,128)(2,1)S(1)} %all-to-all-done.x_ref, f32[1,1280]{1,0:T(1,128)S(1)} %reshape.30.gain_ref, bf16[320,1280]{1,0:T(8,128)(2,1)S(1)} %slice_bitcast_fusion.w_ref), custom_call_target="tpu_custom_call" | custom-call | flops 13107200 | bytes 819200 | tf_op jit(solution)/shard_map/pallas_call | solution.py:247
  26.0 0.0 copy-start.4
  26.0 0.0 collective-permute-done.2.x3_hbm
  26.0 0.0 copy-start.7
  26.0 0.0 collective-permute-done.1.x2_hbm
  26.0 0.0 copy-start.8
  26.0 0.0 collective-permute-done.x1_hbm
  26.0 0.0 copy-start.9
  26.1 16.9 %all-to-all-start.1 = ((bf16[16,40,128]{2,1,0:T(8,128)(2,1)}), bf16[16,40,128]{2,1,0:T(8,128)(2,1)S(1)}, u32[]{:S(2)}, u32[]{:S(2)}) async-start(bf16[16,40,128]{2,1,0:T(8,128)(2,1)} %get-tuple-element.36), calls=%async_computation.1 | async-start | bytes 327680 | tf_op jit(solution)/shard_map/all_to_all | solution.py:329
  43.6 1.1 %copy.14.gain_ref = f32[1280,1]{1,0:T(8,128)} copy(f32[1280,1]{0,1:T(1,128)S(1)} %reshape.27) | data formatting | bytes 10240 | tf_op jit(solution)/shard_map/optimization_barrier | solution.py:304
  44.7 0.0 copy-done.4
  44.7 0.0 copy-done.9
  44.7 0.0 copy-done.7
  44.7 0.0 copy-done.8
  44.7 0.0 copy-start.1
  44.7 0.0 copy-start.2
  44.8 11.2 %shard_map.124 = (f32[320,512]{1,0:T(8,128)}, bf16[320,512]{1,0:T(8,128)(2,1)}, bf16[320,512]{1,0:T(8,128)(2,1)}, bf16[320,512]{1,0:T(8,128)(2,1)}, bf16[2,16,320]{2,1,0:T(8,128)(2,1)}) custom-call(s32[1]{0:T(128)S(6)} %copy.15.len_ref, s32[1]{0:T(128)} %bitcast.tp_ref, f32[1280,1]{1,0:T(8,128)} %copy.14.gain_ref, bf16[16,1280]{1,0:T(8,128)(2,1)} %copy-done.4, ...), custom_call_target="tpu_custom_call" | custom-call | flops 2264924160 | bytes 3276800 | tf_op jit(solution)/shard_map/pallas_call | solution.py:247
  56.0 0.0 copy-start.10
  56.0 0.0 copy-start
  56.0 0.0 copy-start.3
  56.0 0.0 all-to-all-done.1
  56.0 5.1 %all_gather.3.qp_ref = bf16[32,40,128]{2,1,0:T(8,128)(2,1)S(1)} all-gather(bf16[16,40,128]{2,1,0:T(8,128)(2,1)S(1)} %all-to-all-done.1), channel_id=1, replica_groups=mesh['x'=4,'z'=16,'c'=2,'tp'=4] {'c'}, dimensions={0}, use_global_device_ids=true | all-gather | bytes 491520 | tf_op jit(solution)/shard_map/all_gather | solution.py:332
  61.2 0.0 copy-start.6
  61.2 0.0 copy-done.1
  61.2 0.0 copy-done.2
  61.2 4.0 %shard_map.125 = bf16[512,384]{1,0:T(8,128)(2,1)S(1)} custom-call(bf16[32,40,128]{2,1,0:T(8,128)(2,1)S(1)} %all_gather.3.qp_ref, f32[512,2]{1,0:T(8,128)S(1)} %get-tuple-element.38.bounds_ref, bf16[512,512]{1,0:T(8,128)(2,1)S(1)} %get-tuple-element.39.order_ref, bf16[320,640]{1,0:T(8,128)(2,1)S(1)} %bitcast.16, bf16[320,640]{1,0:T(8,128)(2,1)S(1)} %bitcast.17), custom_call_target="tpu_custom_call" | custom-call | flops 419430400 | bytes 819200 | tf_op jit(solution)/shard_map/pallas_call | solution.py:247
  65.2 12.6 %all_to_all.25.in_ref = bf16[8,64,384]{2,1,0:T(8,128)(2,1)S(1)} all-to-all(bf16[8,64,384]{2,1,0:T(8,128)(2,1)S(1)} %bitcast.15), channel_id=1, replica_groups=mesh['x'=4,'z'=16,'c'=2,'tp'=4] {'x','c'}, dimensions={0} | all-to-all | bytes 786432 | tf_op jit(solution)/shard_map/all_to_all | solution.py:344
  77.8 1.4 %shard_map.126 = f32[16,4,384]{2,1,0:T(4,128)} custom-call(bf16[8,64,384]{2,1,0:T(8,128)(2,1)S(1)} %all_to_all.25.in_ref), custom_call_target="tpu_custom_call" | custom-call | flops 196608 | bytes 786432 | tf_op jit(solution)/shard_map/pallas_call | solution.py:247
  79.2 9.3 %all-to-all-start.3 = ((f32[16,4,384]{2,1,0:T(4,128)}), f32[16,4,384]{2,1,0:T(4,128)S(1)}, u32[]{:S(2)}, u32[]{:S(2)}) async-start(f32[16,4,384]{2,1,0:T(4,128)} %shard_map.126), calls=%async_computation.3 | async-start | bytes 196608 | tf_op jit(solution)/shard_map/all_to_all | solution.py:353
  88.4 1.9 %collective-permute-start.3 = (bf16[320,512]{1,0:T(8,128)(2,1)}, bf16[320,512]{1,0:T(8,128)(2,1)S(1)}, u32[]{:S(2)}, u32[]{:S(2)}) collective-permute-start(bf16[320,512]{1,0:T(8,128)(2,1)} %get-tuple-element.32), channel_id=1, source_target_pairs={{0,1},{1,2},{2,3},{3,0},{4,5},{5,6},{6,7},{7,4},{8,9},{9,10},{10,1... | collective-permute-start | bytes 983048 | tf_op jit(solution)/shard_map/ppermute | solution.py:287
  90.4 3.4 %collective-permute-start.4 = (bf16[320,512]{1,0:T(8,128)(2,1)}, bf16[320,512]{1,0:T(8,128)(2,1)S(1)}, u32[]{:S(2)}, u32[]{:S(2)}) collective-permute-start(bf16[320,512]{1,0:T(8,128)(2,1)} %get-tuple-element.33), channel_id=1, source_target_pairs={{0,2},{1,3},{2,0},{3,1},{4,6},{5,7},{6,4},{7,5},{8,10},{9,11},{10,... | collective-permute-start | bytes 983048 | tf_op jit(solution)/shard_map/ppermute | solution.py:287
  93.8 0.0 copy-done.10
  93.8 3.1 %collective-permute-start.5 = (bf16[320,512]{1,0:T(8,128)(2,1)S(1)}, bf16[320,512]{1,0:T(8,128)(2,1)S(1)}, u32[]{:S(2)}, u32[]{:S(2)}) collective-permute-start(bf16[320,512]{1,0:T(8,128)(2,1)S(1)} %copy-done.10), channel_id=1, source_target_pairs={{0,3},{1,0},{2,1},{3,2},{4,7},{5,4},{6,5},{7,6},{8,11},{9,8},{10,9... | collective-permute-start | bytes 983048 | tf_op jit(solution)/shard_map/ppermute | solution.py:287
  96.9 3.4 %all-to-all-done.3.in_ref = f32[16,4,384]{2,1,0:T(4,128)S(1)} async-done(((f32[16,4,384]{2,1,0:T(4,128)}), f32[16,4,384]{2,1,0:T(4,128)S(1)}, u32[]{:S(2)}, u32[]{:S(2)}) %all-to-all-start.3) | async-done | bytes 98336 | tf_op jit(solution)/shard_map/all_to_all | solution.py:353
  100.3 0.0 copy-done
  100.3 0.0 copy-done.3
  100.3 1.3 %shard_map.127 = f32[4,4,320]{2,1,0:T(4,128)} custom-call(s32[1]{0:T(128)} %bitcast.9.own_ref, f32[16,4,384]{2,1,0:T(4,128)S(1)} %all-to-all-done.3.in_ref, bf16[16,320]{1,0:T(8,128)(2,1)S(1)} %get-tuple-element.40.q_ref, bf16[2,16,320]{2,1,0:T(8,128)(2,1)S(1)} %copy-done.3, bf16[320,1280]{1,0:T(8,128)(2,1)S(1)} %copy-done), custom_call_target="tpu_custom_call" | custom-call | flops 6553600 | bytes 819200 | tf_op jit(solution)/shard_map/pallas_call | solution.py:247
  101.6 3.3 %all-to-all-start.4 = ((f32[4,4,320]{2,1,0:T(4,128)}), f32[4,4,320]{2,1,0:T(4,128)S(1)}, u32[]{:S(2)}, u32[]{:S(2)}) async-start(f32[4,4,320]{2,1,0:T(4,128)} %shard_map.127), calls=%async_computation.4 | async-start | bytes 49152 | tf_op jit(solution)/shard_map/all_to_all | solution.py:362
  104.9 0.0 collective-permute-done.3
  104.9 0.8 collective-permute-done.4
  105.7 4.2 %collective-permute-done.5 = bf16[320,512]{1,0:T(8,128)(2,1)S(1)} collective-permute-done((bf16[320,512]{1,0:T(8,128)(2,1)S(1)}, bf16[320,512]{1,0:T(8,128)(2,1)S(1)}, u32[]{:S(2)}, u32[]{:S(2)}) %collective-permute-start.5) | collective-permute-done | bytes 327712 | tf_op jit(solution)/shard_map/ppermute | solution.py:287
  110.0 0.0 copy-done.6
  110.0 0.9 fusion
  110.9 0.0 all-to-all-done.4
  110.9 0.6 reduce_sum.9
Async XLA Ops:
  0.6 25.4 %collective-permute-start.2 = (bf16[320,512]{1,0:T(8,128)(2,1)}, bf16[320,512]{1,0:T(8,128)(2,1)S(1)}, u32[]{:S(2)}, u32[]{:S(2)}) collective-permute-start(bf16[320,512]{1,0:T(8,128)(2,1)} %bitcast.21), channel_id=1, source_target_pairs={{0,3},{1,0},{2,1},{3,2},{4,7},{5,4},{6,5},{7,6},{8,11},{9,8},{10,9... | collective-permute-start | bytes 983048 | tf_op jit(solution)/shard_map/ppermute | solution.py:287
  6.1 19.9 %collective-permute-start.1 = (bf16[320,512]{1,0:T(8,128)(2,1)}, bf16[320,512]{1,0:T(8,128)(2,1)S(1)}, u32[]{:S(2)}, u32[]{:S(2)}) collective-permute-start(bf16[320,512]{1,0:T(8,128)(2,1)} %bitcast.22), channel_id=1, source_target_pairs={{0,2},{1,3},{2,0},{3,1},{4,6},{5,7},{6,4},{7,5},{8,10},{9,11},{10,... | collective-permute-start | bytes 983048 | tf_op jit(solution)/shard_map/ppermute | solution.py:287
  8.4 17.7 %collective-permute-start = (bf16[320,512]{1,0:T(8,128)(2,1)}, bf16[320,512]{1,0:T(8,128)(2,1)S(1)}, u32[]{:S(2)}, u32[]{:S(2)}) collective-permute-start(bf16[320,512]{1,0:T(8,128)(2,1)} %bitcast.23), channel_id=1, source_target_pairs={{0,1},{1,2},{2,3},{3,0},{4,5},{5,6},{6,7},{7,4},{8,9},{9,10},{10,1... | collective-permute-start | bytes 983048 | tf_op jit(solution)/shard_map/ppermute | solution.py:287
  12.3 12.5 %all-to-all-start = ((bf16[16,4,320]{2,1,0:T(4,128)(2,1)}), bf16[16,4,320]{2,1,0:T(4,128)(2,1)S(1)}, u32[]{:S(2)}, u32[]{:S(2)}) async-start(bf16[16,4,320]{2,1,0:T(4,128)(2,1)} %broadcast_in_dim.2), calls=%async_computation | async-start | bytes 98304 | tf_op jit(solution)/shard_map/all_to_all | solution.py:266
  20.8 0.7 copy-start.5
  26.0 18.7 %copy-start.4 = (bf16[16,1280]{1,0:T(8,128)(2,1)}, bf16[16,1280]{1,0:T(8,128)(2,1)S(1)}, u32[]{:S(2)}) copy-start(bf16[16,1280]{1,0:T(8,128)(2,1)S(1)} %get-tuple-element.26.hd_ref) | copy-start | bytes 122884
  26.0 18.7 %copy-start.7 = (bf16[320,512]{1,0:T(8,128)(2,1)}, bf16[320,512]{1,0:T(8,128)(2,1)S(1)}, u32[]{:S(2)}) copy-start(bf16[320,512]{1,0:T(8,128)(2,1)S(1)} %collective-permute-done.2.x3_hbm) | copy-start | bytes 983044
  26.0 18.7 %copy-start.8 = (bf16[320,512]{1,0:T(8,128)(2,1)}, bf16[320,512]{1,0:T(8,128)(2,1)S(1)}, u32[]{:S(2)}) copy-start(bf16[320,512]{1,0:T(8,128)(2,1)S(1)} %collective-permute-done.1.x2_hbm) | copy-start | bytes 983044
  26.0 18.7 %copy-start.9 = (bf16[320,512]{1,0:T(8,128)(2,1)}, bf16[320,512]{1,0:T(8,128)(2,1)S(1)}, u32[]{:S(2)}) copy-start(bf16[320,512]{1,0:T(8,128)(2,1)S(1)} %collective-permute-done.x1_hbm) | copy-start | bytes 983044
  26.1 30.0 %all-to-all-start.1 = ((bf16[16,40,128]{2,1,0:T(8,128)(2,1)}), bf16[16,40,128]{2,1,0:T(8,128)(2,1)S(1)}, u32[]{:S(2)}, u32[]{:S(2)}) async-start(bf16[16,40,128]{2,1,0:T(8,128)(2,1)} %get-tuple-element.36), calls=%async_computation.1 | async-start | bytes 327680 | tf_op jit(solution)/shard_map/all_to_all | solution.py:329
  44.7 16.5 %copy-start.1 = (bf16[640,320]{0,1:T(8,128)(2,1)S(1)}, bf16[640,320]{0,1:T(8,128)(2,1)}, u32[]{:S(2)}) copy-start(bf16[640,320]{0,1:T(8,128)(2,1)} %param.19) | copy-start | bytes 1228804
  44.7 16.4 %copy-start.2 = (bf16[640,320]{0,1:T(8,128)(2,1)S(1)}, bf16[640,320]{0,1:T(8,128)(2,1)}, u32[]{:S(2)}) copy-start(bf16[640,320]{0,1:T(8,128)(2,1)} %param.20) | copy-start | bytes 1228804
  56.0 37.8 %copy-start.10 = (bf16[320,512]{1,0:T(8,128)(2,1)S(1)}, bf16[320,512]{1,0:T(8,128)(2,1)}, u32[]{:S(2)}) copy-start(bf16[320,512]{1,0:T(8,128)(2,1)} %get-tuple-element.34) | copy-start | bytes 983044
  56.0 44.3 %copy-start = (bf16[320,1280]{1,0:T(8,128)(2,1)S(1)}, bf16[320,1280]{1,0:T(8,128)(2,1)}, u32[]{:S(2)}) copy-start(bf16[320,1280]{1,0:T(8,128)(2,1)} %w_ref.1) | copy-start | bytes 2457604
  56.0 44.3 %copy-start.3 = (bf16[2,16,320]{2,1,0:T(8,128)(2,1)S(1)}, bf16[2,16,320]{2,1,0:T(8,128)(2,1)}, u32[]{:S(2)}) copy-start(bf16[2,16,320]{2,1,0:T(8,128)(2,1)} %get-tuple-element.41.kv_ref) | copy-start | bytes 61444
  61.2 48.8 %copy-start.6 = (f32[320,512]{1,0:T(8,128)S(1)}, f32[320,512]{1,0:T(8,128)}, u32[]{:S(2)}) copy-start(f32[320,512]{1,0:T(8,128)} %get-tuple-element.31) | copy-start | bytes 1966084
  79.2 21.1 %all-to-all-start.3 = ((f32[16,4,384]{2,1,0:T(4,128)}), f32[16,4,384]{2,1,0:T(4,128)S(1)}, u32[]{:S(2)}, u32[]{:S(2)}) async-start(f32[16,4,384]{2,1,0:T(4,128)} %shard_map.126), calls=%async_computation.3 | async-start | bytes 196608 | tf_op jit(solution)/shard_map/all_to_all | solution.py:353
  88.4 16.5 %collective-permute-start.3 = (bf16[320,512]{1,0:T(8,128)(2,1)}, bf16[320,512]{1,0:T(8,128)(2,1)S(1)}, u32[]{:S(2)}, u32[]{:S(2)}) collective-permute-start(bf16[320,512]{1,0:T(8,128)(2,1)} %get-tuple-element.32), channel_id=1, source_target_pairs={{0,1},{1,2},{2,3},{3,0},{4,5},{5,6},{6,7},{7,4},{8,9},{9,10},{10,1... | collective-permute-start | bytes 983048 | tf_op jit(solution)/shard_map/ppermute | solution.py:287
  90.4 15.3 %collective-permute-start.4 = (bf16[320,512]{1,0:T(8,128)(2,1)}, bf16[320,512]{1,0:T(8,128)(2,1)S(1)}, u32[]{:S(2)}, u32[]{:S(2)}) collective-permute-start(bf16[320,512]{1,0:T(8,128)(2,1)} %get-tuple-element.33), channel_id=1, source_target_pairs={{0,2},{1,3},{2,0},{3,1},{4,6},{5,7},{6,4},{7,5},{8,10},{9,11},{10,... | collective-permute-start | bytes 983048 | tf_op jit(solution)/shard_map/ppermute | solution.py:287
  93.8 16.2 %collective-permute-start.5 = (bf16[320,512]{1,0:T(8,128)(2,1)S(1)}, bf16[320,512]{1,0:T(8,128)(2,1)S(1)}, u32[]{:S(2)}, u32[]{:S(2)}) collective-permute-start(bf16[320,512]{1,0:T(8,128)(2,1)S(1)} %copy-done.10), channel_id=1, source_target_pairs={{0,3},{1,0},{2,1},{3,2},{4,7},{5,4},{6,5},{7,6},{8,11},{9,8},{10,9... | collective-permute-start | bytes 983048 | tf_op jit(solution)/shard_map/ppermute | solution.py:287
  101.6 9.2 %all-to-all-start.4 = ((f32[4,4,320]{2,1,0:T(4,128)}), f32[4,4,320]{2,1,0:T(4,128)S(1)}, u32[]{:S(2)}, u32[]{:S(2)}) async-start(f32[4,4,320]{2,1,0:T(4,128)} %shard_map.127), calls=%async_computation.4 | async-start | bytes 49152 | tf_op jit(solution)/shard_map/all_to_all | solution.py:362

commit v6 on v5

--- a/solution.py
+++ b/solution.py
@@ -176,7 +176,7 @@
 def prefill_kernel(
     len_ref, tp_ref, gain_ref, hd_ref, x0_hbm, x1_hbm, x2_hbm, x3_hbm, w_hbm, kc_hbm, vc_hbm, wo_hbm,
     o0_ref, o1_ref, o2_ref, o3_ref, kv_ref,
-    x_ref, w_ref, kc_ref, vc_ref, wo_ref, wo4_s, q_s, k_s, v_s, a_s, sems,
+    x_ref, w_ref, kc_ref, vc_ref, wo_ref, wo4_s, gain_s, q_s, k_s, v_s, a_s, sems,
 ):
     tokens, cached = x_ref.shape[1], kc_ref.shape[1]
     block = 256
@@ -188,28 +188,34 @@
         return source.at[:, cols], x_ref.at[at, cols]
 
     sources = (x0_hbm, x1_hbm, x2_hbm, x3_hbm)
-    plan = [piece(source, shift, 0) for shift, source in enumerate(sources)] + [(w_hbm, w_ref)]
+    plan = [piece(source, shift, 0) for shift, source in enumerate(sources)]
+    plan += [(w_hbm.at[part], w_ref.at[part]) for part in range(3)]
     plan += [piece(source, shift, 1) for shift, source in enumerate(sources)]
-    plan += [(wo_hbm, wo_ref), (kc_hbm, kc_ref), (vc_hbm, vc_ref)]
+    plan += [(kc_hbm, kc_ref), (vc_hbm, vc_ref), (wo_hbm, wo_ref)]
     fetches = [
         pltpu.make_async_copy(source, target, sems.at[n]) for n, (source, target) in enumerate(plan)
     ]
     for fetch in fetches:
         fetch.start()
+    lines = gain_ref.shape[0]
+    gain_s[...] = jnp.zeros_like(gain_s)
+    gain_s[0:lines] = gain_ref[...]
+    gain_t = jnp.transpose(gain_s[...])
+    gain = jnp.concatenate([gain_t[:, n : n + 1] for n in range(lines)], axis=0)
     for b in range(tokens // block):
         cols = slice(b * block, (b + 1) * block)
-        for fetch in fetches[5 * b : 5 * b + 4]:
+        for fetch in fetches[7 * b : 7 * b + 4]:
             fetch.wait()
         x = x_ref[:, cols].astype(F32)
         mean_square = jnp.sum(x * x, axis=0, keepdims=True) * (1.0 / x.shape[0])
-        hidden = (x * lax.rsqrt(mean_square + EPSILON) * gain_ref[...]).astype(BF16)
-        if b == 0:
-            fetches[4].wait()
-            for part in (1, 2):
-                kv_ref[part - 1] = dot(hd_ref[...], w_ref[part], ((1,), (1,))).astype(BF16)
+        hidden = (x * lax.rsqrt(mean_square + EPSILON) * gain).astype(BF16)
         for part, held in enumerate((q_s, k_s, v_s)):
+            if b == 0:
+                fetches[4 + part].wait()
             held[:, cols] = dot(w_ref[part], hidden, ((1,), (0,))).astype(BF16)
-    for fetch in fetches[9:]:
+    for part in (1, 2):
+        kv_ref[part - 1] = dot(hd_ref[...], w_ref[part], ((1,), (1,))).astype(BF16)
+    for fetch in fetches[11:]:
         fetch.wait()
     for t in range(NT):
         wo4_s[t] = wo_ref[:, t * WIDTH : (t + 1) * WIDTH]
@@ -300,17 +306,26 @@
         flops=2 * 16 * full * WIDTH,
         moved=2 * full * WIDTH,
     )
-    gain_column = norm_gain.reshape(full, 1)
-    *x_blocks, gain_column, bounds, order, queries = lax.optimization_barrier(
-        (*x_blocks, gain_column, bounds, order, queries)
-    )
+    bounds, order, queries = lax.optimization_barrier((bounds, order, queries))
+    queries = lax.all_to_all(queries, "z", 0, 0, tiled=True)
+    queries = lax.all_gather(queries, "c", axis=0, tiled=True)
+    partial = call(
+        dec_attention_kernel,
+        shape((requests, LANES), BF16),
+        (),
+        (queries, bounds, order, dec_keys.T, dec_values.T),
+        scratch=[pltpu.VMEM((requests, WIDTH), BF16)],
+        flops=4 * requests * pool * WIDTH,
+        moved=4 * pool * WIDTH,
+    )
+    *x_blocks, partial = lax.optimization_barrier((*x_blocks, partial))
     term_blocks = call(
         prefill_kernel,
         (shape((WIDTH, tokens), F32),)
         + (shape((WIDTH, tokens), BF16),) * 3
         + (shape((2, 16, WIDTH), BF16),),
         (pre_lens, tp),
-        (gain_column, hidden),
+        (norm_gain.reshape(full // 128, 128), hidden),
         (*x_blocks, w_t, pre_keys.T, pre_values.T, w_out),
         scratch=[
             pltpu.VMEM((full, tokens), BF16),
@@ -319,29 +334,19 @@
             pltpu.VMEM((WIDTH, pre_keys.shape[0]), BF16),
             pltpu.VMEM((WIDTH, full), BF16),
             pltpu.VMEM((NT, WIDTH, WIDTH), BF16),
+            pltpu.VMEM((128, 128), F32),
         ]
         + [pltpu.VMEM((WIDTH, tokens), BF16)] * 4
-        + [pltpu.SemaphoreType.DMA((12,))],
+        + [pltpu.SemaphoreType.DMA((14,))],
         flops=8 * tokens * full * WIDTH + 4 * tokens * 896 * WIDTH,
         moved=8 * full * WIDTH,
         limit=VMEM_ALL,
     )
-    queries = lax.all_to_all(queries, "z", 0, 0, tiled=True)
+    partial = lax.all_to_all(partial.reshape(NX * NC, NZ * 4, LANES), ("x", "c"), 0, 0, tiled=True)
     *term_blocks, own_kv = term_blocks
-    own_kv, queries = lax.optimization_barrier((own_kv, queries))
-    queries = lax.all_gather(queries, "c", axis=0, tiled=True)
+    own_kv, partial = lax.optimization_barrier((own_kv, partial))
     arrived = [turned(block, shift) for shift, block in enumerate(term_blocks) if shift > 0]
     pre_out = term_blocks[0] + sum(block.astype(F32) for block in arrived)
-    partial = call(
-        dec_attention_kernel,
-        shape((requests, LANES), BF16),
-        (),
-        (queries, bounds, order, dec_keys.T, dec_values.T),
-        scratch=[pltpu.VMEM((requests, WIDTH), BF16)],
-        flops=4 * requests * pool * WIDTH,
-        moved=4 * pool * WIDTH,
-    )
-    partial = lax.all_to_all(partial.reshape(NX * NC, NZ * 4, LANES), ("x", "c"), 0, 0, tiled=True)
     partial = call(
         dec_merge_kernel,
         shape((NZ, 4, LANES), F32),

time: 112 us -> 110 us (0.982)
  blocking collectives: 17.7 us -> 6.64 us
  waiting for transfers between devices: 11.3 us -> 14.8 us
  starting transfers between devices: 54 us -> 57.1 us
    all_to_all x1 -> x0, blocking collectives: 12.6 us -> none  [body(): lax.all_to_all(partial.reshape(NX * NC, NZ * 4, LANES), ('x', 'c'), 0, 0,...]
    all_to_all x1, waiting for transfers between devices: 0.01 us -> 4.31 us  [body(): queries = lax.all_to_all(queries, 'z', 0, 0, tiled=True)]
    all_to_all x0 -> x1, starting transfers between devices: none -> 3.73 us  [body(): lax.all_to_all(partial.reshape(NX * NC, NZ * 4, LANES), ('x', 'c'), 0, 0,...]
    ppermute x6, starting transfers between devices: 18.7 us -> 16.7 us  [turned(): return lax.ppermute(block, 'tp', [(t, (t + shift) % NT) for t in range(NT)])]
    all_to_all x1, starting transfers between devices: 16.9 us -> 14.9 us  [body(): queries = lax.all_to_all(queries, 'z', 0, 0, tiled=True)]
    all_to_all x1, starting transfers between devices: 5.83 us -> 7.58 us  [spread(): return lax.all_to_all(copies, axes, 0, 0, tiled=True)]
    all_to_all x1, starting transfers between devices: 9.26 us -> 10.9 us  [body(): partial = lax.all_to_all(partial, 'z', 0, 0, tiled=True)]
    all_gather x1, blocking collectives: 5.14 us -> 6.64 us  [body(): queries = lax.all_gather(queries, 'c', axis=0, tiled=True)]
  transfers between devices with their start and end apart: 10 -> 11, of which waited for: 4 -> 5; matrix products, arithmetic and copies ran while one was open for 5% -> 4% of each run, Pallas kernels for 13% -> 17%
where the time goes in v6:
time: 110 us; the launch traced here: 109 us
  starting transfers between devices  57.1 us (52%)
  Pallas kernels  20.6 us (19%)
  waiting for transfers between devices  14.8 us (13%)
  blocking collectives  6.64 us (6%)
  local copies, waits for them, and re-layouts  5.38 us (5%)
  other arithmetic  2.61 us (2%)
  between operations  1.49 us (1%)
    pallas_call x6, Pallas kernels, call(): pl.pallas_call(kernel, out_shape=out_shape, in_specs=[pl.BlockSpec(memory...  20.6 us
    ppermute x6, starting transfers between devices, turned(): return lax.ppermute(block, 'tp', [(t, (t + shift) % NT) for t in range(NT)])  16.7 us
    all_to_all x1, starting transfers between devices, body(): queries = lax.all_to_all(queries, 'z', 0, 0, tiled=True)  14.9 us
    all_to_all x1, starting transfers between devices, body(): partial = lax.all_to_all(partial, 'z', 0, 0, tiled=True)  10.9 us
    all_to_all x1, starting transfers between devices, spread(): return lax.all_to_all(copies, axes, 0, 0, tiled=True)  7.58 us
    all_gather x1, blocking collectives, body(): queries = lax.all_gather(queries, 'c', axis=0, tiled=True)  6.64 us
    all_to_all x1, waiting for transfers between devices, body(): queries = lax.all_to_all(queries, 'z', 0, 0, tiled=True)  4.31 us
    ppermute x6, waiting for transfers between devices, turned(): return lax.ppermute(block, 'tp', [(t, (t + shift) % NT) for t in range(NT)])  4.28 us
  transfers between devices with their start and end apart: 11, of which 5 were waited for; matrix products, arithmetic and copies ran while one was open for 4% of the time, Pallas kernels for 17%

profile of v6, /device:TPU:1, one launch (start us, length us, event | category | flops | bytes accessed | tf_op | source)
XLA Modules:
  0.0 108.6 jit_solution(11872257577341893626)
XLA Ops:
  0.6 0.0 copy-start.6
  0.6 0.0 copy-start.2
  0.7 0.0 copy-start.1
  0.7 1.4 %broadcast_in_dim.2 = bf16[16,4,320]{2,1,0:T(4,128)(2,1)} broadcast(bf16[4,320]{1,0:T(4,128)(2,1)} %param.12), dimensions={1,2} | broadcast | bytes 43520 | tf_op jit(solution)/shard_map/broadcast_in_dim | solution.py:271
  2.1 7.6 %all-to-all-start = ((bf16[16,4,320]{2,1,0:T(4,128)(2,1)}), bf16[16,4,320]{2,1,0:T(4,128)(2,1)S(1)}, u32[]{:S(2)}, u32[]{:S(2)}) async-start(bf16[16,4,320]{2,1,0:T(4,128)(2,1)} %broadcast_in_dim.2), calls=%async_computation | async-start | bytes 98304 | tf_op jit(solution)/shard_map/all_to_all | solution.py:272
  9.7 1.2 %slice_bitcast_fusion.w_ref = bf16[320,1280]{1,0:T(8,128)(2,1)S(1)} fusion(bf16[3,320,1280]{2,1,0:T(8,128)(2,1)} %bitcast.19), kind=kLoop, calls=%fused_computation | loop fusion | bytes 1638400 | tf_op jit(solution)/shard_map/squeeze | solution.py:304
  10.9 0.7 reshape.28.gain_ref
  11.6 0.0 copy-start.5
  11.6 0.7 copy-done.5
  12.3 0.6 shard_map.123
  12.8 3.3 %all-to-all-done.x_ref = bf16[16,4,320]{2,1,0:T(4,128)(2,1)S(1)} async-done(((bf16[16,4,320]{2,1,0:T(4,128)(2,1)}), bf16[16,4,320]{2,1,0:T(4,128)(2,1)S(1)}, u32[]{:S(2)}, u32[]{:S(2)}) %all-to-all-start) | async-done | bytes 40992 | tf_op jit(solution)/shard_map/all_to_all | solution.py:272
  16.2 1.2 %shard_map.122 = (bf16[16,40,128]{2,1,0:T(8,128)(2,1)}, bf16[16,320]{1,0:T(8,128)(2,1)S(1)}, bf16[16,1280]{1,0:T(8,128)(2,1)S(1)}) custom-call(bf16[16,4,320]{2,1,0:T(4,128)(2,1)S(1)} %all-to-all-done.x_ref, f32[1,1280]{1,0:T(1,128)S(1)} %reshape.28.gain_ref, bf16[320,1280]{1,0:T(8,128)(2,1)S(1)} %slice_bitcast_fusion.w_ref), custom_call_target="tpu_custom_call" | custom-call | flops 13107200 | bytes 819200 | tf_op jit(solution)/shard_map/pallas_call | solution.py:253
  17.3 0.0 copy-start.4
  17.4 0.6 copy-done.4
  18.0 14.9 %all-to-all-start.1 = ((bf16[16,40,128]{2,1,0:T(8,128)(2,1)}), bf16[16,40,128]{2,1,0:T(8,128)(2,1)S(1)}, u32[]{:S(2)}, u32[]{:S(2)}) async-start(bf16[16,40,128]{2,1,0:T(8,128)(2,1)} %get-tuple-element.26), calls=%async_computation.1 | async-start | bytes 327680 | tf_op jit(solution)/shard_map/all_to_all | solution.py:310
  32.9 0.0 copy-done.6
  32.9 2.9 %collective-permute-start.2 = (bf16[320,512]{1,0:T(8,128)(2,1)S(1)}, bf16[320,512]{1,0:T(8,128)(2,1)S(1)}, u32[]{:S(2)}, u32[]{:S(2)}) collective-permute-start(bf16[320,512]{1,0:T(8,128)(2,1)S(1)} %bitcast.23), channel_id=1, source_target_pairs={{0,3},{1,0},{2,1},{3,2},{4,7},{5,4},{6,5},{7,6},{8,11},{9,8},{10,9... | collective-permute-start | bytes 983048 | tf_op jit(solution)/shard_map/ppermute | solution.py:293
  35.8 3.0 %collective-permute-start.1 = (bf16[320,512]{1,0:T(8,128)(2,1)S(1)}, bf16[320,512]{1,0:T(8,128)(2,1)S(1)}, u32[]{:S(2)}, u32[]{:S(2)}) collective-permute-start(bf16[320,512]{1,0:T(8,128)(2,1)S(1)} %bitcast.24), channel_id=1, source_target_pairs={{0,2},{1,3},{2,0},{3,1},{4,6},{5,7},{6,4},{7,5},{8,10},{9,11},{10,... | collective-permute-start | bytes 983048 | tf_op jit(solution)/shard_map/ppermute | solution.py:293
  38.8 1.9 %collective-permute-start = (bf16[320,512]{1,0:T(8,128)(2,1)S(1)}, bf16[320,512]{1,0:T(8,128)(2,1)S(1)}, u32[]{:S(2)}, u32[]{:S(2)}) collective-permute-start(bf16[320,512]{1,0:T(8,128)(2,1)S(1)} %bitcast.25), channel_id=1, source_target_pairs={{0,1},{1,2},{2,3},{3,0},{4,5},{5,6},{6,7},{7,4},{8,9},{9,10},{10,1... | collective-permute-start | bytes 983048 | tf_op jit(solution)/shard_map/ppermute | solution.py:293
  40.7 4.3 %all-to-all-done.1 = bf16[16,40,128]{2,1,0:T(8,128)(2,1)S(1)} async-done(((bf16[16,40,128]{2,1,0:T(8,128)(2,1)}), bf16[16,40,128]{2,1,0:T(8,128)(2,1)S(1)}, u32[]{:S(2)}, u32[]{:S(2)}) %all-to-all-start.1) | async-done | bytes 163872 | tf_op jit(solution)/shard_map/all_to_all | solution.py:310
  45.0 6.6 %all_gather.3.qp_ref = bf16[32,40,128]{2,1,0:T(8,128)(2,1)S(1)} all-gather(bf16[16,40,128]{2,1,0:T(8,128)(2,1)S(1)} %all-to-all-done.1), channel_id=1, replica_groups=mesh['x'=4,'z'=16,'c'=2,'tp'=4] {'c'}, dimensions={0}, use_global_device_ids=true | all-gather | bytes 491520 | tf_op jit(solution)/shard_map/all_gather | solution.py:311
  51.7 0.0 copy-done.2
  51.7 0.0 copy-done.1
  51.7 4.8 %shard_map.124 = bf16[512,384]{1,0:T(8,128)(2,1)} custom-call(bf16[32,40,128]{2,1,0:T(8,128)(2,1)S(1)} %all_gather.3.qp_ref, f32[512,2]{1,0:T(8,128)S(1)} %get-tuple-element.27.bounds_ref, bf16[512,512]{1,0:T(8,128)(2,1)S(1)} %get-tuple-element.28.order_ref, bf16[320,640]{1,0:T(8,128)(2,1)S(1)} %bitcast.16, bf16[320,640]{1,0:T(8,128)(2,1)S(1)} %bitcast.17), custom_call_target="tpu_custom_call" | custom-call | flops 419430400 | bytes 819200 | tf_op jit(solution)/shard_map/pallas_call | solution.py:253
  56.5 0.0 collective-permute-done.2.x3_hbm
  56.5 0.0 copy-start.7
  56.5 0.0 collective-permute-done.1.x2_hbm
  56.5 0.0 copy-start.8
  56.5 0.0 collective-permute-done.x1_hbm
  56.5 0.0 copy-start.9
  56.5 3.7 %all-to-all-start.2 = ((bf16[8,64,384]{2,1,0:T(8,128)(2,1)}), bf16[8,64,384]{2,1,0:T(8,128)(2,1)S(1)}, u32[]{:S(2)}, u32[]{:S(2)}) async-start(bf16[8,64,384]{2,1,0:T(8,128)(2,1)} %bitcast.13), calls=%async_computation.2 | async-start | bytes 786432 | tf_op jit(solution)/shard_map/all_to_all | solution.py:345
  60.9 0.0 copy-done.7
  60.9 0.0 copy-done.8
  60.9 0.0 copy-done.9
  60.9 0.0 copy-start
  61.0 11.3 %shard_map.125 = (f32[320,512]{1,0:T(8,128)}, bf16[320,512]{1,0:T(8,128)(2,1)}, bf16[320,512]{1,0:T(8,128)(2,1)}, bf16[320,512]{1,0:T(8,128)(2,1)}, bf16[2,16,320]{2,1,0:T(8,128)(2,1)}) custom-call(s32[1]{0:T(128)S(6)} %copy.13.len_ref, s32[1]{0:T(128)} %bitcast.tp_ref, f32[10,128]{1,0:T(8,128)} %bitcast.21, bf16[16,1280]{1,0:T(8,128)(2,1)} %copy-done.4, ...), custom_call_target="tpu_custom_call" | custom-call | flops 2264924160 | bytes 3276800 | tf_op jit(solution)/shard_map/pallas_call | solution.py:253
  72.3 0.0 all-to-all-done.2.in_ref
  72.3 1.4 %shard_map.126 = f32[16,4,384]{2,1,0:T(4,128)} custom-call(bf16[8,64,384]{2,1,0:T(8,128)(2,1)S(1)} %all-to-all-done.2.in_ref), custom_call_target="tpu_custom_call" | custom-call | flops 196608 | bytes 786432 | tf_op jit(solution)/shard_map/pallas_call | solution.py:253
  73.6 10.9 %all-to-all-start.3 = ((f32[16,4,384]{2,1,0:T(4,128)}), f32[16,4,384]{2,1,0:T(4,128)S(1)}, u32[]{:S(2)}, u32[]{:S(2)}) async-start(f32[16,4,384]{2,1,0:T(4,128)} %shard_map.126), calls=%async_computation.3 | async-start | bytes 196608 | tf_op jit(solution)/shard_map/all_to_all | solution.py:358
  84.5 1.9 %collective-permute-start.3 = (bf16[320,512]{1,0:T(8,128)(2,1)}, bf16[320,512]{1,0:T(8,128)(2,1)S(1)}, u32[]{:S(2)}, u32[]{:S(2)}) collective-permute-start(bf16[320,512]{1,0:T(8,128)(2,1)} %get-tuple-element.34), channel_id=1, source_target_pairs={{0,1},{1,2},{2,3},{3,0},{4,5},{5,6},{6,7},{7,4},{8,9},{9,10},{10,1... | collective-permute-start | bytes 983048 | tf_op jit(solution)/shard_map/ppermute | solution.py:293
  86.5 3.4 %collective-permute-start.4 = (bf16[320,512]{1,0:T(8,128)(2,1)}, bf16[320,512]{1,0:T(8,128)(2,1)S(1)}, u32[]{:S(2)}, u32[]{:S(2)}) collective-permute-start(bf16[320,512]{1,0:T(8,128)(2,1)} %get-tuple-element.35), channel_id=1, source_target_pairs={{0,2},{1,3},{2,0},{3,1},{4,6},{5,7},{6,4},{7,5},{8,10},{9,11},{10,... | collective-permute-start | bytes 983048 | tf_op jit(solution)/shard_map/ppermute | solution.py:293
  89.8 3.6 %collective-permute-start.5 = (bf16[320,512]{1,0:T(8,128)(2,1)}, bf16[320,512]{1,0:T(8,128)(2,1)S(1)}, u32[]{:S(2)}, u32[]{:S(2)}) collective-permute-start(bf16[320,512]{1,0:T(8,128)(2,1)} %get-tuple-element.36), channel_id=1, source_target_pairs={{0,3},{1,0},{2,1},{3,2},{4,7},{5,4},{6,5},{7,6},{8,11},{9,8},{10,9... | collective-permute-start | bytes 983048 | tf_op jit(solution)/shard_map/ppermute | solution.py:293
  93.4 2.9 %all-to-all-done.3.in_ref = f32[16,4,384]{2,1,0:T(4,128)S(1)} async-done(((f32[16,4,384]{2,1,0:T(4,128)}), f32[16,4,384]{2,1,0:T(4,128)S(1)}, u32[]{:S(2)}, u32[]{:S(2)}) %all-to-all-start.3) | async-done | bytes 98336 | tf_op jit(solution)/shard_map/all_to_all | solution.py:358
  96.4 0.0 copy-done
  96.4 0.0 copy-start.3
  96.4 0.7 copy-done.3
  97.1 1.4 %shard_map.127 = f32[4,4,320]{2,1,0:T(4,128)} custom-call(s32[1]{0:T(128)} %bitcast.12.own_ref, f32[16,4,384]{2,1,0:T(4,128)S(1)} %all-to-all-done.3.in_ref, bf16[16,320]{1,0:T(8,128)(2,1)S(1)} %get-tuple-element.40.q_ref, bf16[2,16,320]{2,1,0:T(8,128)(2,1)S(1)} %copy-done.3, bf16[320,1280]{1,0:T(8,128)(2,1)S(1)} %copy-done), custom_call_target="tpu_custom_call" | custom-call | flops 6553600 | bytes 819200 | tf_op jit(solution)/shard_map/pallas_call | solution.py:253
  98.5 3.3 %all-to-all-start.4 = ((f32[4,4,320]{2,1,0:T(4,128)}), f32[4,4,320]{2,1,0:T(4,128)S(1)}, u32[]{:S(2)}, u32[]{:S(2)}) async-start(f32[4,4,320]{2,1,0:T(4,128)} %shard_map.127), calls=%async_computation.4 | async-start | bytes 49152 | tf_op jit(solution)/shard_map/all_to_all | solution.py:367
  101.7 1.8 %collective-permute-done.3 = bf16[320,512]{1,0:T(8,128)(2,1)S(1)} collective-permute-done((bf16[320,512]{1,0:T(8,128)(2,1)}, bf16[320,512]{1,0:T(8,128)(2,1)S(1)}, u32[]{:S(2)}, u32[]{:S(2)}) %collective-permute-start.3) | collective-permute-done | bytes 327712 | tf_op jit(solution)/shard_map/ppermute | solution.py:293
  103.6 0.0 collective-permute-done.4
  103.6 2.4 %collective-permute-done.5 = bf16[320,512]{1,0:T(8,128)(2,1)S(1)} collective-permute-done((bf16[320,512]{1,0:T(8,128)(2,1)}, bf16[320,512]{1,0:T(8,128)(2,1)S(1)}, u32[]{:S(2)}, u32[]{:S(2)}) %collective-permute-start.5) | collective-permute-done | bytes 327712 | tf_op jit(solution)/shard_map/ppermute | solution.py:293
  106.0 2.0 %fusion = bf16[512,320]{0,1:T(8,128)(2,1)} fusion(f32[320,512]{1,0:T(8,128)} %get-tuple-element.33, bf16[320,512]{1,0:T(8,128)(2,1)S(1)} %collective-permute-done.5, bf16[320,512]{1,0:T(8,128)(2,1)S(1)} %collective-permute-done.4, bf16[320,512]{1,0:T(8,128)(2,1)S(1)} %collective-permute-done.3), kind=kLoop, calls=%fused_computation.2 | loop fusion | flops 1146880 | bytes 1966080 | tf_op jit(solution)/shard_map/transpose | solution.py:369
  108.0 0.0 all-to-all-done.4
  108.0 0.6 reduce_sum.9
Async XLA Ops:
  0.6 32.3 %copy-start.6 = (bf16[512,320]{0,1:T(8,128)(2,1)S(1)}, bf16[512,320]{0,1:T(8,128)(2,1)}, u32[]{:S(2)}) copy-start(bf16[512,320]{0,1:T(8,128)(2,1)} %param.11) | copy-start | bytes 983044
  0.6 51.0 %copy-start.2 = (bf16[640,320]{0,1:T(8,128)(2,1)S(1)}, bf16[640,320]{0,1:T(8,128)(2,1)}, u32[]{:S(2)}) copy-start(bf16[640,320]{0,1:T(8,128)(2,1)} %param.20) | copy-start | bytes 1228804
  0.7 51.0 %copy-start.1 = (bf16[640,320]{0,1:T(8,128)(2,1)S(1)}, bf16[640,320]{0,1:T(8,128)(2,1)}, u32[]{:S(2)}) copy-start(bf16[640,320]{0,1:T(8,128)(2,1)} %param.19) | copy-start | bytes 1228804
  2.1 14.1 %all-to-all-start = ((bf16[16,4,320]{2,1,0:T(4,128)(2,1)}), bf16[16,4,320]{2,1,0:T(4,128)(2,1)S(1)}, u32[]{:S(2)}, u32[]{:S(2)}) async-start(bf16[16,4,320]{2,1,0:T(4,128)(2,1)} %broadcast_in_dim.2), calls=%async_computation | async-start | bytes 98304 | tf_op jit(solution)/shard_map/all_to_all | solution.py:272
  11.6 0.7 copy-start.5
  17.3 0.6 copy-start.4
  18.0 27.1 %all-to-all-start.1 = ((bf16[16,40,128]{2,1,0:T(8,128)(2,1)}), bf16[16,40,128]{2,1,0:T(8,128)(2,1)S(1)}, u32[]{:S(2)}, u32[]{:S(2)}) async-start(bf16[16,40,128]{2,1,0:T(8,128)(2,1)} %get-tuple-element.26), calls=%async_computation.1 | async-start | bytes 327680 | tf_op jit(solution)/shard_map/all_to_all | solution.py:310
  32.9 23.6 %collective-permute-start.2 = (bf16[320,512]{1,0:T(8,128)(2,1)S(1)}, bf16[320,512]{1,0:T(8,128)(2,1)S(1)}, u32[]{:S(2)}, u32[]{:S(2)}) collective-permute-start(bf16[320,512]{1,0:T(8,128)(2,1)S(1)} %bitcast.23), channel_id=1, source_target_pairs={{0,3},{1,0},{2,1},{3,2},{4,7},{5,4},{6,5},{7,6},{8,11},{9,8},{10,9... | collective-permute-start | bytes 983048 | tf_op jit(solution)/shard_map/ppermute | solution.py:293
  35.8 20.7 %collective-permute-start.1 = (bf16[320,512]{1,0:T(8,128)(2,1)S(1)}, bf16[320,512]{1,0:T(8,128)(2,1)S(1)}, u32[]{:S(2)}, u32[]{:S(2)}) collective-permute-start(bf16[320,512]{1,0:T(8,128)(2,1)S(1)} %bitcast.24), channel_id=1, source_target_pairs={{0,2},{1,3},{2,0},{3,1},{4,6},{5,7},{6,4},{7,5},{8,10},{9,11},{10,... | collective-permute-start | bytes 983048 | tf_op jit(solution)/shard_map/ppermute | solution.py:293
  38.8 17.7 %collective-permute-start = (bf16[320,512]{1,0:T(8,128)(2,1)S(1)}, bf16[320,512]{1,0:T(8,128)(2,1)S(1)}, u32[]{:S(2)}, u32[]{:S(2)}) collective-permute-start(bf16[320,512]{1,0:T(8,128)(2,1)S(1)} %bitcast.25), channel_id=1, source_target_pairs={{0,1},{1,2},{2,3},{3,0},{4,5},{5,6},{6,7},{7,4},{8,9},{9,10},{10,1... | collective-permute-start | bytes 983048 | tf_op jit(solution)/shard_map/ppermute | solution.py:293
  56.5 4.4 %copy-start.7 = (bf16[320,512]{1,0:T(8,128)(2,1)}, bf16[320,512]{1,0:T(8,128)(2,1)S(1)}, u32[]{:S(2)}) copy-start(bf16[320,512]{1,0:T(8,128)(2,1)S(1)} %collective-permute-done.2.x3_hbm) | copy-start | bytes 983044
  56.5 4.4 %copy-start.8 = (bf16[320,512]{1,0:T(8,128)(2,1)}, bf16[320,512]{1,0:T(8,128)(2,1)S(1)}, u32[]{:S(2)}) copy-start(bf16[320,512]{1,0:T(8,128)(2,1)S(1)} %collective-permute-done.1.x2_hbm) | copy-start | bytes 983044
  56.5 4.4 %copy-start.9 = (bf16[320,512]{1,0:T(8,128)(2,1)}, bf16[320,512]{1,0:T(8,128)(2,1)S(1)}, u32[]{:S(2)}) copy-start(bf16[320,512]{1,0:T(8,128)(2,1)S(1)} %collective-permute-done.x1_hbm) | copy-start | bytes 983044
  56.5 15.7 %all-to-all-start.2 = ((bf16[8,64,384]{2,1,0:T(8,128)(2,1)}), bf16[8,64,384]{2,1,0:T(8,128)(2,1)S(1)}, u32[]{:S(2)}, u32[]{:S(2)}) async-start(bf16[8,64,384]{2,1,0:T(8,128)(2,1)} %bitcast.13), calls=%async_computation.2 | async-start | bytes 786432 | tf_op jit(solution)/shard_map/all_to_all | solution.py:345
  60.9 35.4 %copy-start = (bf16[320,1280]{1,0:T(8,128)(2,1)S(1)}, bf16[320,1280]{1,0:T(8,128)(2,1)}, u32[]{:S(2)}) copy-start(bf16[320,1280]{1,0:T(8,128)(2,1)} %w_ref.1) | copy-start | bytes 2457604
  73.6 22.7 %all-to-all-start.3 = ((f32[16,4,384]{2,1,0:T(4,128)}), f32[16,4,384]{2,1,0:T(4,128)S(1)}, u32[]{:S(2)}, u32[]{:S(2)}) async-start(f32[16,4,384]{2,1,0:T(4,128)} %shard_map.126), calls=%async_computation.3 | async-start | bytes 196608 | tf_op jit(solution)/shard_map/all_to_all | solution.py:358
  84.5 19.0 %collective-permute-start.3 = (bf16[320,512]{1,0:T(8,128)(2,1)}, bf16[320,512]{1,0:T(8,128)(2,1)S(1)}, u32[]{:S(2)}, u32[]{:S(2)}) collective-permute-start(bf16[320,512]{1,0:T(8,128)(2,1)} %get-tuple-element.34), channel_id=1, source_target_pairs={{0,1},{1,2},{2,3},{3,0},{4,5},{5,6},{6,7},{7,4},{8,9},{9,10},{10,1... | collective-permute-start | bytes 983048 | tf_op jit(solution)/shard_map/ppermute | solution.py:293
  86.5 17.1 %collective-permute-start.4 = (bf16[320,512]{1,0:T(8,128)(2,1)}, bf16[320,512]{1,0:T(8,128)(2,1)S(1)}, u32[]{:S(2)}, u32[]{:S(2)}) collective-permute-start(bf16[320,512]{1,0:T(8,128)(2,1)} %get-tuple-element.35), channel_id=1, source_target_pairs={{0,2},{1,3},{2,0},{3,1},{4,6},{5,7},{6,4},{7,5},{8,10},{9,11},{10,... | collective-permute-start | bytes 983048 | tf_op jit(solution)/shard_map/ppermute | solution.py:293
  89.8 16.2 %collective-permute-start.5 = (bf16[320,512]{1,0:T(8,128)(2,1)}, bf16[320,512]{1,0:T(8,128)(2,1)S(1)}, u32[]{:S(2)}, u32[]{:S(2)}) collective-permute-start(bf16[320,512]{1,0:T(8,128)(2,1)} %get-tuple-element.36), channel_id=1, source_target_pairs={{0,3},{1,0},{2,1},{3,2},{4,7},{5,4},{6,5},{7,6},{8,11},{9,8},{10,9... | collective-permute-start | bytes 983048 | tf_op jit(solution)/shard_map/ppermute | solution.py:293
  96.4 0.7 copy-start.3
  98.5 9.6 %all-to-all-start.4 = ((f32[4,4,320]{2,1,0:T(4,128)}), f32[4,4,320]{2,1,0:T(4,128)S(1)}, u32[]{:S(2)}, u32[]{:S(2)}) async-start(f32[4,4,320]{2,1,0:T(4,128)} %shard_map.127), calls=%async_computation.4 | async-start | bytes 49152 | tf_op jit(solution)/shard_map/all_to_all | solution.py:367

commit v7 on v6

--- a/solution.py
+++ b/solution.py
@@ -174,23 +174,21 @@
 
 
 def prefill_kernel(
-    len_ref, tp_ref, gain_ref, hd_ref, x0_hbm, x1_hbm, x2_hbm, x3_hbm, w_hbm, kc_hbm, vc_hbm, wo_hbm,
-    o0_ref, o1_ref, o2_ref, o3_ref, kv_ref,
-    x_ref, w_ref, kc_ref, vc_ref, wo_ref, wo4_s, gain_s, q_s, k_s, v_s, a_s, sems,
+    len_ref, tp_ref, gain_ref, x0_hbm, x1_hbm, x2_hbm, x3_hbm, w_hbm, kc_hbm, vc_hbm, wo_hbm,
+    o0_hbm, o1_hbm, o2_hbm, o3_hbm,
+    x_ref, w_ref, kc_ref, vc_ref, wo_ref, wo4_s, gain_s, q_s, k_s, v_s, a_s, own_s, out_s, sems, out_sems,
 ):
     tokens, cached = x_ref.shape[1], kc_ref.shape[1]
     block = 256
     me = tp_ref[0]
 
-    def piece(source, shift, b):
-        at = pl.ds(pl.multiple_of(((me - shift + NT) & (NT - 1)) * WIDTH, WIDTH), WIDTH)
-        cols = slice(b * block, (b + 1) * block)
-        return source.at[:, cols], x_ref.at[at, cols]
+    def place(shift):
+        at = pl.multiple_of(((me - shift + NT) & (NT - 1)) * WIDTH, WIDTH)
+        return x_ref.at[pl.ds(at, WIDTH), :]
 
     sources = (x0_hbm, x1_hbm, x2_hbm, x3_hbm)
-    plan = [piece(source, shift, 0) for shift, source in enumerate(sources)]
+    plan = [(source, place(shift)) for shift, source in enumerate(sources)]
     plan += [(w_hbm.at[part], w_ref.at[part]) for part in range(3)]
-    plan += [piece(source, shift, 1) for shift, source in enumerate(sources)]
     plan += [(kc_hbm, kc_ref), (vc_hbm, vc_ref), (wo_hbm, wo_ref)]
     fetches = [
         pltpu.make_async_copy(source, target, sems.at[n]) for n, (source, target) in enumerate(plan)
@@ -204,8 +202,9 @@
     gain = jnp.concatenate([gain_t[:, n : n + 1] for n in range(lines)], axis=0)
     for b in range(tokens // block):
         cols = slice(b * block, (b + 1) * block)
-        for fetch in fetches[7 * b : 7 * b + 4]:
-            fetch.wait()
+        if b == 0:
+            for fetch in fetches[0:4]:
+                fetch.wait()
         x = x_ref[:, cols].astype(F32)
         mean_square = jnp.sum(x * x, axis=0, keepdims=True) * (1.0 / x.shape[0])
         hidden = (x * lax.rsqrt(mean_square + EPSILON) * gain).astype(BF16)
@@ -213,9 +212,7 @@
             if b == 0:
                 fetches[4 + part].wait()
             held[:, cols] = dot(w_ref[part], hidden, ((1,), (0,))).astype(BF16)
-    for part in (1, 2):
-        kv_ref[part - 1] = dot(hd_ref[...], w_ref[part], ((1,), (1,))).astype(BF16)
-    for fetch in fetches[11:]:
+    for fetch in fetches[7:]:
         fetch.wait()
     for t in range(NT):
         wo4_s[t] = wo_ref[:, t * WIDTH : (t + 1) * WIDTH]
@@ -242,13 +239,29 @@
                 v_s[feats, 0:seen], w_new.astype(BF16), ((1,), (0,))
             )
             a_s[feats, cols] = (mixed / total).astype(BF16)
-    for shift, out_ref in enumerate((o0_ref, o1_ref, o2_ref, o3_ref)):
+    sends = []
+    for shift, target in ((1, o1_hbm), (2, o2_hbm), (3, o3_hbm), (0, o0_hbm)):
         terms = dot(wo4_s[(me + shift) & (NT - 1)], a_s[...], ((0,), (0,)))
-        out_ref[...] = terms.astype(out_ref.dtype)
+        held = out_s.at[shift - 1] if shift else own_s
+        held[...] = terms.astype(target.dtype)
+        sends.append(pltpu.make_async_copy(held, target, out_sems.at[shift]))
+        sends[-1].start()
+    for send in sends:
+        send.wait()
+
+
+def dec_kv_kernel(hd_ref, w_hbm, kv_ref, w_ref, sems):
+    fetches = [pltpu.make_async_copy(w_hbm.at[n + 1], w_ref.at[n], sems.at[n]) for n in range(2)]
+    for fetch in fetches:
+        fetch.start()
+    for n, fetch in enumerate(fetches):
+        fetch.wait()
+        kv_ref[n] = dot(hd_ref[...], w_ref[n], ((1,), (1,))).astype(BF16)
 
 
 def call(
-    kernel, out_shape, scalars, arrays, stored=(), scratch=(), flops=0, moved=0, limit=VMEM_LIMIT
+    kernel, out_shape, scalars, arrays, stored=(), scratch=(), flops=0, moved=0, limit=VMEM_LIMIT,
+    out_space=pltpu.VMEM,
 ):
     return pl.pallas_call(
         kernel,
@@ -256,7 +269,7 @@
         in_specs=[pl.BlockSpec(memory_space=pltpu.SMEM)] * len(scalars)
         + [pl.BlockSpec(memory_space=pltpu.VMEM)] * len(arrays)
         + [pl.BlockSpec(memory_space=pltpu.HBM)] * len(stored),
-        out_specs=jax.tree.map(lambda _: pl.BlockSpec(memory_space=pltpu.VMEM), out_shape),
+        out_specs=jax.tree.map(lambda _: pl.BlockSpec(memory_space=out_space), out_shape),
         scratch_shapes=scratch,
         compiler_params=pltpu.CompilerParams(vmem_limit_bytes=limit),
         cost_estimate=pl.CostEstimate(flops=flops, bytes_accessed=moved, transcendentals=0),
@@ -307,7 +320,19 @@
         moved=2 * full * WIDTH,
     )
     bounds, order, queries = lax.optimization_barrier((bounds, order, queries))
+    own_kv = call(
+        dec_kv_kernel,
+        shape((2, 16, WIDTH), BF16),
+        (),
+        (hidden,),
+        (w_t,),
+        scratch=[pltpu.VMEM((2, WIDTH, full), BF16), pltpu.SemaphoreType.DMA((2,))],
+        flops=4 * 16 * full * WIDTH,
+        moved=4 * full * WIDTH,
+        limit=VMEM_ALL,
+    )
     queries = lax.all_to_all(queries, "z", 0, 0, tiled=True)
+    own_kv, queries = lax.optimization_barrier((own_kv, queries))
     queries = lax.all_gather(queries, "c", axis=0, tiled=True)
     partial = call(
         dec_attention_kernel,
@@ -321,11 +346,9 @@
     *x_blocks, partial = lax.optimization_barrier((*x_blocks, partial))
     term_blocks = call(
         prefill_kernel,
-        (shape((WIDTH, tokens), F32),)
-        + (shape((WIDTH, tokens), BF16),) * 3
-        + (shape((2, 16, WIDTH), BF16),),
+        (shape((WIDTH, tokens), F32),) + (shape((WIDTH, tokens), BF16),) * 3,
         (pre_lens, tp),
-        (norm_gain.reshape(full // 128, 128), hidden),
+        (norm_gain.reshape(full // 128, 128),),
         (*x_blocks, w_t, pre_keys.T, pre_values.T, w_out),
         scratch=[
             pltpu.VMEM((full, tokens), BF16),
@@ -337,14 +360,20 @@
             pltpu.VMEM((128, 128), F32),
         ]
         + [pltpu.VMEM((WIDTH, tokens), BF16)] * 4
-        + [pltpu.SemaphoreType.DMA((14,))],
+        + [
+            pltpu.VMEM((WIDTH, tokens), F32),
+            pltpu.VMEM((3, WIDTH, tokens), BF16),
+            pltpu.SemaphoreType.DMA((10,)),
+            pltpu.SemaphoreType.DMA((4,)),
+        ],
+        out_space=pltpu.HBM,
         flops=8 * tokens * full * WIDTH + 4 * tokens * 896 * WIDTH,
         moved=8 * full * WIDTH,
         limit=VMEM_ALL,
     )
     partial = lax.all_to_all(partial.reshape(NX * NC, NZ * 4, LANES), ("x", "c"), 0, 0, tiled=True)
-    *term_blocks, own_kv = term_blocks
-    own_kv, partial = lax.optimization_barrier((own_kv, partial))
+    term_blocks = list(term_blocks)
+    term_blocks[-1], partial = lax.optimization_barrier((term_blocks[-1], partial))
     arrived = [turned(block, shift) for shift, block in enumerate(term_blocks) if shift > 0]
     pre_out = term_blocks[0] + sum(block.astype(F32) for block in arrived)
     partial = call(

time: 110 us -> 109 us (level)
  waiting for transfers between devices: 14.8 us -> 12 us
  Pallas kernels: 20.6 us -> 23.1 us
    all_to_all x1, waiting for transfers between devices: 4.31 us -> 0.85 us  [body(): queries = lax.all_to_all(queries, 'z', 0, 0, tiled=True)]
    pallas_call x6 -> x7, Pallas kernels: 20.6 us -> 23.1 us  [call(): pl.pallas_call(kernel, out_shape=out_shape, in_specs=[pl.BlockSpec(memory...]
  transfers between devices with their start and end apart: 11 -> 11, of which waited for: 5 -> 5; matrix products, arithmetic and copies ran while one was open for 4% -> 4% of each run, Pallas kernels for 17% -> 19%
where the time goes in v7:
time: 109 us; the launch traced here: 108 us
  starting transfers between devices  57.2 us (52%)
  Pallas kernels  23.1 us (21%)
  waiting for transfers between devices  12 us (11%)
  blocking collectives  6.64 us (6%)
  local copies, waits for them, and re-layouts  4.67 us (4%)
  other arithmetic  2.61 us (2%)
  between operations  1.5 us (1%)
    pallas_call x7, Pallas kernels, call(): pl.pallas_call(kernel, out_shape=out_shape, in_specs=[pl.BlockSpec(memory...  23.1 us
    ppermute x6, starting transfers between devices, turned(): return lax.ppermute(block, 'tp', [(t, (t + shift) % NT) for t in range(NT)])  16.7 us
    all_to_all x1, starting transfers between devices, body(): queries = lax.all_to_all(queries, 'z', 0, 0, tiled=True)  14.9 us
    all_to_all x1, starting transfers between devices, body(): partial = lax.all_to_all(partial, 'z', 0, 0, tiled=True)  11 us
    all_to_all x1, starting transfers between devices, spread(): return lax.all_to_all(copies, axes, 0, 0, tiled=True)  7.58 us
    all_gather x1, blocking collectives, body(): queries = lax.all_gather(queries, 'c', axis=0, tiled=True)  6.64 us
    ppermute x6, waiting for transfers between devices, turned(): return lax.ppermute(block, 'tp', [(t, (t + shift) % NT) for t in range(NT)])  5.02 us
    all_to_all x1, starting transfers between devices, body(): lax.all_to_all(partial.reshape(NX * NC, NZ * 4, LANES), ('x', 'c'), 0, 0,...  3.73 us
  transfers between devices with their start and end apart: 11, of which 5 were waited for; matrix products, arithmetic and copies ran while one was open for 4% of the time, Pallas kernels for 19%

profile of v7, /device:TPU:1, one launch (start us, length us, event | category | flops | bytes accessed | tf_op | source)
XLA Modules:
  0.0 107.7 jit_solution(12470176325221247148)
XLA Ops:
  0.6 0.0 copy-start.6
  0.6 1.4 %broadcast_in_dim.2 = bf16[16,4,320]{2,1,0:T(4,128)(2,1)} broadcast(bf16[4,320]{1,0:T(4,128)(2,1)} %param.12), dimensions={1,2} | broadcast | bytes 43520 | tf_op jit(solution)/shard_map/broadcast_in_dim | solution.py:284
  2.0 7.6 %all-to-all-start = ((bf16[16,4,320]{2,1,0:T(4,128)(2,1)}), bf16[16,4,320]{2,1,0:T(4,128)(2,1)S(1)}, u32[]{:S(2)}, u32[]{:S(2)}) async-start(bf16[16,4,320]{2,1,0:T(4,128)(2,1)} %broadcast_in_dim.2), calls=%async_computation | async-start | bytes 98304 | tf_op jit(solution)/shard_map/all_to_all | solution.py:285
  9.6 1.2 %slice_bitcast_fusion.w_ref = bf16[320,1280]{1,0:T(8,128)(2,1)S(1)} fusion(bf16[3,320,1280]{2,1,0:T(8,128)(2,1)} %bitcast.19), kind=kLoop, calls=%fused_computation | loop fusion | bytes 1638400 | tf_op jit(solution)/shard_map/squeeze | solution.py:317
  10.8 0.0 copy-start.1
  10.8 0.0 copy-start.2
  10.8 0.8 reshape.28.gain_ref
  11.6 0.0 copy-start.5
  11.6 0.7 copy-done.5
  12.3 0.6 shard_map.124
  12.9 3.2 %all-to-all-done.x_ref = bf16[16,4,320]{2,1,0:T(4,128)(2,1)S(1)} async-done(((bf16[16,4,320]{2,1,0:T(4,128)(2,1)}), bf16[16,4,320]{2,1,0:T(4,128)(2,1)S(1)}, u32[]{:S(2)}, u32[]{:S(2)}) %all-to-all-start) | async-done | bytes 40992 | tf_op jit(solution)/shard_map/all_to_all | solution.py:285
  16.1 1.2 %shard_map.122 = (bf16[16,40,128]{2,1,0:T(8,128)(2,1)}, bf16[16,320]{1,0:T(8,128)(2,1)S(1)}, bf16[16,1280]{1,0:T(8,128)(2,1)S(1)}) custom-call(bf16[16,4,320]{2,1,0:T(4,128)(2,1)S(1)} %all-to-all-done.x_ref, f32[1,1280]{1,0:T(1,128)S(1)} %reshape.28.gain_ref, bf16[320,1280]{1,0:T(8,128)(2,1)S(1)} %slice_bitcast_fusion.w_ref), custom_call_target="tpu_custom_call" | custom-call | flops 13107200 | bytes 819200 | tf_op jit(solution)/shard_map/pallas_call | solution.py:266
  17.3 0.0 copy-start.4
  17.3 0.6 copy-done.4
  17.9 14.9 %all-to-all-start.1 = ((bf16[16,40,128]{2,1,0:T(8,128)(2,1)}), bf16[16,40,128]{2,1,0:T(8,128)(2,1)S(1)}, u32[]{:S(2)}, u32[]{:S(2)}) async-start(bf16[16,40,128]{2,1,0:T(8,128)(2,1)} %get-tuple-element.27), calls=%async_computation.1 | async-start | bytes 327680 | tf_op jit(solution)/shard_map/all_to_all | solution.py:334
  32.8 0.0 copy-done.6
  32.8 2.9 %collective-permute-start.2 = (bf16[320,512]{1,0:T(8,128)(2,1)S(1)}, bf16[320,512]{1,0:T(8,128)(2,1)S(1)}, u32[]{:S(2)}, u32[]{:S(2)}) collective-permute-start(bf16[320,512]{1,0:T(8,128)(2,1)S(1)} %bitcast.24), channel_id=1, source_target_pairs={{0,3},{1,0},{2,1},{3,2},{4,7},{5,4},{6,5},{7,6},{8,11},{9,8},{10,9... | collective-permute-start | bytes 983048 | tf_op jit(solution)/shard_map/ppermute | solution.py:306
  35.7 3.0 %collective-permute-start.1 = (bf16[320,512]{1,0:T(8,128)(2,1)S(1)}, bf16[320,512]{1,0:T(8,128)(2,1)S(1)}, u32[]{:S(2)}, u32[]{:S(2)}) collective-permute-start(bf16[320,512]{1,0:T(8,128)(2,1)S(1)} %bitcast.25), channel_id=1, source_target_pairs={{0,2},{1,3},{2,0},{3,1},{4,6},{5,7},{6,4},{7,5},{8,10},{9,11},{10,... | collective-permute-start | bytes 983048 | tf_op jit(solution)/shard_map/ppermute | solution.py:306
  38.7 1.9 %collective-permute-start = (bf16[320,512]{1,0:T(8,128)(2,1)S(1)}, bf16[320,512]{1,0:T(8,128)(2,1)}, u32[]{:S(2)}, u32[]{:S(2)}) collective-permute-start(bf16[320,512]{1,0:T(8,128)(2,1)S(1)} %bitcast.26), channel_id=1, source_target_pairs={{0,1},{1,2},{2,3},{3,0},{4,5},{5,6},{6,7},{7,4},{8,9},{9,10},{10,1... | collective-permute-start | bytes 983048 | tf_op jit(solution)/shard_map/ppermute | solution.py:306
  40.7 3.5 %shard_map.123.kv_ref = bf16[2,16,320]{2,1,0:T(8,128)(2,1)} custom-call(bf16[16,1280]{1,0:T(8,128)(2,1)} %copy-done.4, bf16[3,320,1280]{2,1,0:T(8,128)(2,1)} %bitcast.20), custom_call_target="tpu_custom_call" | custom-call | flops 26214400 | bytes 1638400 | tf_op jit(solution)/shard_map/pallas_call | solution.py:266
  44.1 0.9 all-to-all-done.1
  45.0 6.6 %all_gather.3.qp_ref = bf16[32,40,128]{2,1,0:T(8,128)(2,1)S(1)} all-gather(bf16[16,40,128]{2,1,0:T(8,128)(2,1)S(1)} %all-to-all-done.1), channel_id=1, replica_groups=mesh['x'=4,'z'=16,'c'=2,'tp'=4] {'c'}, dimensions={0}, use_global_device_ids=true | all-gather | bytes 491520 | tf_op jit(solution)/shard_map/all_gather | solution.py:336
  51.6 0.0 copy-done.1
  51.6 0.0 copy-done.2
  51.6 4.8 %shard_map.125 = bf16[512,384]{1,0:T(8,128)(2,1)} custom-call(bf16[32,40,128]{2,1,0:T(8,128)(2,1)S(1)} %all_gather.3.qp_ref, f32[512,2]{1,0:T(8,128)S(1)} %get-tuple-element.29.bounds_ref, bf16[512,512]{1,0:T(8,128)(2,1)S(1)} %get-tuple-element.30.order_ref, bf16[320,640]{1,0:T(8,128)(2,1)S(1)} %bitcast.16, bf16[320,640]{1,0:T(8,128)(2,1)S(1)} %bitcast.17), custom_call_target="tpu_custom_call" | custom-call | flops 419430400 | bytes 819200 | tf_op jit(solution)/shard_map/pallas_call | solution.py:266
  56.4 0.0 collective-permute-done.2.x3_hbm
  56.4 0.0 copy-start.7
  56.4 0.0 collective-permute-done.1.x2_hbm
  56.4 0.0 copy-start.8
  56.4 0.0 collective-permute-done.x1_hbm
  56.5 3.7 %all-to-all-start.2 = ((bf16[8,64,384]{2,1,0:T(8,128)(2,1)}), bf16[8,64,384]{2,1,0:T(8,128)(2,1)S(1)}, u32[]{:S(2)}, u32[]{:S(2)}) async-start(bf16[8,64,384]{2,1,0:T(8,128)(2,1)} %bitcast.11), calls=%async_computation.2 | async-start | bytes 786432 | tf_op jit(solution)/shard_map/all_to_all | solution.py:374
  60.8 0.0 copy-done.7
  60.8 0.0 copy-done.8
  60.9 0.0 copy-start
  60.9 0.0 copy-start.3
  60.9 10.4 %shard_map.126 = (f32[320,512]{1,0:T(8,128)}, bf16[320,512]{1,0:T(8,128)(2,1)}, bf16[320,512]{1,0:T(8,128)(2,1)}, bf16[320,512]{1,0:T(8,128)(2,1)}) custom-call(s32[1]{0:T(128)S(6)} %copy.13.len_ref, s32[1]{0:T(128)} %bitcast.tp_ref, f32[10,128]{1,0:T(8,128)} %bitcast.22, bf16[320,512]{1,0:T(8,128)(2,1)} %bitcast.23, ...), custom_call_target="tpu_custom_call" | custom-call | flops 2264924160 | bytes 3276800 | tf_op jit(solution)/shard_map/pallas_call | solution.py:266
  71.3 0.0 all-to-all-done.2.in_ref
  71.3 1.4 %shard_map.127 = f32[16,4,384]{2,1,0:T(4,128)} custom-call(bf16[8,64,384]{2,1,0:T(8,128)(2,1)S(1)} %all-to-all-done.2.in_ref), custom_call_target="tpu_custom_call" | custom-call | flops 196608 | bytes 786432 | tf_op jit(solution)/shard_map/pallas_call | solution.py:266
  72.6 11.0 %all-to-all-start.3 = ((f32[16,4,384]{2,1,0:T(4,128)}), f32[16,4,384]{2,1,0:T(4,128)S(1)}, u32[]{:S(2)}, u32[]{:S(2)}) async-start(f32[16,4,384]{2,1,0:T(4,128)} %shard_map.127), calls=%async_computation.3 | async-start | bytes 196608 | tf_op jit(solution)/shard_map/all_to_all | solution.py:387
  83.7 1.9 %collective-permute-start.3 = (bf16[320,512]{1,0:T(8,128)(2,1)}, bf16[320,512]{1,0:T(8,128)(2,1)S(1)}, u32[]{:S(2)}, u32[]{:S(2)}) collective-permute-start(bf16[320,512]{1,0:T(8,128)(2,1)} %get-tuple-element.36), channel_id=1, source_target_pairs={{0,1},{1,2},{2,3},{3,0},{4,5},{5,6},{6,7},{7,4},{8,9},{9,10},{10,1... | collective-permute-start | bytes 983048 | tf_op jit(solution)/shard_map/ppermute | solution.py:306
  85.6 3.9 %collective-permute-start.4 = (bf16[320,512]{1,0:T(8,128)(2,1)}, bf16[320,512]{1,0:T(8,128)(2,1)S(1)}, u32[]{:S(2)}, u32[]{:S(2)}) collective-permute-start(bf16[320,512]{1,0:T(8,128)(2,1)} %get-tuple-element.37), channel_id=1, source_target_pairs={{0,2},{1,3},{2,0},{3,1},{4,6},{5,7},{6,4},{7,5},{8,10},{9,11},{10,... | collective-permute-start | bytes 983048 | tf_op jit(solution)/shard_map/ppermute | solution.py:306
  89.5 3.1 %collective-permute-start.5 = (bf16[320,512]{1,0:T(8,128)(2,1)}, bf16[320,512]{1,0:T(8,128)(2,1)S(1)}, u32[]{:S(2)}, u32[]{:S(2)}) collective-permute-start(bf16[320,512]{1,0:T(8,128)(2,1)} %get-tuple-element.40), channel_id=1, source_target_pairs={{0,3},{1,0},{2,1},{3,2},{4,7},{5,4},{6,5},{7,6},{8,11},{9,8},{10,9... | collective-permute-start | bytes 983048 | tf_op jit(solution)/shard_map/ppermute | solution.py:306
  92.6 2.9 %all-to-all-done.3.in_ref = f32[16,4,384]{2,1,0:T(4,128)S(1)} async-done(((f32[16,4,384]{2,1,0:T(4,128)}), f32[16,4,384]{2,1,0:T(4,128)S(1)}, u32[]{:S(2)}, u32[]{:S(2)}) %all-to-all-start.3) | async-done | bytes 98336 | tf_op jit(solution)/shard_map/all_to_all | solution.py:387
  95.5 0.0 copy-done
  95.5 0.0 copy-done.3
  95.5 1.3 %shard_map.128 = f32[4,4,320]{2,1,0:T(4,128)} custom-call(s32[1]{0:T(128)} %bitcast.13.own_ref, f32[16,4,384]{2,1,0:T(4,128)S(1)} %all-to-all-done.3.in_ref, bf16[16,320]{1,0:T(8,128)(2,1)S(1)} %get-tuple-element.42.q_ref, bf16[2,16,320]{2,1,0:T(8,128)(2,1)S(1)} %copy-done.3, bf16[320,1280]{1,0:T(8,128)(2,1)S(1)} %copy-done), custom_call_target="tpu_custom_call" | custom-call | flops 6553600 | bytes 819200 | tf_op jit(solution)/shard_map/pallas_call | solution.py:266
  96.8 3.3 %all-to-all-start.4 = ((f32[4,4,320]{2,1,0:T(4,128)}), f32[4,4,320]{2,1,0:T(4,128)S(1)}, u32[]{:S(2)}, u32[]{:S(2)}) async-start(f32[4,4,320]{2,1,0:T(4,128)} %shard_map.128), calls=%async_computation.4 | async-start | bytes 49152 | tf_op jit(solution)/shard_map/all_to_all | solution.py:396
  100.1 0.0 collective-permute-done.3
  100.1 1.9 %collective-permute-done.4 = bf16[320,512]{1,0:T(8,128)(2,1)S(1)} collective-permute-done((bf16[320,512]{1,0:T(8,128)(2,1)}, bf16[320,512]{1,0:T(8,128)(2,1)S(1)}, u32[]{:S(2)}, u32[]{:S(2)}) %collective-permute-start.4) | collective-permute-done | bytes 327712 | tf_op jit(solution)/shard_map/ppermute | solution.py:306
  102.1 3.1 %collective-permute-done.5 = bf16[320,512]{1,0:T(8,128)(2,1)S(1)} collective-permute-done((bf16[320,512]{1,0:T(8,128)(2,1)}, bf16[320,512]{1,0:T(8,128)(2,1)S(1)}, u32[]{:S(2)}, u32[]{:S(2)}) %collective-permute-start.5) | collective-permute-done | bytes 327712 | tf_op jit(solution)/shard_map/ppermute | solution.py:306
  105.1 2.0 %fusion = bf16[512,320]{0,1:T(8,128)(2,1)} fusion(f32[320,512]{1,0:T(8,128)} %get-tuple-element.35, bf16[320,512]{1,0:T(8,128)(2,1)S(1)} %collective-permute-done.5, bf16[320,512]{1,0:T(8,128)(2,1)S(1)} %collective-permute-done.4, bf16[320,512]{1,0:T(8,128)(2,1)S(1)} %collective-permute-done.3), kind=kLoop, calls=%fused_computation.2 | loop fusion | flops 1146880 | bytes 1966080 | tf_op jit(solution)/shard_map/transpose | solution.py:398
  107.1 0.0 all-to-all-done.4
  107.2 0.6 reduce_sum.9
Async XLA Ops:
  0.6 32.2 %copy-start.6 = (bf16[512,320]{0,1:T(8,128)(2,1)S(1)}, bf16[512,320]{0,1:T(8,128)(2,1)}, u32[]{:S(2)}) copy-start(bf16[512,320]{0,1:T(8,128)(2,1)} %param.11) | copy-start | bytes 983044
  2.0 14.1 %all-to-all-start = ((bf16[16,4,320]{2,1,0:T(4,128)(2,1)}), bf16[16,4,320]{2,1,0:T(4,128)(2,1)S(1)}, u32[]{:S(2)}, u32[]{:S(2)}) async-start(bf16[16,4,320]{2,1,0:T(4,128)(2,1)} %broadcast_in_dim.2), calls=%async_computation | async-start | bytes 98304 | tf_op jit(solution)/shard_map/all_to_all | solution.py:285
  10.8 40.8 %copy-start.1 = (bf16[640,320]{0,1:T(8,128)(2,1)S(1)}, bf16[640,320]{0,1:T(8,128)(2,1)}, u32[]{:S(2)}) copy-start(bf16[640,320]{0,1:T(8,128)(2,1)} %param.19) | copy-start | bytes 1228804
  10.8 40.8 %copy-start.2 = (bf16[640,320]{0,1:T(8,128)(2,1)S(1)}, bf16[640,320]{0,1:T(8,128)(2,1)}, u32[]{:S(2)}) copy-start(bf16[640,320]{0,1:T(8,128)(2,1)} %param.20) | copy-start | bytes 1228804
  11.6 0.7 copy-start.5
  17.3 0.6 copy-start.4
  17.9 27.1 %all-to-all-start.1 = ((bf16[16,40,128]{2,1,0:T(8,128)(2,1)}), bf16[16,40,128]{2,1,0:T(8,128)(2,1)S(1)}, u32[]{:S(2)}, u32[]{:S(2)}) async-start(bf16[16,40,128]{2,1,0:T(8,128)(2,1)} %get-tuple-element.27), calls=%async_computation.1 | async-start | bytes 327680 | tf_op jit(solution)/shard_map/all_to_all | solution.py:334
  32.8 23.6 %collective-permute-start.2 = (bf16[320,512]{1,0:T(8,128)(2,1)S(1)}, bf16[320,512]{1,0:T(8,128)(2,1)S(1)}, u32[]{:S(2)}, u32[]{:S(2)}) collective-permute-start(bf16[320,512]{1,0:T(8,128)(2,1)S(1)} %bitcast.24), channel_id=1, source_target_pairs={{0,3},{1,0},{2,1},{3,2},{4,7},{5,4},{6,5},{7,6},{8,11},{9,8},{10,9... | collective-permute-start | bytes 983048 | tf_op jit(solution)/shard_map/ppermute | solution.py:306
  35.7 20.7 %collective-permute-start.1 = (bf16[320,512]{1,0:T(8,128)(2,1)S(1)}, bf16[320,512]{1,0:T(8,128)(2,1)S(1)}, u32[]{:S(2)}, u32[]{:S(2)}) collective-permute-start(bf16[320,512]{1,0:T(8,128)(2,1)S(1)} %bitcast.25), channel_id=1, source_target_pairs={{0,2},{1,3},{2,0},{3,1},{4,6},{5,7},{6,4},{7,5},{8,10},{9,11},{10,... | collective-permute-start | bytes 983048 | tf_op jit(solution)/shard_map/ppermute | solution.py:306
  38.7 17.7 %collective-permute-start = (bf16[320,512]{1,0:T(8,128)(2,1)S(1)}, bf16[320,512]{1,0:T(8,128)(2,1)}, u32[]{:S(2)}, u32[]{:S(2)}) collective-permute-start(bf16[320,512]{1,0:T(8,128)(2,1)S(1)} %bitcast.26), channel_id=1, source_target_pairs={{0,1},{1,2},{2,3},{3,0},{4,5},{5,6},{6,7},{7,4},{8,9},{9,10},{10,1... | collective-permute-start | bytes 983048 | tf_op jit(solution)/shard_map/ppermute | solution.py:306
  56.4 4.4 %copy-start.7 = (bf16[320,512]{1,0:T(8,128)(2,1)}, bf16[320,512]{1,0:T(8,128)(2,1)S(1)}, u32[]{:S(2)}) copy-start(bf16[320,512]{1,0:T(8,128)(2,1)S(1)} %collective-permute-done.2.x3_hbm) | copy-start | bytes 983044
  56.4 4.4 %copy-start.8 = (bf16[320,512]{1,0:T(8,128)(2,1)}, bf16[320,512]{1,0:T(8,128)(2,1)S(1)}, u32[]{:S(2)}) copy-start(bf16[320,512]{1,0:T(8,128)(2,1)S(1)} %collective-permute-done.1.x2_hbm) | copy-start | bytes 983044
  56.5 14.8 %all-to-all-start.2 = ((bf16[8,64,384]{2,1,0:T(8,128)(2,1)}), bf16[8,64,384]{2,1,0:T(8,128)(2,1)S(1)}, u32[]{:S(2)}, u32[]{:S(2)}) async-start(bf16[8,64,384]{2,1,0:T(8,128)(2,1)} %bitcast.11), calls=%async_computation.2 | async-start | bytes 786432 | tf_op jit(solution)/shard_map/all_to_all | solution.py:374
  60.9 34.6 %copy-start = (bf16[320,1280]{1,0:T(8,128)(2,1)S(1)}, bf16[320,1280]{1,0:T(8,128)(2,1)}, u32[]{:S(2)}) copy-start(bf16[320,1280]{1,0:T(8,128)(2,1)} %w_ref.1) | copy-start | bytes 2457604
  60.9 34.6 %copy-start.3 = (bf16[2,16,320]{2,1,0:T(8,128)(2,1)S(1)}, bf16[2,16,320]{2,1,0:T(8,128)(2,1)}, u32[]{:S(2)}) copy-start(bf16[2,16,320]{2,1,0:T(8,128)(2,1)} %shard_map.123.kv_ref) | copy-start | bytes 61444
  72.6 22.9 %all-to-all-start.3 = ((f32[16,4,384]{2,1,0:T(4,128)}), f32[16,4,384]{2,1,0:T(4,128)S(1)}, u32[]{:S(2)}, u32[]{:S(2)}) async-start(f32[16,4,384]{2,1,0:T(4,128)} %shard_map.127), calls=%async_computation.3 | async-start | bytes 196608 | tf_op jit(solution)/shard_map/all_to_all | solution.py:387
  83.7 16.5 %collective-permute-start.3 = (bf16[320,512]{1,0:T(8,128)(2,1)}, bf16[320,512]{1,0:T(8,128)(2,1)S(1)}, u32[]{:S(2)}, u32[]{:S(2)}) collective-permute-start(bf16[320,512]{1,0:T(8,128)(2,1)} %get-tuple-element.36), channel_id=1, source_target_pairs={{0,1},{1,2},{2,3},{3,0},{4,5},{5,6},{6,7},{7,4},{8,9},{9,10},{10,1... | collective-permute-start | bytes 983048 | tf_op jit(solution)/shard_map/ppermute | solution.py:306
  85.6 16.5 %collective-permute-start.4 = (bf16[320,512]{1,0:T(8,128)(2,1)}, bf16[320,512]{1,0:T(8,128)(2,1)S(1)}, u32[]{:S(2)}, u32[]{:S(2)}) collective-permute-start(bf16[320,512]{1,0:T(8,128)(2,1)} %get-tuple-element.37), channel_id=1, source_target_pairs={{0,2},{1,3},{2,0},{3,1},{4,6},{5,7},{6,4},{7,5},{8,10},{9,11},{10,... | collective-permute-start | bytes 983048 | tf_op jit(solution)/shard_map/ppermute | solution.py:306
  89.5 15.6 %collective-permute-start.5 = (bf16[320,512]{1,0:T(8,128)(2,1)}, bf16[320,512]{1,0:T(8,128)(2,1)S(1)}, u32[]{:S(2)}, u32[]{:S(2)}) collective-permute-start(bf16[320,512]{1,0:T(8,128)(2,1)} %get-tuple-element.40), channel_id=1, source_target_pairs={{0,3},{1,0},{2,1},{3,2},{4,7},{5,4},{6,5},{7,6},{8,11},{9,8},{10,9... | collective-permute-start | bytes 983048 | tf_op jit(solution)/shard_map/ppermute | solution.py:306
  96.8 10.3 %all-to-all-start.4 = ((f32[4,4,320]{2,1,0:T(4,128)}), f32[4,4,320]{2,1,0:T(4,128)S(1)}, u32[]{:S(2)}, u32[]{:S(2)}) async-start(f32[4,4,320]{2,1,0:T(4,128)} %shard_map.128), calls=%async_computation.4 | async-start | bytes 49152 | tf_op jit(solution)/shard_map/all_to_all | solution.py:396

commit v8 on v7

--- a/solution.py
+++ b/solution.py
@@ -133,13 +133,37 @@
     return values, tops, totals
 
 
+def pick(at, rows_first):
+    lanes = LANES - WIDTH
+    dims = (WIDTH, lanes) if rows_first else (lanes, WIDTH)
+    head = lax.broadcasted_iota(jnp.int32, dims, 0 if rows_first else 1)
+    lane = lax.broadcasted_iota(jnp.int32, dims, 1 if rows_first else 0)
+    out = jnp.zeros(dims, F32)
+    for h in range(HEADS):
+        inside = (head == h * HD) if rows_first else (head >= h * HD) & (head < (h + 1) * HD)
+        out = jnp.where(inside & at(lane, h), 1.0, out)
+    return out.astype(BF16)
+
+
 def dec_merge_kernel(in_ref, out_ref):
     count, rows = in_ref.shape[0], in_ref.shape[1]
-    values, tops, totals = merged([in_ref[n] for n in range(count)], rows)
-    lane = lax.broadcasted_iota(jnp.int32, (rows, LANES - WIDTH), 1)
+    of_top = pick(lambda lane, h: (lane >= 3 * h) & (lane < 3 * h + 3), False)
+    of_total = pick(lambda lane, h: (lane >= 12 + 3 * h) & (lane < 15 + 3 * h), False)
+    extras = [in_ref[n, :, WIDTH:LANES] for n in range(count)]
+    part_tops = [dot(extra, of_top, ((1,), (0,))) for extra in extras]
+    best = part_tops[0]
+    for top in part_tops[1:]:
+        best = jnp.maximum(best, top)
+    values, totals = jnp.zeros((rows, WIDTH), F32), jnp.zeros((rows, WIDTH), F32)
+    for n, top in enumerate(part_tops):
+        scale = jnp.exp2((top - best) * LOG2E_SCALE)
+        values = values + scale * in_ref[n, :, 0:WIDTH].astype(F32)
+        totals = totals + scale * dot(extras[n], of_total, ((1,), (0,)))
     extra = jnp.zeros((rows, LANES - WIDTH), F32)
-    for n, value in enumerate(tops + totals):
-        extra = jnp.where(lane == n, value, extra)
+    top_lanes = pick(lambda lane, h: lane == h, True)
+    total_lanes = pick(lambda lane, h: lane == HEADS + h, True)
+    for top, total in zip(thirds(best), thirds(totals)):
+        extra = extra + dot(top, top_lanes, ((1,), (0,))) + dot(total, total_lanes, ((1,), (0,)))
     for z in range(NZ):
         out_ref[z, :, 0:WIDTH] = values[4 * z : 4 * z + 4]
         out_ref[z, :, WIDTH:LANES] = extra[4 * z : 4 * z + 4]
@@ -250,6 +274,11 @@
         send.wait()
 
 
+def add_terms_kernel(own_ref, a_ref, b_ref, c_ref, out_ref):
+    total = own_ref[...] + a_ref[...].astype(F32) + b_ref[...].astype(F32) + c_ref[...].astype(F32)
+    out_ref[...] = total.astype(BF16)
+
+
 def dec_kv_kernel(hd_ref, w_hbm, kv_ref, w_ref, sems):
     fetches = [pltpu.make_async_copy(w_hbm.at[n + 1], w_ref.at[n], sems.at[n]) for n in range(2)]
     for fetch in fetches:
@@ -375,7 +404,14 @@
     term_blocks = list(term_blocks)
     term_blocks[-1], partial = lax.optimization_barrier((term_blocks[-1], partial))
     arrived = [turned(block, shift) for shift, block in enumerate(term_blocks) if shift > 0]
-    pre_out = term_blocks[0] + sum(block.astype(F32) for block in arrived)
+    pre_out = call(
+        add_terms_kernel,
+        shape((WIDTH, tokens), BF16),
+        (),
+        (term_blocks[0], *arrived),
+        flops=4 * WIDTH * tokens,
+        moved=12 * WIDTH * tokens,
+    )
     partial = call(
         dec_merge_kernel,
         shape((NZ, 4, LANES), F32),
@@ -395,7 +431,7 @@
     )
     terms = lax.all_to_all(terms, "tp", 0, 0, tiled=True)
     dec_out = jnp.sum(terms, axis=0).astype(BF16)
-    return pre_out.astype(BF16).T, dec_out
+    return pre_out.T, dec_out
 
 
 def solution(mesh):

time: 109 us -> 109 us (level)
  other arithmetic: 2.61 us -> 0.59 us
    transpose x1 -> x0, other arithmetic: 2.02 us -> none  [body(): return (pre_out.astype(BF16).T, dec_out)]
    unnamed x18 -> x20, local copies, waits for them, and re-layouts: 1.33 us -> 2.42 us
    pallas_call x7 -> x8, Pallas kernels: 23.1 us -> 24.1 us  [call(): pl.pallas_call(kernel, out_shape=out_shape, in_specs=[pl.BlockSpec(memory...]
  transfers between devices with their start and end apart: 11 -> 11, of which waited for: 5 -> 5; matrix products, arithmetic and copies ran while one was open for 4% -> 2% of each run, Pallas kernels for 19% -> 20%
where the time goes in v8:
time: 109 us; the launch traced here: 108 us
  starting transfers between devices  57.2 us (52%)
  Pallas kernels  24.1 us (22%)
  waiting for transfers between devices  12 us (11%)
  blocking collectives  6.64 us (6%)
  local copies, waits for them, and re-layouts  5.76 us (5%)
  between operations  1.5 us (1%)
    pallas_call x8, Pallas kernels, call(): pl.pallas_call(kernel, out_shape=out_shape, in_specs=[pl.BlockSpec(memory...  24.1 us
    ppermute x6, starting transfers between devices, turned(): return lax.ppermute(block, 'tp', [(t, (t + shift) % NT) for t in range(NT)])  16.7 us
    all_to_all x1, starting transfers between devices, body(): queries = lax.all_to_all(queries, 'z', 0, 0, tiled=True)  14.9 us
    all_to_all x1, starting transfers between devices, body(): partial = lax.all_to_all(partial, 'z', 0, 0, tiled=True)  11 us
    all_to_all x1, starting transfers between devices, spread(): return lax.all_to_all(copies, axes, 0, 0, tiled=True)  7.58 us
    all_gather x1, blocking collectives, body(): queries = lax.all_gather(queries, 'c', axis=0, tiled=True)  6.64 us
    ppermute x6, waiting for transfers between devices, turned(): return lax.ppermute(block, 'tp', [(t, (t + shift) % NT) for t in range(NT)])  5 us
    all_to_all x1, starting transfers between devices, body(): lax.all_to_all(partial.reshape(NX * NC, NZ * 4, LANES), ('x', 'c'), 0, 0,...  3.73 us
  transfers between devices with their start and end apart: 11, of which 5 were waited for; matrix products, arithmetic and copies ran while one was open for 2% of the time, Pallas kernels for 20%

profile of v8, /device:TPU:1, one launch (start us, length us, event | category | flops | bytes accessed | tf_op | source)
XLA Modules:
  0.0 107.8 jit_solution(18323385259690402696)
XLA Ops:
  0.6 0.0 copy-start.7
  0.6 1.4 %broadcast_in_dim.2 = bf16[16,4,320]{2,1,0:T(4,128)(2,1)} broadcast(bf16[4,320]{1,0:T(4,128)(2,1)} %param.12), dimensions={1,2} | broadcast | bytes 43520 | tf_op jit(solution)/shard_map/broadcast_in_dim | solution.py:313
  2.0 7.6 %all-to-all-start = ((bf16[16,4,320]{2,1,0:T(4,128)(2,1)}), bf16[16,4,320]{2,1,0:T(4,128)(2,1)S(1)}, u32[]{:S(2)}, u32[]{:S(2)}) async-start(bf16[16,4,320]{2,1,0:T(4,128)(2,1)} %broadcast_in_dim.2), calls=%async_computation | async-start | bytes 98304 | tf_op jit(solution)/shard_map/all_to_all | solution.py:314
  9.6 1.2 %slice_bitcast_fusion.w_ref = bf16[320,1280]{1,0:T(8,128)(2,1)S(1)} fusion(bf16[3,320,1280]{2,1,0:T(8,128)(2,1)} %bitcast.18), kind=kLoop, calls=%fused_computation | loop fusion | bytes 1638400 | tf_op jit(solution)/shard_map/squeeze | solution.py:346
  10.8 0.0 copy-start.2
  10.8 0.0 copy-start.3
  10.8 0.8 reshape.28.gain_ref
  11.6 0.0 copy-start.6
  11.6 0.7 copy-done.6
  12.3 0.6 shard_map.124
  12.9 3.2 %all-to-all-done.x_ref = bf16[16,4,320]{2,1,0:T(4,128)(2,1)S(1)} async-done(((bf16[16,4,320]{2,1,0:T(4,128)(2,1)}), bf16[16,4,320]{2,1,0:T(4,128)(2,1)S(1)}, u32[]{:S(2)}, u32[]{:S(2)}) %all-to-all-start) | async-done | bytes 40992 | tf_op jit(solution)/shard_map/all_to_all | solution.py:314
  16.1 1.2 %shard_map.122 = (bf16[16,40,128]{2,1,0:T(8,128)(2,1)}, bf16[16,320]{1,0:T(8,128)(2,1)S(1)}, bf16[16,1280]{1,0:T(8,128)(2,1)S(1)}) custom-call(bf16[16,4,320]{2,1,0:T(4,128)(2,1)S(1)} %all-to-all-done.x_ref, f32[1,1280]{1,0:T(1,128)S(1)} %reshape.28.gain_ref, bf16[320,1280]{1,0:T(8,128)(2,1)S(1)} %slice_bitcast_fusion.w_ref), custom_call_target="tpu_custom_call" | custom-call | flops 13107200 | bytes 819200 | tf_op jit(solution)/shard_map/pallas_call | solution.py:295
  17.3 0.0 copy-start.5
  17.3 0.6 copy-done.5
  17.9 14.9 %all-to-all-start.1 = ((bf16[16,40,128]{2,1,0:T(8,128)(2,1)}), bf16[16,40,128]{2,1,0:T(8,128)(2,1)S(1)}, u32[]{:S(2)}, u32[]{:S(2)}) async-start(bf16[16,40,128]{2,1,0:T(8,128)(2,1)} %get-tuple-element.27), calls=%async_computation.1 | async-start | bytes 327680 | tf_op jit(solution)/shard_map/all_to_all | solution.py:363
  32.8 0.0 copy-done.7
  32.8 2.9 %collective-permute-start.2 = (bf16[320,512]{1,0:T(8,128)(2,1)S(1)}, bf16[320,512]{1,0:T(8,128)(2,1)S(1)}, u32[]{:S(2)}, u32[]{:S(2)}) collective-permute-start(bf16[320,512]{1,0:T(8,128)(2,1)S(1)} %bitcast.24), channel_id=1, source_target_pairs={{0,3},{1,0},{2,1},{3,2},{4,7},{5,4},{6,5},{7,6},{8,11},{9,8},{10,9... | collective-permute-start | bytes 983048 | tf_op jit(solution)/shard_map/ppermute | solution.py:335
  35.7 3.0 %collective-permute-start.1 = (bf16[320,512]{1,0:T(8,128)(2,1)S(1)}, bf16[320,512]{1,0:T(8,128)(2,1)S(1)}, u32[]{:S(2)}, u32[]{:S(2)}) collective-permute-start(bf16[320,512]{1,0:T(8,128)(2,1)S(1)} %bitcast.25), channel_id=1, source_target_pairs={{0,2},{1,3},{2,0},{3,1},{4,6},{5,7},{6,4},{7,5},{8,10},{9,11},{10,... | collective-permute-start | bytes 983048 | tf_op jit(solution)/shard_map/ppermute | solution.py:335
  38.7 1.9 %collective-permute-start = (bf16[320,512]{1,0:T(8,128)(2,1)S(1)}, bf16[320,512]{1,0:T(8,128)(2,1)}, u32[]{:S(2)}, u32[]{:S(2)}) collective-permute-start(bf16[320,512]{1,0:T(8,128)(2,1)S(1)} %bitcast.26), channel_id=1, source_target_pairs={{0,1},{1,2},{2,3},{3,0},{4,5},{5,6},{6,7},{7,4},{8,9},{9,10},{10,1... | collective-permute-start | bytes 983048 | tf_op jit(solution)/shard_map/ppermute | solution.py:335
  40.7 3.5 %shard_map.123.kv_ref = bf16[2,16,320]{2,1,0:T(8,128)(2,1)} custom-call(bf16[16,1280]{1,0:T(8,128)(2,1)} %copy-done.5, bf16[3,320,1280]{2,1,0:T(8,128)(2,1)} %bitcast.19), custom_call_target="tpu_custom_call" | custom-call | flops 26214400 | bytes 1638400 | tf_op jit(solution)/shard_map/pallas_call | solution.py:295
  44.1 0.8 all-to-all-done.1
  45.0 6.6 %all_gather.3.qp_ref = bf16[32,40,128]{2,1,0:T(8,128)(2,1)S(1)} all-gather(bf16[16,40,128]{2,1,0:T(8,128)(2,1)S(1)} %all-to-all-done.1), channel_id=1, replica_groups=mesh['x'=4,'z'=16,'c'=2,'tp'=4] {'c'}, dimensions={0}, use_global_device_ids=true | all-gather | bytes 491520 | tf_op jit(solution)/shard_map/all_gather | solution.py:365
  51.6 0.0 copy-done.2
  51.6 0.0 copy-done.3
  51.6 4.8 %shard_map.125 = bf16[512,384]{1,0:T(8,128)(2,1)} custom-call(bf16[32,40,128]{2,1,0:T(8,128)(2,1)S(1)} %all_gather.3.qp_ref, f32[512,2]{1,0:T(8,128)S(1)} %get-tuple-element.29.bounds_ref, bf16[512,512]{1,0:T(8,128)(2,1)S(1)} %get-tuple-element.30.order_ref, bf16[320,640]{1,0:T(8,128)(2,1)S(1)} %bitcast.15, bf16[320,640]{1,0:T(8,128)(2,1)S(1)} %bitcast.16), custom_call_target="tpu_custom_call" | custom-call | flops 419430400 | bytes 819200 | tf_op jit(solution)/shard_map/pallas_call | solution.py:295
  56.4 0.0 collective-permute-done.2.x3_hbm
  56.4 0.0 copy-start.8
  56.4 0.0 collective-permute-done.1.x2_hbm
  56.4 0.0 copy-start.9
  56.4 0.0 collective-permute-done.x1_hbm
  56.5 3.7 %all-to-all-start.2 = ((bf16[8,64,384]{2,1,0:T(8,128)(2,1)}), bf16[8,64,384]{2,1,0:T(8,128)(2,1)S(1)}, u32[]{:S(2)}, u32[]{:S(2)}) async-start(bf16[8,64,384]{2,1,0:T(8,128)(2,1)} %bitcast.11), calls=%async_computation.2 | async-start | bytes 786432 | tf_op jit(solution)/shard_map/all_to_all | solution.py:403
  60.8 0.0 copy-done.8
  60.8 0.0 copy-done.9
  60.9 0.0 copy-start
  60.9 0.0 copy-start.4
  60.9 10.4 %shard_map.126 = (f32[320,512]{1,0:T(8,128)}, bf16[320,512]{1,0:T(8,128)(2,1)}, bf16[320,512]{1,0:T(8,128)(2,1)}, bf16[320,512]{1,0:T(8,128)(2,1)}) custom-call(s32[1]{0:T(128)S(6)} %copy.13.len_ref, s32[1]{0:T(128)} %bitcast.tp_ref, f32[10,128]{1,0:T(8,128)} %bitcast.22, bf16[320,512]{1,0:T(8,128)(2,1)} %bitcast.23, ...), custom_call_target="tpu_custom_call" | custom-call | flops 2264924160 | bytes 3276800 | tf_op jit(solution)/shard_map/pallas_call | solution.py:295
  71.3 0.0 all-to-all-done.2.in_ref
  71.3 1.4 %shard_map.128 = f32[16,4,384]{2,1,0:T(4,128)} custom-call(bf16[8,64,384]{2,1,0:T(8,128)(2,1)S(1)} %all-to-all-done.2.in_ref), custom_call_target="tpu_custom_call" | custom-call | flops 196608 | bytes 786432 | tf_op jit(solution)/shard_map/pallas_call | solution.py:295
  72.7 11.0 %all-to-all-start.3 = ((f32[16,4,384]{2,1,0:T(4,128)}), f32[16,4,384]{2,1,0:T(4,128)S(1)}, u32[]{:S(2)}, u32[]{:S(2)}) async-start(f32[16,4,384]{2,1,0:T(4,128)} %shard_map.128), calls=%async_computation.3 | async-start | bytes 196608 | tf_op jit(solution)/shard_map/all_to_all | solution.py:423
  83.7 1.9 %collective-permute-start.3 = (bf16[320,512]{1,0:T(8,128)(2,1)}, bf16[320,512]{1,0:T(8,128)(2,1)S(1)}, u32[]{:S(2)}, u32[]{:S(2)}) collective-permute-start(bf16[320,512]{1,0:T(8,128)(2,1)} %get-tuple-element.36), channel_id=1, source_target_pairs={{0,1},{1,2},{2,3},{3,0},{4,5},{5,6},{6,7},{7,4},{8,9},{9,10},{10,1... | collective-permute-start | bytes 983048 | tf_op jit(solution)/shard_map/ppermute | solution.py:335
  85.6 3.9 %collective-permute-start.4 = (bf16[320,512]{1,0:T(8,128)(2,1)}, bf16[320,512]{1,0:T(8,128)(2,1)S(1)}, u32[]{:S(2)}, u32[]{:S(2)}) collective-permute-start(bf16[320,512]{1,0:T(8,128)(2,1)} %get-tuple-element.37), channel_id=1, source_target_pairs={{0,2},{1,3},{2,0},{3,1},{4,6},{5,7},{6,4},{7,5},{8,10},{9,11},{10,... | collective-permute-start | bytes 983048 | tf_op jit(solution)/shard_map/ppermute | solution.py:335
  89.6 3.1 %collective-permute-start.5 = (bf16[320,512]{1,0:T(8,128)(2,1)}, bf16[320,512]{1,0:T(8,128)(2,1)S(1)}, u32[]{:S(2)}, u32[]{:S(2)}) collective-permute-start(bf16[320,512]{1,0:T(8,128)(2,1)} %get-tuple-element.40), channel_id=1, source_target_pairs={{0,3},{1,0},{2,1},{3,2},{4,7},{5,4},{6,5},{7,6},{8,11},{9,8},{10,9... | collective-permute-start | bytes 983048 | tf_op jit(solution)/shard_map/ppermute | solution.py:335
  92.7 2.9 %all-to-all-done.3.in_ref = f32[16,4,384]{2,1,0:T(4,128)S(1)} async-done(((f32[16,4,384]{2,1,0:T(4,128)}), f32[16,4,384]{2,1,0:T(4,128)S(1)}, u32[]{:S(2)}, u32[]{:S(2)}) %all-to-all-start.3) | async-done | bytes 98336 | tf_op jit(solution)/shard_map/all_to_all | solution.py:423
  95.5 0.0 copy-done
  95.6 0.0 copy-done.4
  95.6 1.4 %shard_map.129 = f32[4,4,320]{2,1,0:T(4,128)} custom-call(s32[1]{0:T(128)} %bitcast.13.own_ref, f32[16,4,384]{2,1,0:T(4,128)S(1)} %all-to-all-done.3.in_ref, bf16[16,320]{1,0:T(8,128)(2,1)S(1)} %get-tuple-element.42.q_ref, bf16[2,16,320]{2,1,0:T(8,128)(2,1)S(1)} %copy-done.4, bf16[320,1280]{1,0:T(8,128)(2,1)S(1)} %copy-done), custom_call_target="tpu_custom_call" | custom-call | flops 6553600 | bytes 819200 | tf_op jit(solution)/shard_map/pallas_call | solution.py:295
  96.9 3.3 %all-to-all-start.4 = ((f32[4,4,320]{2,1,0:T(4,128)}), f32[4,4,320]{2,1,0:T(4,128)S(1)}, u32[]{:S(2)}, u32[]{:S(2)}) async-start(f32[4,4,320]{2,1,0:T(4,128)} %shard_map.129), calls=%async_computation.4 | async-start | bytes 49152 | tf_op jit(solution)/shard_map/all_to_all | solution.py:432
  100.2 0.0 collective-permute-done.3.a_ref
  100.2 1.9 %collective-permute-done.4.b_ref = bf16[320,512]{1,0:T(8,128)(2,1)S(1)} collective-permute-done((bf16[320,512]{1,0:T(8,128)(2,1)}, bf16[320,512]{1,0:T(8,128)(2,1)S(1)}, u32[]{:S(2)}, u32[]{:S(2)}) %collective-permute-start.4) | collective-permute-done | bytes 327712 | tf_op jit(solution)/shard_map/ppermute | solution.py:335
  102.1 3.0 %collective-permute-done.5.c_ref = bf16[320,512]{1,0:T(8,128)(2,1)S(1)} collective-permute-done((bf16[320,512]{1,0:T(8,128)(2,1)}, bf16[320,512]{1,0:T(8,128)(2,1)S(1)}, u32[]{:S(2)}, u32[]{:S(2)}) %collective-permute-start.5) | collective-permute-done | bytes 327712 | tf_op jit(solution)/shard_map/ppermute | solution.py:335
  105.2 0.0 copy-start.1
  105.2 1.1 %copy-done.1 = f32[320,512]{1,0:T(8,128)S(1)} copy-done((f32[320,512]{1,0:T(8,128)S(1)}, f32[320,512]{1,0:T(8,128)}, u32[]{:S(2)}) %copy-start.1) | copy-done | bytes 655384
  106.3 0.9 shard_map.127
  107.2 0.0 all-to-all-done.4
  107.2 0.6 reduce_sum.9
Async XLA Ops:
  0.6 32.2 %copy-start.7 = (bf16[512,320]{0,1:T(8,128)(2,1)S(1)}, bf16[512,320]{0,1:T(8,128)(2,1)}, u32[]{:S(2)}) copy-start(bf16[512,320]{0,1:T(8,128)(2,1)} %param.11) | copy-start | bytes 983044
  2.0 14.1 %all-to-all-start = ((bf16[16,4,320]{2,1,0:T(4,128)(2,1)}), bf16[16,4,320]{2,1,0:T(4,128)(2,1)S(1)}, u32[]{:S(2)}, u32[]{:S(2)}) async-start(bf16[16,4,320]{2,1,0:T(4,128)(2,1)} %broadcast_in_dim.2), calls=%async_computation | async-start | bytes 98304 | tf_op jit(solution)/shard_map/all_to_all | solution.py:314
  10.8 40.8 %copy-start.2 = (bf16[640,320]{0,1:T(8,128)(2,1)S(1)}, bf16[640,320]{0,1:T(8,128)(2,1)}, u32[]{:S(2)}) copy-start(bf16[640,320]{0,1:T(8,128)(2,1)} %param.19) | copy-start | bytes 1228804
  10.8 40.8 %copy-start.3 = (bf16[640,320]{0,1:T(8,128)(2,1)S(1)}, bf16[640,320]{0,1:T(8,128)(2,1)}, u32[]{:S(2)}) copy-start(bf16[640,320]{0,1:T(8,128)(2,1)} %param.20) | copy-start | bytes 1228804
  11.6 0.7 copy-start.6
  17.3 0.6 copy-start.5
  17.9 27.1 %all-to-all-start.1 = ((bf16[16,40,128]{2,1,0:T(8,128)(2,1)}), bf16[16,40,128]{2,1,0:T(8,128)(2,1)S(1)}, u32[]{:S(2)}, u32[]{:S(2)}) async-start(bf16[16,40,128]{2,1,0:T(8,128)(2,1)} %get-tuple-element.27), calls=%async_computation.1 | async-start | bytes 327680 | tf_op jit(solution)/shard_map/all_to_all | solution.py:363
  32.8 23.6 %collective-permute-start.2 = (bf16[320,512]{1,0:T(8,128)(2,1)S(1)}, bf16[320,512]{1,0:T(8,128)(2,1)S(1)}, u32[]{:S(2)}, u32[]{:S(2)}) collective-permute-start(bf16[320,512]{1,0:T(8,128)(2,1)S(1)} %bitcast.24), channel_id=1, source_target_pairs={{0,3},{1,0},{2,1},{3,2},{4,7},{5,4},{6,5},{7,6},{8,11},{9,8},{10,9... | collective-permute-start | bytes 983048 | tf_op jit(solution)/shard_map/ppermute | solution.py:335
  35.7 20.7 %collective-permute-start.1 = (bf16[320,512]{1,0:T(8,128)(2,1)S(1)}, bf16[320,512]{1,0:T(8,128)(2,1)S(1)}, u32[]{:S(2)}, u32[]{:S(2)}) collective-permute-start(bf16[320,512]{1,0:T(8,128)(2,1)S(1)} %bitcast.25), channel_id=1, source_target_pairs={{0,2},{1,3},{2,0},{3,1},{4,6},{5,7},{6,4},{7,5},{8,10},{9,11},{10,... | collective-permute-start | bytes 983048 | tf_op jit(solution)/shard_map/ppermute | solution.py:335
  38.7 17.7 %collective-permute-start = (bf16[320,512]{1,0:T(8,128)(2,1)S(1)}, bf16[320,512]{1,0:T(8,128)(2,1)}, u32[]{:S(2)}, u32[]{:S(2)}) collective-permute-start(bf16[320,512]{1,0:T(8,128)(2,1)S(1)} %bitcast.26), channel_id=1, source_target_pairs={{0,1},{1,2},{2,3},{3,0},{4,5},{5,6},{6,7},{7,4},{8,9},{9,10},{10,1... | collective-permute-start | bytes 983048 | tf_op jit(solution)/shard_map/ppermute | solution.py:335
  56.4 4.4 %copy-start.8 = (bf16[320,512]{1,0:T(8,128)(2,1)}, bf16[320,512]{1,0:T(8,128)(2,1)S(1)}, u32[]{:S(2)}) copy-start(bf16[320,512]{1,0:T(8,128)(2,1)S(1)} %collective-permute-done.2.x3_hbm) | copy-start | bytes 983044
  56.4 4.4 %copy-start.9 = (bf16[320,512]{1,0:T(8,128)(2,1)}, bf16[320,512]{1,0:T(8,128)(2,1)S(1)}, u32[]{:S(2)}) copy-start(bf16[320,512]{1,0:T(8,128)(2,1)S(1)} %collective-permute-done.1.x2_hbm) | copy-start | bytes 983044
  56.5 14.8 %all-to-all-start.2 = ((bf16[8,64,384]{2,1,0:T(8,128)(2,1)}), bf16[8,64,384]{2,1,0:T(8,128)(2,1)S(1)}, u32[]{:S(2)}, u32[]{:S(2)}) async-start(bf16[8,64,384]{2,1,0:T(8,128)(2,1)} %bitcast.11), calls=%async_computation.2 | async-start | bytes 786432 | tf_op jit(solution)/shard_map/all_to_all | solution.py:403
  60.9 34.7 %copy-start = (bf16[320,1280]{1,0:T(8,128)(2,1)S(1)}, bf16[320,1280]{1,0:T(8,128)(2,1)}, u32[]{:S(2)}) copy-start(bf16[320,1280]{1,0:T(8,128)(2,1)} %w_ref.1) | copy-start | bytes 2457604
  60.9 34.7 %copy-start.4 = (bf16[2,16,320]{2,1,0:T(8,128)(2,1)S(1)}, bf16[2,16,320]{2,1,0:T(8,128)(2,1)}, u32[]{:S(2)}) copy-start(bf16[2,16,320]{2,1,0:T(8,128)(2,1)} %shard_map.123.kv_ref) | copy-start | bytes 61444
  72.7 22.8 %all-to-all-start.3 = ((f32[16,4,384]{2,1,0:T(4,128)}), f32[16,4,384]{2,1,0:T(4,128)S(1)}, u32[]{:S(2)}, u32[]{:S(2)}) async-start(f32[16,4,384]{2,1,0:T(4,128)} %shard_map.128), calls=%async_computation.3 | async-start | bytes 196608 | tf_op jit(solution)/shard_map/all_to_all | solution.py:423
  83.7 16.5 %collective-permute-start.3 = (bf16[320,512]{1,0:T(8,128)(2,1)}, bf16[320,512]{1,0:T(8,128)(2,1)S(1)}, u32[]{:S(2)}, u32[]{:S(2)}) collective-permute-start(bf16[320,512]{1,0:T(8,128)(2,1)} %get-tuple-element.36), channel_id=1, source_target_pairs={{0,1},{1,2},{2,3},{3,0},{4,5},{5,6},{6,7},{7,4},{8,9},{9,10},{10,1... | collective-permute-start | bytes 983048 | tf_op jit(solution)/shard_map/ppermute | solution.py:335
  85.6 16.5 %collective-permute-start.4 = (bf16[320,512]{1,0:T(8,128)(2,1)}, bf16[320,512]{1,0:T(8,128)(2,1)S(1)}, u32[]{:S(2)}, u32[]{:S(2)}) collective-permute-start(bf16[320,512]{1,0:T(8,128)(2,1)} %get-tuple-element.37), channel_id=1, source_target_pairs={{0,2},{1,3},{2,0},{3,1},{4,6},{5,7},{6,4},{7,5},{8,10},{9,11},{10,... | collective-permute-start | bytes 983048 | tf_op jit(solution)/shard_map/ppermute | solution.py:335
  89.6 15.6 %collective-permute-start.5 = (bf16[320,512]{1,0:T(8,128)(2,1)}, bf16[320,512]{1,0:T(8,128)(2,1)S(1)}, u32[]{:S(2)}, u32[]{:S(2)}) collective-permute-start(bf16[320,512]{1,0:T(8,128)(2,1)} %get-tuple-element.40), channel_id=1, source_target_pairs={{0,3},{1,0},{2,1},{3,2},{4,7},{5,4},{6,5},{7,6},{8,11},{9,8},{10,9... | collective-permute-start | bytes 983048 | tf_op jit(solution)/shard_map/ppermute | solution.py:335
  96.9 10.3 %all-to-all-start.4 = ((f32[4,4,320]{2,1,0:T(4,128)}), f32[4,4,320]{2,1,0:T(4,128)S(1)}, u32[]{:S(2)}, u32[]{:S(2)}) async-start(f32[4,4,320]{2,1,0:T(4,128)} %shard_map.129), calls=%async_computation.4 | async-start | bytes 49152 | tf_op jit(solution)/shard_map/all_to_all | solution.py:432
  105.2 1.1 %copy-start.1 = (f32[320,512]{1,0:T(8,128)S(1)}, f32[320,512]{1,0:T(8,128)}, u32[]{:S(2)}) copy-start(f32[320,512]{1,0:T(8,128)} %get-tuple-element.35.own_ref) | copy-start | bytes 1966084

commit v9 on v8

--- a/solution.py
+++ b/solution.py
@@ -203,7 +203,7 @@
     x_ref, w_ref, kc_ref, vc_ref, wo_ref, wo4_s, gain_s, q_s, k_s, v_s, a_s, own_s, out_s, sems, out_sems,
 ):
     tokens, cached = x_ref.shape[1], kc_ref.shape[1]
-    block = 256
+    block = 512
     me = tp_ref[0]
 
     def place(shift):
@@ -241,26 +241,28 @@
     for t in range(NT):
         wo4_s[t] = wo_ref[:, t * WIDTH : (t + 1) * WIDTH]
     length = len_ref[0]
-    for b in range(tokens // block):
-        cols = slice(b * block, (b + 1) * block)
-        seen = (b + 1) * block
-        in_cache = lax.broadcasted_iota(jnp.int32, (cached, block), 0) < length
-        causal = lax.broadcasted_iota(jnp.int32, (seen, block), 0) <= (
-            lax.broadcasted_iota(jnp.int32, (seen, block), 1) + b * block
-        )
-        for h in range(HEADS):
-            feats = slice(h * HD, (h + 1) * HD)
-            query = q_s[feats, cols]
-            s_old = jnp.where(in_cache, dot(kc_ref[feats, :], query, ((0,), (0,))), MASKED)
-            s_new = jnp.where(causal, dot(k_s[feats, 0:seen], query, ((0,), (0,))), MASKED)
-            top = jnp.maximum(
-                jnp.max(s_old, axis=0, keepdims=True), jnp.max(s_new, axis=0, keepdims=True)
-            )
-            w_old = jnp.exp2((s_old - top) * LOG2E_SCALE)
-            w_new = jnp.exp2((s_new - top) * LOG2E_SCALE)
-            total = jnp.sum(w_old, axis=0, keepdims=True) + jnp.sum(w_new, axis=0, keepdims=True)
-            mixed = dot(vc_ref[feats, :], w_old.astype(BF16), ((1,), (0,))) + dot(
-                v_s[feats, 0:seen], w_new.astype(BF16), ((1,), (0,))
+    half = tokens // 2
+    in_cache = lax.broadcasted_iota(jnp.int32, (cached, tokens), 0) < length
+    causal = lax.broadcasted_iota(jnp.int32, (half, half), 0) <= lax.broadcasted_iota(
+        jnp.int32, (half, half), 1
+    )
+    for h in range(HEADS):
+        feats = slice(h * HD, (h + 1) * HD)
+        old = jnp.where(in_cache, dot(kc_ref[feats, :], q_s[feats, :], ((0,), (0,))), MASKED)
+        low = dot(k_s[feats, 0:half], q_s[feats, :], ((0,), (0,)))
+        high = dot(k_s[feats, half:tokens], q_s[feats, half:tokens], ((0,), (0,)))
+        first = [old[:, 0:half], jnp.where(causal, low[:, 0:half], MASKED)]
+        second = [old[:, half:tokens], low[:, half:tokens], jnp.where(causal, high, MASKED)]
+        for scores, cols in ((first, slice(0, half)), (second, slice(half, tokens))):
+            top = jnp.max(scores[0], axis=0, keepdims=True)
+            for part in scores[1:]:
+                top = jnp.maximum(top, jnp.max(part, axis=0, keepdims=True))
+            weights = [jnp.exp2((part - top) * LOG2E_SCALE) for part in scores]
+            total = sum(jnp.sum(part, axis=0, keepdims=True) for part in weights)
+            values = [vc_ref[feats, :], v_s[feats, 0:half], v_s[feats, half:tokens]]
+            mixed = sum(
+                dot(value, weight.astype(BF16), ((1,), (0,)))
+                for value, weight in zip(values, weights)
             )
             a_s[feats, cols] = (mixed / total).astype(BF16)
     sends = []
@@ -403,7 +405,7 @@
     partial = lax.all_to_all(partial.reshape(NX * NC, NZ * 4, LANES), ("x", "c"), 0, 0, tiled=True)
     term_blocks = list(term_blocks)
     term_blocks[-1], partial = lax.optimization_barrier((term_blocks[-1], partial))
-    arrived = [turned(block, shift) for shift, block in enumerate(term_blocks) if shift > 0]
+    arrived = [turned(term_blocks[shift], shift) for shift in (2, 1, 3)]
     pre_out = call(
         add_terms_kernel,
         shape((WIDTH, tokens), BF16),

time: 109 us -> 107 us (0.982)
  waiting for transfers between devices: 12 us -> 10.1 us
  Pallas kernels: 24.1 us -> 22.8 us
    ppermute x6, waiting for transfers between devices: 5 us -> 3.65 us  [turned(): return lax.ppermute(block, 'tp', [(t, (t + shift) % NT) for t in range(NT)])]
    pallas_call x8, Pallas kernels: 24.1 us -> 22.8 us  [call(): pl.pallas_call(kernel, out_shape=out_shape, in_specs=[pl.BlockSpec(memory...]
  transfers between devices with their start and end apart: 11 -> 11, of which waited for: 5 -> 4; matrix products, arithmetic and copies ran while one was open for 2% -> 2% of each run, Pallas kernels for 20% -> 19%
where the time goes in v9:
time: 107 us; the launch traced here: 105 us
  starting transfers between devices  57.9 us (54%)
  Pallas kernels  22.8 us (21%)
  waiting for transfers between devices  10.1 us (9%)
  blocking collectives  6.64 us (6%)
  local copies, waits for them, and re-layouts  5.76 us (5%)
  between operations  1.5 us (1%)
    pallas_call x8, Pallas kernels, call(): pl.pallas_call(kernel, out_shape=out_shape, in_specs=[pl.BlockSpec(memory...  22.8 us
    ppermute x6, starting transfers between devices, turned(): return lax.ppermute(block, 'tp', [(t, (t + shift) % NT) for t in range(NT)])  17.4 us
    all_to_all x1, starting transfers between devices, body(): queries = lax.all_to_all(queries, 'z', 0, 0, tiled=True)  14.9 us
    all_to_all x1, starting transfers between devices, body(): partial = lax.all_to_all(partial, 'z', 0, 0, tiled=True)  11 us
    all_to_all x1, starting transfers between devices, spread(): return lax.all_to_all(copies, axes, 0, 0, tiled=True)  7.58 us
    all_gather x1, blocking collectives, body(): queries = lax.all_gather(queries, 'c', axis=0, tiled=True)  6.64 us
    all_to_all x1, starting transfers between devices, body(): lax.all_to_all(partial.reshape(NX * NC, NZ * 4, LANES), ('x', 'c'), 0, 0,...  3.74 us
    ppermute x6, waiting for transfers between devices, turned(): return lax.ppermute(block, 'tp', [(t, (t + shift) % NT) for t in range(NT)])  3.65 us
  transfers between devices with their start and end apart: 11, of which 4 were waited for; matrix products, arithmetic and copies ran while one was open for 2% of the time, Pallas kernels for 19%

profile of v9, /device:TPU:1, one launch (start us, length us, event | category | flops | bytes accessed | tf_op | source)
XLA Modules:
  0.0 105.2 jit_solution(18410361647834045481)
XLA Ops:
  0.6 0.0 copy-start.7
  0.6 1.4 %broadcast_in_dim.2 = bf16[16,4,320]{2,1,0:T(4,128)(2,1)} broadcast(bf16[4,320]{1,0:T(4,128)(2,1)} %param.12), dimensions={1,2} | broadcast | bytes 43520 | tf_op jit(solution)/shard_map/broadcast_in_dim | solution.py:315
  2.0 7.6 %all-to-all-start = ((bf16[16,4,320]{2,1,0:T(4,128)(2,1)}), bf16[16,4,320]{2,1,0:T(4,128)(2,1)S(1)}, u32[]{:S(2)}, u32[]{:S(2)}) async-start(bf16[16,4,320]{2,1,0:T(4,128)(2,1)} %broadcast_in_dim.2), calls=%async_computation | async-start | bytes 98304 | tf_op jit(solution)/shard_map/all_to_all | solution.py:316
  9.6 1.2 %slice_bitcast_fusion.w_ref = bf16[320,1280]{1,0:T(8,128)(2,1)S(1)} fusion(bf16[3,320,1280]{2,1,0:T(8,128)(2,1)} %bitcast.18), kind=kLoop, calls=%fused_computation | loop fusion | bytes 1638400 | tf_op jit(solution)/shard_map/squeeze | solution.py:348
  10.8 0.0 copy-start.2
  10.8 0.0 copy-start.3
  10.8 0.8 reshape.28.gain_ref
  11.6 0.0 copy-start.6
  11.6 0.7 copy-done.6
  12.3 0.6 shard_map.124
  12.9 3.2 %all-to-all-done.x_ref = bf16[16,4,320]{2,1,0:T(4,128)(2,1)S(1)} async-done(((bf16[16,4,320]{2,1,0:T(4,128)(2,1)}), bf16[16,4,320]{2,1,0:T(4,128)(2,1)S(1)}, u32[]{:S(2)}, u32[]{:S(2)}) %all-to-all-start) | async-done | bytes 40992 | tf_op jit(solution)/shard_map/all_to_all | solution.py:316
  16.1 1.2 %shard_map.122 = (bf16[16,40,128]{2,1,0:T(8,128)(2,1)}, bf16[16,320]{1,0:T(8,128)(2,1)S(1)}, bf16[16,1280]{1,0:T(8,128)(2,1)S(1)}) custom-call(bf16[16,4,320]{2,1,0:T(4,128)(2,1)S(1)} %all-to-all-done.x_ref, f32[1,1280]{1,0:T(1,128)S(1)} %reshape.28.gain_ref, bf16[320,1280]{1,0:T(8,128)(2,1)S(1)} %slice_bitcast_fusion.w_ref), custom_call_target="tpu_custom_call" | custom-call | flops 13107200 | bytes 819200 | tf_op jit(solution)/shard_map/pallas_call | solution.py:297
  17.3 0.0 copy-start.5
  17.3 0.6 copy-done.5
  17.9 14.9 %all-to-all-start.1 = ((bf16[16,40,128]{2,1,0:T(8,128)(2,1)}), bf16[16,40,128]{2,1,0:T(8,128)(2,1)S(1)}, u32[]{:S(2)}, u32[]{:S(2)}) async-start(bf16[16,40,128]{2,1,0:T(8,128)(2,1)} %get-tuple-element.27), calls=%async_computation.1 | async-start | bytes 327680 | tf_op jit(solution)/shard_map/all_to_all | solution.py:365
  32.8 0.0 copy-done.7
  32.8 2.9 %collective-permute-start.2 = (bf16[320,512]{1,0:T(8,128)(2,1)S(1)}, bf16[320,512]{1,0:T(8,128)(2,1)S(1)}, u32[]{:S(2)}, u32[]{:S(2)}) collective-permute-start(bf16[320,512]{1,0:T(8,128)(2,1)S(1)} %bitcast.24), channel_id=1, source_target_pairs={{0,3},{1,0},{2,1},{3,2},{4,7},{5,4},{6,5},{7,6},{8,11},{9,8},{10,9... | collective-permute-start | bytes 983048 | tf_op jit(solution)/shard_map/ppermute | solution.py:337
  35.7 3.0 %collective-permute-start.1 = (bf16[320,512]{1,0:T(8,128)(2,1)S(1)}, bf16[320,512]{1,0:T(8,128)(2,1)S(1)}, u32[]{:S(2)}, u32[]{:S(2)}) collective-permute-start(bf16[320,512]{1,0:T(8,128)(2,1)S(1)} %bitcast.25), channel_id=1, source_target_pairs={{0,2},{1,3},{2,0},{3,1},{4,6},{5,7},{6,4},{7,5},{8,10},{9,11},{10,... | collective-permute-start | bytes 983048 | tf_op jit(solution)/shard_map/ppermute | solution.py:337
  38.7 1.9 %collective-permute-start = (bf16[320,512]{1,0:T(8,128)(2,1)S(1)}, bf16[320,512]{1,0:T(8,128)(2,1)}, u32[]{:S(2)}, u32[]{:S(2)}) collective-permute-start(bf16[320,512]{1,0:T(8,128)(2,1)S(1)} %bitcast.26), channel_id=1, source_target_pairs={{0,1},{1,2},{2,3},{3,0},{4,5},{5,6},{6,7},{7,4},{8,9},{9,10},{10,1... | collective-permute-start | bytes 983048 | tf_op jit(solution)/shard_map/ppermute | solution.py:337
  40.7 3.5 %shard_map.123.kv_ref = bf16[2,16,320]{2,1,0:T(8,128)(2,1)} custom-call(bf16[16,1280]{1,0:T(8,128)(2,1)} %copy-done.5, bf16[3,320,1280]{2,1,0:T(8,128)(2,1)} %bitcast.19), custom_call_target="tpu_custom_call" | custom-call | flops 26214400 | bytes 1638400 | tf_op jit(solution)/shard_map/pallas_call | solution.py:297
  44.1 0.8 all-to-all-done.1
  45.0 6.6 %all_gather.3.qp_ref = bf16[32,40,128]{2,1,0:T(8,128)(2,1)S(1)} all-gather(bf16[16,40,128]{2,1,0:T(8,128)(2,1)S(1)} %all-to-all-done.1), channel_id=1, replica_groups=mesh['x'=4,'z'=16,'c'=2,'tp'=4] {'c'}, dimensions={0}, use_global_device_ids=true | all-gather | bytes 491520 | tf_op jit(solution)/shard_map/all_gather | solution.py:367
  51.6 0.0 copy-done.2
  51.6 0.0 copy-done.3
  51.6 4.8 %shard_map.125 = bf16[512,384]{1,0:T(8,128)(2,1)} custom-call(bf16[32,40,128]{2,1,0:T(8,128)(2,1)S(1)} %all_gather.3.qp_ref, f32[512,2]{1,0:T(8,128)S(1)} %get-tuple-element.29.bounds_ref, bf16[512,512]{1,0:T(8,128)(2,1)S(1)} %get-tuple-element.30.order_ref, bf16[320,640]{1,0:T(8,128)(2,1)S(1)} %bitcast.15, bf16[320,640]{1,0:T(8,128)(2,1)S(1)} %bitcast.16), custom_call_target="tpu_custom_call" | custom-call | flops 419430400 | bytes 819200 | tf_op jit(solution)/shard_map/pallas_call | solution.py:297
  56.4 0.0 collective-permute-done.2.x3_hbm
  56.4 0.0 copy-start.8
  56.4 0.0 collective-permute-done.1.x2_hbm
  56.4 0.0 copy-start.9
  56.4 0.0 collective-permute-done.x1_hbm
  56.5 3.7 %all-to-all-start.2 = ((bf16[8,64,384]{2,1,0:T(8,128)(2,1)}), bf16[8,64,384]{2,1,0:T(8,128)(2,1)S(1)}, u32[]{:S(2)}, u32[]{:S(2)}) async-start(bf16[8,64,384]{2,1,0:T(8,128)(2,1)} %bitcast.11), calls=%async_computation.2 | async-start | bytes 786432 | tf_op jit(solution)/shard_map/all_to_all | solution.py:405
  60.8 0.0 copy-done.8
  60.9 0.0 copy-done.9
  60.9 0.0 copy-start
  60.9 0.0 copy-start.4
  60.9 9.1 %shard_map.126 = (f32[320,512]{1,0:T(8,128)}, bf16[320,512]{1,0:T(8,128)(2,1)}, bf16[320,512]{1,0:T(8,128)(2,1)}, bf16[320,512]{1,0:T(8,128)(2,1)}) custom-call(s32[1]{0:T(128)S(6)} %copy.13.len_ref, s32[1]{0:T(128)} %bitcast.tp_ref, f32[10,128]{1,0:T(8,128)} %bitcast.22, bf16[320,512]{1,0:T(8,128)(2,1)} %bitcast.23, ...), custom_call_target="tpu_custom_call" | custom-call | flops 2264924160 | bytes 3276800 | tf_op jit(solution)/shard_map/pallas_call | solution.py:297
  69.9 0.0 all-to-all-done.2.in_ref
  70.0 1.4 %shard_map.128 = f32[16,4,384]{2,1,0:T(4,128)} custom-call(bf16[8,64,384]{2,1,0:T(8,128)(2,1)S(1)} %all-to-all-done.2.in_ref), custom_call_target="tpu_custom_call" | custom-call | flops 196608 | bytes 786432 | tf_op jit(solution)/shard_map/pallas_call | solution.py:297
  71.4 11.0 %all-to-all-start.3 = ((f32[16,4,384]{2,1,0:T(4,128)}), f32[16,4,384]{2,1,0:T(4,128)S(1)}, u32[]{:S(2)}, u32[]{:S(2)}) async-start(f32[16,4,384]{2,1,0:T(4,128)} %shard_map.128), calls=%async_computation.3 | async-start | bytes 196608 | tf_op jit(solution)/shard_map/all_to_all | solution.py:425
  82.4 3.1 %collective-permute-start.3 = (bf16[320,512]{1,0:T(8,128)(2,1)}, bf16[320,512]{1,0:T(8,128)(2,1)S(1)}, u32[]{:S(2)}, u32[]{:S(2)}) collective-permute-start(bf16[320,512]{1,0:T(8,128)(2,1)} %get-tuple-element.36), channel_id=1, source_target_pairs={{0,2},{1,3},{2,0},{3,1},{4,6},{5,7},{6,4},{7,5},{8,10},{9,11},{10,... | collective-permute-start | bytes 983048 | tf_op jit(solution)/shard_map/ppermute | solution.py:337
  85.4 2.2 %collective-permute-start.4 = (bf16[320,512]{1,0:T(8,128)(2,1)}, bf16[320,512]{1,0:T(8,128)(2,1)S(1)}, u32[]{:S(2)}, u32[]{:S(2)}) collective-permute-start(bf16[320,512]{1,0:T(8,128)(2,1)} %get-tuple-element.37), channel_id=1, source_target_pairs={{0,1},{1,2},{2,3},{3,0},{4,5},{5,6},{6,7},{7,4},{8,9},{9,10},{10,1... | collective-permute-start | bytes 983048 | tf_op jit(solution)/shard_map/ppermute | solution.py:337
  87.6 4.3 %collective-permute-start.5 = (bf16[320,512]{1,0:T(8,128)(2,1)}, bf16[320,512]{1,0:T(8,128)(2,1)S(1)}, u32[]{:S(2)}, u32[]{:S(2)}) collective-permute-start(bf16[320,512]{1,0:T(8,128)(2,1)} %get-tuple-element.40), channel_id=1, source_target_pairs={{0,3},{1,0},{2,1},{3,2},{4,7},{5,4},{6,5},{7,6},{8,11},{9,8},{10,9... | collective-permute-start | bytes 983048 | tf_op jit(solution)/shard_map/ppermute | solution.py:337
  91.9 2.4 %all-to-all-done.3.in_ref = f32[16,4,384]{2,1,0:T(4,128)S(1)} async-done(((f32[16,4,384]{2,1,0:T(4,128)}), f32[16,4,384]{2,1,0:T(4,128)S(1)}, u32[]{:S(2)}, u32[]{:S(2)}) %all-to-all-start.3) | async-done | bytes 98336 | tf_op jit(solution)/shard_map/all_to_all | solution.py:425
  94.4 0.0 copy-done
  94.4 0.0 copy-done.4
  94.4 1.4 %shard_map.129 = f32[4,4,320]{2,1,0:T(4,128)} custom-call(s32[1]{0:T(128)} %bitcast.13.own_ref, f32[16,4,384]{2,1,0:T(4,128)S(1)} %all-to-all-done.3.in_ref, bf16[16,320]{1,0:T(8,128)(2,1)S(1)} %get-tuple-element.42.q_ref, bf16[2,16,320]{2,1,0:T(8,128)(2,1)S(1)} %copy-done.4, bf16[320,1280]{1,0:T(8,128)(2,1)S(1)} %copy-done), custom_call_target="tpu_custom_call" | custom-call | flops 6553600 | bytes 819200 | tf_op jit(solution)/shard_map/pallas_call | solution.py:297
  95.7 3.3 %all-to-all-start.4 = ((f32[4,4,320]{2,1,0:T(4,128)}), f32[4,4,320]{2,1,0:T(4,128)S(1)}, u32[]{:S(2)}, u32[]{:S(2)}) async-start(f32[4,4,320]{2,1,0:T(4,128)} %shard_map.129), calls=%async_computation.4 | async-start | bytes 49152 | tf_op jit(solution)/shard_map/all_to_all | solution.py:434
  99.0 0.0 collective-permute-done.3.a_ref
  99.0 3.6 %collective-permute-done.4.b_ref = bf16[320,512]{1,0:T(8,128)(2,1)S(1)} collective-permute-done((bf16[320,512]{1,0:T(8,128)(2,1)}, bf16[320,512]{1,0:T(8,128)(2,1)S(1)}, u32[]{:S(2)}, u32[]{:S(2)}) %collective-permute-start.4) | collective-permute-done | bytes 327712 | tf_op jit(solution)/shard_map/ppermute | solution.py:337
  102.6 0.0 collective-permute-done.5.c_ref
  102.6 0.0 copy-start.1
  102.6 1.1 %copy-done.1 = f32[320,512]{1,0:T(8,128)S(1)} copy-done((f32[320,512]{1,0:T(8,128)S(1)}, f32[320,512]{1,0:T(8,128)}, u32[]{:S(2)}) %copy-start.1) | copy-done | bytes 655384
  103.7 0.9 shard_map.127
  104.6 0.0 all-to-all-done.4
  104.6 0.6 reduce_sum.9
Async XLA Ops:
  0.6 32.2 %copy-start.7 = (bf16[512,320]{0,1:T(8,128)(2,1)S(1)}, bf16[512,320]{0,1:T(8,128)(2,1)}, u32[]{:S(2)}) copy-start(bf16[512,320]{0,1:T(8,128)(2,1)} %param.11) | copy-start | bytes 983044
  2.0 14.1 %all-to-all-start = ((bf16[16,4,320]{2,1,0:T(4,128)(2,1)}), bf16[16,4,320]{2,1,0:T(4,128)(2,1)S(1)}, u32[]{:S(2)}, u32[]{:S(2)}) async-start(bf16[16,4,320]{2,1,0:T(4,128)(2,1)} %broadcast_in_dim.2), calls=%async_computation | async-start | bytes 98304 | tf_op jit(solution)/shard_map/all_to_all | solution.py:316
  10.8 40.8 %copy-start.2 = (bf16[640,320]{0,1:T(8,128)(2,1)S(1)}, bf16[640,320]{0,1:T(8,128)(2,1)}, u32[]{:S(2)}) copy-start(bf16[640,320]{0,1:T(8,128)(2,1)} %param.19) | copy-start | bytes 1228804
  10.8 40.8 %copy-start.3 = (bf16[640,320]{0,1:T(8,128)(2,1)S(1)}, bf16[640,320]{0,1:T(8,128)(2,1)}, u32[]{:S(2)}) copy-start(bf16[640,320]{0,1:T(8,128)(2,1)} %param.20) | copy-start | bytes 1228804
  11.6 0.7 copy-start.6
  17.3 0.6 copy-start.5
  17.9 27.1 %all-to-all-start.1 = ((bf16[16,40,128]{2,1,0:T(8,128)(2,1)}), bf16[16,40,128]{2,1,0:T(8,128)(2,1)S(1)}, u32[]{:S(2)}, u32[]{:S(2)}) async-start(bf16[16,40,128]{2,1,0:T(8,128)(2,1)} %get-tuple-element.27), calls=%async_computation.1 | async-start | bytes 327680 | tf_op jit(solution)/shard_map/all_to_all | solution.py:365
  32.8 23.6 %collective-permute-start.2 = (bf16[320,512]{1,0:T(8,128)(2,1)S(1)}, bf16[320,512]{1,0:T(8,128)(2,1)S(1)}, u32[]{:S(2)}, u32[]{:S(2)}) collective-permute-start(bf16[320,512]{1,0:T(8,128)(2,1)S(1)} %bitcast.24), channel_id=1, source_target_pairs={{0,3},{1,0},{2,1},{3,2},{4,7},{5,4},{6,5},{7,6},{8,11},{9,8},{10,9... | collective-permute-start | bytes 983048 | tf_op jit(solution)/shard_map/ppermute | solution.py:337
  35.7 20.7 %collective-permute-start.1 = (bf16[320,512]{1,0:T(8,128)(2,1)S(1)}, bf16[320,512]{1,0:T(8,128)(2,1)S(1)}, u32[]{:S(2)}, u32[]{:S(2)}) collective-permute-start(bf16[320,512]{1,0:T(8,128)(2,1)S(1)} %bitcast.25), channel_id=1, source_target_pairs={{0,2},{1,3},{2,0},{3,1},{4,6},{5,7},{6,4},{7,5},{8,10},{9,11},{10,... | collective-permute-start | bytes 983048 | tf_op jit(solution)/shard_map/ppermute | solution.py:337
  38.7 17.7 %collective-permute-start = (bf16[320,512]{1,0:T(8,128)(2,1)S(1)}, bf16[320,512]{1,0:T(8,128)(2,1)}, u32[]{:S(2)}, u32[]{:S(2)}) collective-permute-start(bf16[320,512]{1,0:T(8,128)(2,1)S(1)} %bitcast.26), channel_id=1, source_target_pairs={{0,1},{1,2},{2,3},{3,0},{4,5},{5,6},{6,7},{7,4},{8,9},{9,10},{10,1... | collective-permute-start | bytes 983048 | tf_op jit(solution)/shard_map/ppermute | solution.py:337
  56.4 4.4 %copy-start.8 = (bf16[320,512]{1,0:T(8,128)(2,1)}, bf16[320,512]{1,0:T(8,128)(2,1)S(1)}, u32[]{:S(2)}) copy-start(bf16[320,512]{1,0:T(8,128)(2,1)S(1)} %collective-permute-done.2.x3_hbm) | copy-start | bytes 983044
  56.4 4.4 %copy-start.9 = (bf16[320,512]{1,0:T(8,128)(2,1)}, bf16[320,512]{1,0:T(8,128)(2,1)S(1)}, u32[]{:S(2)}) copy-start(bf16[320,512]{1,0:T(8,128)(2,1)S(1)} %collective-permute-done.1.x2_hbm) | copy-start | bytes 983044
  56.5 13.5 %all-to-all-start.2 = ((bf16[8,64,384]{2,1,0:T(8,128)(2,1)}), bf16[8,64,384]{2,1,0:T(8,128)(2,1)S(1)}, u32[]{:S(2)}, u32[]{:S(2)}) async-start(bf16[8,64,384]{2,1,0:T(8,128)(2,1)} %bitcast.11), calls=%async_computation.2 | async-start | bytes 786432 | tf_op jit(solution)/shard_map/all_to_all | solution.py:405
  60.9 33.5 %copy-start = (bf16[320,1280]{1,0:T(8,128)(2,1)S(1)}, bf16[320,1280]{1,0:T(8,128)(2,1)}, u32[]{:S(2)}) copy-start(bf16[320,1280]{1,0:T(8,128)(2,1)} %w_ref.1) | copy-start | bytes 2457604
  60.9 33.5 %copy-start.4 = (bf16[2,16,320]{2,1,0:T(8,128)(2,1)S(1)}, bf16[2,16,320]{2,1,0:T(8,128)(2,1)}, u32[]{:S(2)}) copy-start(bf16[2,16,320]{2,1,0:T(8,128)(2,1)} %shard_map.123.kv_ref) | copy-start | bytes 61444
  71.4 23.0 %all-to-all-start.3 = ((f32[16,4,384]{2,1,0:T(4,128)}), f32[16,4,384]{2,1,0:T(4,128)S(1)}, u32[]{:S(2)}, u32[]{:S(2)}) async-start(f32[16,4,384]{2,1,0:T(4,128)} %shard_map.128), calls=%async_computation.3 | async-start | bytes 196608 | tf_op jit(solution)/shard_map/all_to_all | solution.py:425
  82.4 16.6 %collective-permute-start.3 = (bf16[320,512]{1,0:T(8,128)(2,1)}, bf16[320,512]{1,0:T(8,128)(2,1)S(1)}, u32[]{:S(2)}, u32[]{:S(2)}) collective-permute-start(bf16[320,512]{1,0:T(8,128)(2,1)} %get-tuple-element.36), channel_id=1, source_target_pairs={{0,2},{1,3},{2,0},{3,1},{4,6},{5,7},{6,4},{7,5},{8,10},{9,11},{10,... | collective-permute-start | bytes 983048 | tf_op jit(solution)/shard_map/ppermute | solution.py:337
  85.4 17.2 %collective-permute-start.4 = (bf16[320,512]{1,0:T(8,128)(2,1)}, bf16[320,512]{1,0:T(8,128)(2,1)S(1)}, u32[]{:S(2)}, u32[]{:S(2)}) collective-permute-start(bf16[320,512]{1,0:T(8,128)(2,1)} %get-tuple-element.37), channel_id=1, source_target_pairs={{0,1},{1,2},{2,3},{3,0},{4,5},{5,6},{6,7},{7,4},{8,9},{9,10},{10,1... | collective-permute-start | bytes 983048 | tf_op jit(solution)/shard_map/ppermute | solution.py:337
  87.6 15.0 %collective-permute-start.5 = (bf16[320,512]{1,0:T(8,128)(2,1)}, bf16[320,512]{1,0:T(8,128)(2,1)S(1)}, u32[]{:S(2)}, u32[]{:S(2)}) collective-permute-start(bf16[320,512]{1,0:T(8,128)(2,1)} %get-tuple-element.40), channel_id=1, source_target_pairs={{0,3},{1,0},{2,1},{3,2},{4,7},{5,4},{6,5},{7,6},{8,11},{9,8},{10,9... | collective-permute-start | bytes 983048 | tf_op jit(solution)/shard_map/ppermute | solution.py:337
  95.7 8.9 %all-to-all-start.4 = ((f32[4,4,320]{2,1,0:T(4,128)}), f32[4,4,320]{2,1,0:T(4,128)S(1)}, u32[]{:S(2)}, u32[]{:S(2)}) async-start(f32[4,4,320]{2,1,0:T(4,128)} %shard_map.129), calls=%async_computation.4 | async-start | bytes 49152 | tf_op jit(solution)/shard_map/all_to_all | solution.py:434
  102.6 1.1 %copy-start.1 = (f32[320,512]{1,0:T(8,128)S(1)}, f32[320,512]{1,0:T(8,128)}, u32[]{:S(2)}) copy-start(f32[320,512]{1,0:T(8,128)} %get-tuple-element.35.own_ref) | copy-start | bytes 1966084

commit v10 on v9

--- a/solution.py
+++ b/solution.py
@@ -82,7 +82,7 @@
         s = dot(queries[:, h * HD : (h + 1) * HD], k_ref[h * HD : (h + 1) * HD, :], ((1,), (0,)))
         s = jnp.where(allowed, s, MASKED)
         top = jnp.max(s, axis=1, keepdims=True)
-        w = jnp.where(allowed, jnp.exp2((s - top) * LOG2E_SCALE), 0.0)
+        w = jnp.exp2((s - top) * LOG2E_SCALE)
         total = jnp.sum(w, axis=1, keepdims=True)
         mixed = dot(w.astype(BF16), v_ref[h * HD : (h + 1) * HD, :], ((1,), (1,)))
         out_ref[:, h * HD : (h + 1) * HD] = mixed.astype(BF16)
@@ -99,11 +99,17 @@
 
 
 def stats(tops, totals, rows):
-    lane = lax.broadcasted_iota(jnp.int32, (rows, LANES - WIDTH), 1)
-    out = jnp.zeros((rows, LANES - WIDTH), F32)
+    lanes = LANES - WIDTH
+    lane = lax.broadcasted_iota(jnp.int32, (rows, lanes), 1)
+    flat = jnp.zeros((rows, lanes), F32)
     for n, value in enumerate(tops + totals):
-        for k, part in enumerate(thirds(value)):
-            out = jnp.where(lane == 3 * n + k, part.astype(F32), out)
+        flat = jnp.where(lane == n, value, flat)
+    source = lax.broadcasted_iota(jnp.int32, (lanes, lanes), 0)
+    target = lax.broadcasted_iota(jnp.int32, (lanes, lanes), 1)
+    out = jnp.zeros((rows, lanes), F32)
+    for k, part in enumerate(thirds(flat)):
+        move = jnp.where((target == 3 * source + k) & (source < 2 * HEADS), 1.0, 0.0).astype(BF16)
+        out = out + dot(part, move, ((1,), (0,)))
     return out.astype(BF16)
 
 

time: 107 us -> 107 us (level)
  transfers between devices with their start and end apart: 11 -> 11, of which waited for: 4 -> 4; matrix products, arithmetic and copies ran while one was open for 2% -> 2% of each run, Pallas kernels for 19% -> 18%
where the time goes in v10:
time: 107 us; the launch traced here: 105 us
  starting transfers between devices  58.6 us (55%)
  Pallas kernels  21.9 us (20%)
  waiting for transfers between devices  10.2 us (10%)
  blocking collectives  6.64 us (6%)
  local copies, waits for them, and re-layouts  5.76 us (5%)
  between operations  1.5 us (1%)
    pallas_call x8, Pallas kernels, call(): pl.pallas_call(kernel, out_shape=out_shape, in_specs=[pl.BlockSpec(memory...  21.9 us
    ppermute x6, starting transfers between devices, turned(): return lax.ppermute(block, 'tp', [(t, (t + shift) % NT) for t in range(NT)])  17.3 us
    all_to_all x1, starting transfers between devices, body(): queries = lax.all_to_all(queries, 'z', 0, 0, tiled=True)  14.9 us
    all_to_all x1, starting transfers between devices, body(): partial = lax.all_to_all(partial, 'z', 0, 0, tiled=True)  11.5 us
    all_to_all x1, starting transfers between devices, spread(): return lax.all_to_all(copies, axes, 0, 0, tiled=True)  7.58 us
    all_gather x1, blocking collectives, body(): queries = lax.all_gather(queries, 'c', axis=0, tiled=True)  6.64 us
    all_to_all x1, starting transfers between devices, body(): lax.all_to_all(partial.reshape(NX * NC, NZ * 4, LANES), ('x', 'c'), 0, 0,...  4.08 us
    ppermute x6, waiting for transfers between devices, turned(): return lax.ppermute(block, 'tp', [(t, (t + shift) % NT) for t in range(NT)])  3.65 us
  transfers between devices with their start and end apart: 11, of which 4 were waited for; matrix products, arithmetic and copies ran while one was open for 2% of the time, Pallas kernels for 18%

profile of v10, /device:TPU:1, one launch (start us, length us, event | category | flops | bytes accessed | tf_op | source)
XLA Modules:
  0.0 105.2 jit_solution(14936218120945548998)
XLA Ops:
  0.6 0.0 copy-start.7
  0.6 1.4 %broadcast_in_dim.2 = bf16[16,4,320]{2,1,0:T(4,128)(2,1)} broadcast(bf16[4,320]{1,0:T(4,128)(2,1)} %param.12), dimensions={1,2} | broadcast | bytes 43520 | tf_op jit(solution)/shard_map/broadcast_in_dim | solution.py:321
  2.0 7.6 %all-to-all-start = ((bf16[16,4,320]{2,1,0:T(4,128)(2,1)}), bf16[16,4,320]{2,1,0:T(4,128)(2,1)S(1)}, u32[]{:S(2)}, u32[]{:S(2)}) async-start(bf16[16,4,320]{2,1,0:T(4,128)(2,1)} %broadcast_in_dim.2), calls=%async_computation | async-start | bytes 98304 | tf_op jit(solution)/shard_map/all_to_all | solution.py:322
  9.6 1.2 %slice_bitcast_fusion.w_ref = bf16[320,1280]{1,0:T(8,128)(2,1)S(1)} fusion(bf16[3,320,1280]{2,1,0:T(8,128)(2,1)} %bitcast.18), kind=kLoop, calls=%fused_computation | loop fusion | bytes 1638400 | tf_op jit(solution)/shard_map/squeeze | solution.py:354
  10.8 0.0 copy-start.2
  10.8 0.0 copy-start.3
  10.8 0.8 reshape.28.gain_ref
  11.6 0.0 copy-start.6
  11.6 0.7 copy-done.6
  12.3 0.6 shard_map.124
  12.9 3.2 %all-to-all-done.x_ref = bf16[16,4,320]{2,1,0:T(4,128)(2,1)S(1)} async-done(((bf16[16,4,320]{2,1,0:T(4,128)(2,1)}), bf16[16,4,320]{2,1,0:T(4,128)(2,1)S(1)}, u32[]{:S(2)}, u32[]{:S(2)}) %all-to-all-start) | async-done | bytes 40992 | tf_op jit(solution)/shard_map/all_to_all | solution.py:322
  16.1 1.2 %shard_map.122 = (bf16[16,40,128]{2,1,0:T(8,128)(2,1)}, bf16[16,320]{1,0:T(8,128)(2,1)S(1)}, bf16[16,1280]{1,0:T(8,128)(2,1)S(1)}) custom-call(bf16[16,4,320]{2,1,0:T(4,128)(2,1)S(1)} %all-to-all-done.x_ref, f32[1,1280]{1,0:T(1,128)S(1)} %reshape.28.gain_ref, bf16[320,1280]{1,0:T(8,128)(2,1)S(1)} %slice_bitcast_fusion.w_ref), custom_call_target="tpu_custom_call" | custom-call | flops 13107200 | bytes 819200 | tf_op jit(solution)/shard_map/pallas_call | solution.py:303
  17.3 0.0 copy-start.5
  17.3 0.6 copy-done.5
  17.9 14.9 %all-to-all-start.1 = ((bf16[16,40,128]{2,1,0:T(8,128)(2,1)}), bf16[16,40,128]{2,1,0:T(8,128)(2,1)S(1)}, u32[]{:S(2)}, u32[]{:S(2)}) async-start(bf16[16,40,128]{2,1,0:T(8,128)(2,1)} %get-tuple-element.27), calls=%async_computation.1 | async-start | bytes 327680 | tf_op jit(solution)/shard_map/all_to_all | solution.py:371
  32.8 0.0 copy-done.7
  32.8 2.9 %collective-permute-start.2 = (bf16[320,512]{1,0:T(8,128)(2,1)S(1)}, bf16[320,512]{1,0:T(8,128)(2,1)S(1)}, u32[]{:S(2)}, u32[]{:S(2)}) collective-permute-start(bf16[320,512]{1,0:T(8,128)(2,1)S(1)} %bitcast.24), channel_id=1, source_target_pairs={{0,3},{1,0},{2,1},{3,2},{4,7},{5,4},{6,5},{7,6},{8,11},{9,8},{10,9... | collective-permute-start | bytes 983048 | tf_op jit(solution)/shard_map/ppermute | solution.py:343
  35.7 3.0 %collective-permute-start.1 = (bf16[320,512]{1,0:T(8,128)(2,1)S(1)}, bf16[320,512]{1,0:T(8,128)(2,1)S(1)}, u32[]{:S(2)}, u32[]{:S(2)}) collective-permute-start(bf16[320,512]{1,0:T(8,128)(2,1)S(1)} %bitcast.25), channel_id=1, source_target_pairs={{0,2},{1,3},{2,0},{3,1},{4,6},{5,7},{6,4},{7,5},{8,10},{9,11},{10,... | collective-permute-start | bytes 983048 | tf_op jit(solution)/shard_map/ppermute | solution.py:343
  38.7 1.9 %collective-permute-start = (bf16[320,512]{1,0:T(8,128)(2,1)S(1)}, bf16[320,512]{1,0:T(8,128)(2,1)}, u32[]{:S(2)}, u32[]{:S(2)}) collective-permute-start(bf16[320,512]{1,0:T(8,128)(2,1)S(1)} %bitcast.26), channel_id=1, source_target_pairs={{0,1},{1,2},{2,3},{3,0},{4,5},{5,6},{6,7},{7,4},{8,9},{9,10},{10,1... | collective-permute-start | bytes 983048 | tf_op jit(solution)/shard_map/ppermute | solution.py:343
  40.7 3.5 %shard_map.123.kv_ref = bf16[2,16,320]{2,1,0:T(8,128)(2,1)} custom-call(bf16[16,1280]{1,0:T(8,128)(2,1)} %copy-done.5, bf16[3,320,1280]{2,1,0:T(8,128)(2,1)} %bitcast.19), custom_call_target="tpu_custom_call" | custom-call | flops 26214400 | bytes 1638400 | tf_op jit(solution)/shard_map/pallas_call | solution.py:303
  44.1 0.8 all-to-all-done.1
  45.0 6.6 %all_gather.3.qp_ref = bf16[32,40,128]{2,1,0:T(8,128)(2,1)S(1)} all-gather(bf16[16,40,128]{2,1,0:T(8,128)(2,1)S(1)} %all-to-all-done.1), channel_id=1, replica_groups=mesh['x'=4,'z'=16,'c'=2,'tp'=4] {'c'}, dimensions={0}, use_global_device_ids=true | all-gather | bytes 491520 | tf_op jit(solution)/shard_map/all_gather | solution.py:373
  51.6 0.0 copy-done.2
  51.6 0.0 copy-done.3
  51.6 4.0 %shard_map.125 = bf16[512,384]{1,0:T(8,128)(2,1)} custom-call(bf16[32,40,128]{2,1,0:T(8,128)(2,1)S(1)} %all_gather.3.qp_ref, f32[512,2]{1,0:T(8,128)S(1)} %get-tuple-element.29.bounds_ref, bf16[512,512]{1,0:T(8,128)(2,1)S(1)} %get-tuple-element.30.order_ref, bf16[320,640]{1,0:T(8,128)(2,1)S(1)} %bitcast.15, bf16[320,640]{1,0:T(8,128)(2,1)S(1)} %bitcast.16), custom_call_target="tpu_custom_call" | custom-call | flops 419430400 | bytes 819200 | tf_op jit(solution)/shard_map/pallas_call | solution.py:303
  55.6 0.0 collective-permute-done.2.x3_hbm
  55.6 0.0 copy-start.8
  55.6 0.0 collective-permute-done.1.x2_hbm
  55.6 0.0 copy-start.9
  55.6 0.0 collective-permute-done.x1_hbm
  55.6 4.1 %all-to-all-start.2 = ((bf16[8,64,384]{2,1,0:T(8,128)(2,1)}), bf16[8,64,384]{2,1,0:T(8,128)(2,1)S(1)}, u32[]{:S(2)}, u32[]{:S(2)}) async-start(bf16[8,64,384]{2,1,0:T(8,128)(2,1)} %bitcast.11), calls=%async_computation.2 | async-start | bytes 786432 | tf_op jit(solution)/shard_map/all_to_all | solution.py:411
  60.4 0.0 copy-done.8
  60.4 0.0 copy-done.9
  60.4 0.0 copy-start
  60.4 0.0 copy-start.4
  60.4 9.1 %shard_map.126 = (f32[320,512]{1,0:T(8,128)}, bf16[320,512]{1,0:T(8,128)(2,1)}, bf16[320,512]{1,0:T(8,128)(2,1)}, bf16[320,512]{1,0:T(8,128)(2,1)}) custom-call(s32[1]{0:T(128)S(6)} %copy.13.len_ref, s32[1]{0:T(128)} %bitcast.tp_ref, f32[10,128]{1,0:T(8,128)} %bitcast.22, bf16[320,512]{1,0:T(8,128)(2,1)} %bitcast.23, ...), custom_call_target="tpu_custom_call" | custom-call | flops 2264924160 | bytes 3276800 | tf_op jit(solution)/shard_map/pallas_call | solution.py:303
  69.5 0.0 all-to-all-done.2.in_ref
  69.5 1.4 %shard_map.128 = f32[16,4,384]{2,1,0:T(4,128)} custom-call(bf16[8,64,384]{2,1,0:T(8,128)(2,1)S(1)} %all-to-all-done.2.in_ref), custom_call_target="tpu_custom_call" | custom-call | flops 196608 | bytes 786432 | tf_op jit(solution)/shard_map/pallas_call | solution.py:303
  70.9 11.5 %all-to-all-start.3 = ((f32[16,4,384]{2,1,0:T(4,128)}), f32[16,4,384]{2,1,0:T(4,128)S(1)}, u32[]{:S(2)}, u32[]{:S(2)}) async-start(f32[16,4,384]{2,1,0:T(4,128)} %shard_map.128), calls=%async_computation.3 | async-start | bytes 196608 | tf_op jit(solution)/shard_map/all_to_all | solution.py:431
  82.4 3.0 %collective-permute-start.3 = (bf16[320,512]{1,0:T(8,128)(2,1)}, bf16[320,512]{1,0:T(8,128)(2,1)S(1)}, u32[]{:S(2)}, u32[]{:S(2)}) collective-permute-start(bf16[320,512]{1,0:T(8,128)(2,1)} %get-tuple-element.36), channel_id=1, source_target_pairs={{0,2},{1,3},{2,0},{3,1},{4,6},{5,7},{6,4},{7,5},{8,10},{9,11},{10,... | collective-permute-start | bytes 983048 | tf_op jit(solution)/shard_map/ppermute | solution.py:343
  85.4 1.9 %collective-permute-start.4 = (bf16[320,512]{1,0:T(8,128)(2,1)}, bf16[320,512]{1,0:T(8,128)(2,1)S(1)}, u32[]{:S(2)}, u32[]{:S(2)}) collective-permute-start(bf16[320,512]{1,0:T(8,128)(2,1)} %get-tuple-element.37), channel_id=1, source_target_pairs={{0,1},{1,2},{2,3},{3,0},{4,5},{5,6},{6,7},{7,4},{8,9},{9,10},{10,1... | collective-permute-start | bytes 983048 | tf_op jit(solution)/shard_map/ppermute | solution.py:343
  87.3 4.6 %collective-permute-start.5 = (bf16[320,512]{1,0:T(8,128)(2,1)}, bf16[320,512]{1,0:T(8,128)(2,1)S(1)}, u32[]{:S(2)}, u32[]{:S(2)}) collective-permute-start(bf16[320,512]{1,0:T(8,128)(2,1)} %get-tuple-element.40), channel_id=1, source_target_pairs={{0,3},{1,0},{2,1},{3,2},{4,7},{5,4},{6,5},{7,6},{8,11},{9,8},{10,9... | collective-permute-start | bytes 983048 | tf_op jit(solution)/shard_map/ppermute | solution.py:343
  91.9 2.4 %all-to-all-done.3.in_ref = f32[16,4,384]{2,1,0:T(4,128)S(1)} async-done(((f32[16,4,384]{2,1,0:T(4,128)}), f32[16,4,384]{2,1,0:T(4,128)S(1)}, u32[]{:S(2)}, u32[]{:S(2)}) %all-to-all-start.3) | async-done | bytes 98336 | tf_op jit(solution)/shard_map/all_to_all | solution.py:431
  94.4 0.0 copy-done
  94.4 0.0 copy-done.4
  94.4 1.4 %shard_map.129 = f32[4,4,320]{2,1,0:T(4,128)} custom-call(s32[1]{0:T(128)} %bitcast.13.own_ref, f32[16,4,384]{2,1,0:T(4,128)S(1)} %all-to-all-done.3.in_ref, bf16[16,320]{1,0:T(8,128)(2,1)S(1)} %get-tuple-element.42.q_ref, bf16[2,16,320]{2,1,0:T(8,128)(2,1)S(1)} %copy-done.4, bf16[320,1280]{1,0:T(8,128)(2,1)S(1)} %copy-done), custom_call_target="tpu_custom_call" | custom-call | flops 6553600 | bytes 819200 | tf_op jit(solution)/shard_map/pallas_call | solution.py:303
  95.7 3.3 %all-to-all-start.4 = ((f32[4,4,320]{2,1,0:T(4,128)}), f32[4,4,320]{2,1,0:T(4,128)S(1)}, u32[]{:S(2)}, u32[]{:S(2)}) async-start(f32[4,4,320]{2,1,0:T(4,128)} %shard_map.129), calls=%async_computation.4 | async-start | bytes 49152 | tf_op jit(solution)/shard_map/all_to_all | solution.py:440
  99.0 0.0 collective-permute-done.3.a_ref
  99.0 3.6 %collective-permute-done.4.b_ref = bf16[320,512]{1,0:T(8,128)(2,1)S(1)} collective-permute-done((bf16[320,512]{1,0:T(8,128)(2,1)}, bf16[320,512]{1,0:T(8,128)(2,1)S(1)}, u32[]{:S(2)}, u32[]{:S(2)}) %collective-permute-start.4) | collective-permute-done | bytes 327712 | tf_op jit(solution)/shard_map/ppermute | solution.py:343
  102.6 0.0 collective-permute-done.5.c_ref
  102.6 0.0 copy-start.1
  102.6 1.1 %copy-done.1 = f32[320,512]{1,0:T(8,128)S(1)} copy-done((f32[320,512]{1,0:T(8,128)S(1)}, f32[320,512]{1,0:T(8,128)}, u32[]{:S(2)}) %copy-start.1) | copy-done | bytes 655384
  103.7 0.9 shard_map.127
  104.6 0.0 all-to-all-done.4
  104.6 0.6 reduce_sum.9
Async XLA Ops:
  0.6 32.2 %copy-start.7 = (bf16[512,320]{0,1:T(8,128)(2,1)S(1)}, bf16[512,320]{0,1:T(8,128)(2,1)}, u32[]{:S(2)}) copy-start(bf16[512,320]{0,1:T(8,128)(2,1)} %param.11) | copy-start | bytes 983044
  2.0 14.1 %all-to-all-start = ((bf16[16,4,320]{2,1,0:T(4,128)(2,1)}), bf16[16,4,320]{2,1,0:T(4,128)(2,1)S(1)}, u32[]{:S(2)}, u32[]{:S(2)}) async-start(bf16[16,4,320]{2,1,0:T(4,128)(2,1)} %broadcast_in_dim.2), calls=%async_computation | async-start | bytes 98304 | tf_op jit(solution)/shard_map/all_to_all | solution.py:322
  10.8 40.8 %copy-start.2 = (bf16[640,320]{0,1:T(8,128)(2,1)S(1)}, bf16[640,320]{0,1:T(8,128)(2,1)}, u32[]{:S(2)}) copy-start(bf16[640,320]{0,1:T(8,128)(2,1)} %param.19) | copy-start | bytes 1228804
  10.8 40.8 %copy-start.3 = (bf16[640,320]{0,1:T(8,128)(2,1)S(1)}, bf16[640,320]{0,1:T(8,128)(2,1)}, u32[]{:S(2)}) copy-start(bf16[640,320]{0,1:T(8,128)(2,1)} %param.20) | copy-start | bytes 1228804
  11.6 0.7 copy-start.6
  17.3 0.6 copy-start.5
  17.9 27.1 %all-to-all-start.1 = ((bf16[16,40,128]{2,1,0:T(8,128)(2,1)}), bf16[16,40,128]{2,1,0:T(8,128)(2,1)S(1)}, u32[]{:S(2)}, u32[]{:S(2)}) async-start(bf16[16,40,128]{2,1,0:T(8,128)(2,1)} %get-tuple-element.27), calls=%async_computation.1 | async-start | bytes 327680 | tf_op jit(solution)/shard_map/all_to_all | solution.py:371
  32.8 22.8 %collective-permute-start.2 = (bf16[320,512]{1,0:T(8,128)(2,1)S(1)}, bf16[320,512]{1,0:T(8,128)(2,1)S(1)}, u32[]{:S(2)}, u32[]{:S(2)}) collective-permute-start(bf16[320,512]{1,0:T(8,128)(2,1)S(1)} %bitcast.24), channel_id=1, source_target_pairs={{0,3},{1,0},{2,1},{3,2},{4,7},{5,4},{6,5},{7,6},{8,11},{9,8},{10,9... | collective-permute-start | bytes 983048 | tf_op jit(solution)/shard_map/ppermute | solution.py:343
  35.7 19.9 %collective-permute-start.1 = (bf16[320,512]{1,0:T(8,128)(2,1)S(1)}, bf16[320,512]{1,0:T(8,128)(2,1)S(1)}, u32[]{:S(2)}, u32[]{:S(2)}) collective-permute-start(bf16[320,512]{1,0:T(8,128)(2,1)S(1)} %bitcast.25), channel_id=1, source_target_pairs={{0,2},{1,3},{2,0},{3,1},{4,6},{5,7},{6,4},{7,5},{8,10},{9,11},{10,... | collective-permute-start | bytes 983048 | tf_op jit(solution)/shard_map/ppermute | solution.py:343
  38.7 16.9 %collective-permute-start = (bf16[320,512]{1,0:T(8,128)(2,1)S(1)}, bf16[320,512]{1,0:T(8,128)(2,1)}, u32[]{:S(2)}, u32[]{:S(2)}) collective-permute-start(bf16[320,512]{1,0:T(8,128)(2,1)S(1)} %bitcast.26), channel_id=1, source_target_pairs={{0,1},{1,2},{2,3},{3,0},{4,5},{5,6},{6,7},{7,4},{8,9},{9,10},{10,1... | collective-permute-start | bytes 983048 | tf_op jit(solution)/shard_map/ppermute | solution.py:343
  55.6 4.8 %copy-start.8 = (bf16[320,512]{1,0:T(8,128)(2,1)}, bf16[320,512]{1,0:T(8,128)(2,1)S(1)}, u32[]{:S(2)}) copy-start(bf16[320,512]{1,0:T(8,128)(2,1)S(1)} %collective-permute-done.2.x3_hbm) | copy-start | bytes 983044
  55.6 4.8 %copy-start.9 = (bf16[320,512]{1,0:T(8,128)(2,1)}, bf16[320,512]{1,0:T(8,128)(2,1)S(1)}, u32[]{:S(2)}) copy-start(bf16[320,512]{1,0:T(8,128)(2,1)S(1)} %collective-permute-done.1.x2_hbm) | copy-start | bytes 983044
  55.6 13.8 %all-to-all-start.2 = ((bf16[8,64,384]{2,1,0:T(8,128)(2,1)}), bf16[8,64,384]{2,1,0:T(8,128)(2,1)S(1)}, u32[]{:S(2)}, u32[]{:S(2)}) async-start(bf16[8,64,384]{2,1,0:T(8,128)(2,1)} %bitcast.11), calls=%async_computation.2 | async-start | bytes 786432 | tf_op jit(solution)/shard_map/all_to_all | solution.py:411
  60.4 34.0 %copy-start = (bf16[320,1280]{1,0:T(8,128)(2,1)S(1)}, bf16[320,1280]{1,0:T(8,128)(2,1)}, u32[]{:S(2)}) copy-start(bf16[320,1280]{1,0:T(8,128)(2,1)} %w_ref.1) | copy-start | bytes 2457604
  60.4 34.0 %copy-start.4 = (bf16[2,16,320]{2,1,0:T(8,128)(2,1)S(1)}, bf16[2,16,320]{2,1,0:T(8,128)(2,1)}, u32[]{:S(2)}) copy-start(bf16[2,16,320]{2,1,0:T(8,128)(2,1)} %shard_map.123.kv_ref) | copy-start | bytes 61444
  70.9 23.5 %all-to-all-start.3 = ((f32[16,4,384]{2,1,0:T(4,128)}), f32[16,4,384]{2,1,0:T(4,128)S(1)}, u32[]{:S(2)}, u32[]{:S(2)}) async-start(f32[16,4,384]{2,1,0:T(4,128)} %shard_map.128), calls=%async_computation.3 | async-start | bytes 196608 | tf_op jit(solution)/shard_map/all_to_all | solution.py:431
  82.4 16.6 %collective-permute-start.3 = (bf16[320,512]{1,0:T(8,128)(2,1)}, bf16[320,512]{1,0:T(8,128)(2,1)S(1)}, u32[]{:S(2)}, u32[]{:S(2)}) collective-permute-start(bf16[320,512]{1,0:T(8,128)(2,1)} %get-tuple-element.36), channel_id=1, source_target_pairs={{0,2},{1,3},{2,0},{3,1},{4,6},{5,7},{6,4},{7,5},{8,10},{9,11},{10,... | collective-permute-start | bytes 983048 | tf_op jit(solution)/shard_map/ppermute | solution.py:343
  85.4 17.2 %collective-permute-start.4 = (bf16[320,512]{1,0:T(8,128)(2,1)}, bf16[320,512]{1,0:T(8,128)(2,1)S(1)}, u32[]{:S(2)}, u32[]{:S(2)}) collective-permute-start(bf16[320,512]{1,0:T(8,128)(2,1)} %get-tuple-element.37), channel_id=1, source_target_pairs={{0,1},{1,2},{2,3},{3,0},{4,5},{5,6},{6,7},{7,4},{8,9},{9,10},{10,1... | collective-permute-start | bytes 983048 | tf_op jit(solution)/shard_map/ppermute | solution.py:343
  87.3 15.3 %collective-permute-start.5 = (bf16[320,512]{1,0:T(8,128)(2,1)}, bf16[320,512]{1,0:T(8,128)(2,1)S(1)}, u32[]{:S(2)}, u32[]{:S(2)}) collective-permute-start(bf16[320,512]{1,0:T(8,128)(2,1)} %get-tuple-element.40), channel_id=1, source_target_pairs={{0,3},{1,0},{2,1},{3,2},{4,7},{5,4},{6,5},{7,6},{8,11},{9,8},{10,9... | collective-permute-start | bytes 983048 | tf_op jit(solution)/shard_map/ppermute | solution.py:343
  95.7 8.9 %all-to-all-start.4 = ((f32[4,4,320]{2,1,0:T(4,128)}), f32[4,4,320]{2,1,0:T(4,128)S(1)}, u32[]{:S(2)}, u32[]{:S(2)}) async-start(f32[4,4,320]{2,1,0:T(4,128)} %shard_map.129), calls=%async_computation.4 | async-start | bytes 49152 | tf_op jit(solution)/shard_map/all_to_all | solution.py:440
  102.6 1.1 %copy-start.1 = (f32[320,512]{1,0:T(8,128)S(1)}, f32[320,512]{1,0:T(8,128)}, u32[]{:S(2)}) copy-start(f32[320,512]{1,0:T(8,128)} %get-tuple-element.35.own_ref) | copy-start | bytes 1966084
